TPU v7x, 32 devices: a whole 2x2x4 slice. The times are simulated.
32 devices in a mesh: lat: 8 (over z, x), lon: 4 (over y, core).
Axes of the slice: x: 2, y: 2, z: 4, core: 2. Of those that a mesh axis runs over, the one named last changes fastest.
Arguments:
- pixels: bfloat16 [2, 48, 48, 1280], P(None, 'lat', 'lon'), may hold values from -6 to 6
- targets: bfloat16 [2, 2, 48, 48, 1280], P(None, None, 'lat', 'lon'), may hold values from -6 to 6
- mask: int32 [2, 48, 48], P(None, 'lat', 'lon'), may hold values 0 or 1
- lat_rows: int32 [48], P('lat'), may hold values from 0 to 47
- adam_params: float32 [6510080], P(('lat', 'lon')), may hold values from -1.5 to 1.5
- adam_m: float32 [6510080], P(('lat', 'lon')), may hold values from -1.7881393e-07 to 1.7881393e-07
- adam_v: float32 [6510080], P(('lat', 'lon')), may hold values from 3.135334e-15 to 1.2541336e-14
- mlp_weights: float32 [2, 2, 3072, 768], P(None, None, 'lon'), may hold values from -1 to 1
- mlp_momentum: float32 [2, 2, 3072, 768], P(None, None, 'lon'), may hold values from -1.4305115e-06 to 1.4305115e-06
Outputs:
- adam_params_new: float32 [6510080], P(('lat', 'lon'))
- adam_m_new: float32 [6510080], P(('lat', 'lon'))
- adam_v_new: float32 [6510080], P(('lat', 'lon'))
- mlp_weights_new: float32 [2, 2, 3072, 768], P(None, None, 'lon')
- mlp_momentum_new: float32 [2, 2, 3072, 768], P(None, None, 'lon')
- loss: float32 [], replicated
- grad_norm: float32 [], replicated
All inputs are finite; a program needn't handle non-finite values. No bound on the sum of `mask` on one device may be relied on, other than what follows from the above.
Results may differ from a plain program's by a relative error of at most 0.012.
Values may be sent and summed in bfloat16 or wider, within the bound.
No kernel may reach another device: no remote copies, remote signals or barrier semaphores. Data moves between devices by JAX's collectives and lax.ppermute only.
A program may use at most 512 MiB of HBM per device.

v0:
```python
import math

import jax
import jax.numpy as jnp
from jax import lax
from jax.sharding import PartitionSpec as P

D = 768
FF = 3072
NB = 8
PIX = 1280
BS = 96
L = 2
STEPS = 2
NS_STEPS = 2
STEP_NUM = 5


HIGH_PREC = lax.Precision.HIGHEST
NORM_EPS = 1e-05
CLIP_LEVEL = 0.001
BETA_FIRST = 0.9
BETA_SECOND = 0.95
ADAM_RATE = 0.01
MUON_RATE = 0.8
DECAY_RATE = 0.05
MOMENT_KEEP = 0.95
POLY_COEF = (3.4445, -4.775, 2.0315)


def for_sending(value):

    def short(part):
        return part.astype(jnp.bfloat16) if part.dtype == jnp.float32 else part

    return jax.tree.map(short, value)


def with_halo(block, sides, width):
    for axis, dim in sides:
        count = lax.axis_size(axis)
        forward = [(i, i + 1) for i in range(count - 1)]
        forward.append((count - 1, 0))
        backward = [(target, source) for source, target in forward]
        low = lax.ppermute(
            lax.slice_in_dim(block, block.shape[dim] - width, None, axis=dim), axis, forward
        )
        high = lax.ppermute(lax.slice_in_dim(block, 0, width, axis=dim), axis, backward)
        block = jnp.concatenate([low, block, high], axis=dim)
    return block


def unpack(flat_params):
    layout = [
        (3, PIX, D),
        (3, D, PIX),
        (L, 2, 2, NB, BS, BS),
        (D,),
        (PIX,),
        (L, 2, 2, D),
        (L, 4, D),
        (L, FF + D),
    ]
    pieces_out = []
    offset = 0
    for dims_now in layout:
        amount = math.prod(dims_now)
        pieces_out.append(flat_params[offset : offset + amount].reshape(dims_now))
        offset = offset + amount
    return pieces_out


def along(matrix, values, axis_dim):
    if axis_dim == 1:
        return jnp.einsum("kn,bncd->bkcd", matrix, values, precision=HIGH_PREC)
    return jnp.einsum("kn,brnd->brkd", matrix, values, precision=HIGH_PREC)


def phase_table(out_count, in_count, length_all):
    out_index = jnp.arange(out_count, dtype=jnp.int32)
    in_index = jnp.arange(in_count, dtype=jnp.int32)
    phase = out_index[:, None] * in_index[None, :] % length_all
    angle = phase.astype(jnp.float32) * (2.0 * math.pi / length_all)
    scale_value = 1.0 / math.sqrt(length_all)
    return (jnp.cos(angle) * scale_value, jnp.sin(angle) * scale_value)


def combine(pieces, axis_dim, sign_value, tables, real_only):
    cosine, sine_table = tables
    values = [piece_now.astype(jnp.float32) for piece_now in pieces]
    real_out = along(cosine, values[0], axis_dim)
    if len(values) > 1:
        real_out = real_out - sign_value * along(sine_table, values[1], axis_dim)
    if real_only:
        return (real_out,)
    imag_out = sign_value * along(sine_table, values[0], axis_dim)
    if len(values) > 1:
        imag_out = imag_out + along(cosine, values[1], axis_dim)
    return (real_out, imag_out)


def turn_transform(pieces, axis_dim, sign_value, real_only):
    if axis_dim == 1:
        wide = jax.tree.map(
            lambda part, own: part.astype(own.dtype),
            lax.all_to_all(for_sending(pieces), "lat", split_axis=3, concat_axis=1, tiled=True),
            pieces,
        )
        length_all = wide[0].shape[1]
        result = combine(
            wide, 1, sign_value, phase_table(length_all, length_all, length_all), real_only
        )
        narrow = tuple((piece_now.astype(jnp.bfloat16) for piece_now in result))
        returned = jax.tree.map(
            lambda part, own: part.astype(own.dtype),
            lax.all_to_all(for_sending(narrow), "lat", split_axis=1, concat_axis=3, tiled=True),
            narrow,
        )
        return tuple((piece_now.astype(jnp.float32) for piece_now in returned))
    wide = jax.tree.map(
        lambda part, own: part.astype(own.dtype),
        lax.all_to_all(for_sending(pieces), "lon", split_axis=3, concat_axis=2, tiled=True),
        pieces,
    )
    length_all = wide[0].shape[2]
    result = combine(
        wide, 2, sign_value, phase_table(length_all, length_all, length_all), real_only
    )
    return jax.tree.map(
        lambda part, own: part.astype(own.dtype),
        lax.all_to_all(for_sending(result), "lon", split_axis=2, concat_axis=3, tiled=True),
        result,
    )


def transform(pieces, axis_dim, sign_value, real_only):
    return turn_transform(pieces, axis_dim, sign_value, real_only)


def to_low(pieces):
    return tuple((piece_now.astype(jnp.bfloat16) for piece_now in pieces))


def exact_gelu(values):
    return jax.nn.gelu(values, approximate=False)


def gelu_back(values, upstream):
    return jax.vjp(exact_gelu, values)[1](upstream)[0]


def norm_forward(inputs, gain, shift):
    center = inputs - jnp.mean(inputs, axis=-1, keepdims=True)
    inverse = lax.rsqrt(jnp.mean(center * center, axis=-1, keepdims=True) + NORM_EPS)
    scaled = center * inverse
    return (scaled * gain + shift, (scaled, inverse))


def norm_backward(upstream, saved, gain):
    scaled, inverse = saved
    g_gain = jnp.sum(upstream * scaled, axis=(0, 1, 2))
    g_shift = jnp.sum(upstream, axis=(0, 1, 2))
    g_scaled = upstream * gain
    g_input = inverse * (
        g_scaled
        - jnp.mean(g_scaled, axis=-1, keepdims=True)
        - scaled * jnp.mean(g_scaled * scaled, axis=-1, keepdims=True)
    )
    return (g_input, g_gain, g_shift)


def block_mix(pieces, weights, bias):
    shaped = [piece_now.reshape(piece_now.shape[:-1] + (NB, BS)) for piece_now in pieces]

    def multiply(left_side, right_side):
        return jnp.einsum(
            "brcni,nio->brcno", left_side, right_side, preferred_element_type=jnp.float32
        )

    real_out = multiply(shaped[0], weights[0]) - multiply(shaped[1], weights[1])
    imag_out = multiply(shaped[0], weights[1]) + multiply(shaped[1], weights[0])
    full_dims = pieces[0].shape
    return (
        real_out.reshape(full_dims) + bias[0].astype(jnp.float32),
        imag_out.reshape(full_dims) + bias[1].astype(jnp.float32),
    )


def block_back(grads_low, pieces, weights):
    shaped = [piece_now.reshape(piece_now.shape[:-1] + (NB, BS)) for piece_now in pieces]
    g_shaped = [grad_now.reshape(grad_now.shape[:-1] + (NB, BS)) for grad_now in grads_low]

    def back_multiply(grad_side, weight_side):
        return jnp.einsum(
            "brcno,nio->brcni", grad_side, weight_side, preferred_element_type=jnp.float32
        )

    def weight_multiply(input_side, grad_side):
        return jnp.einsum(
            "brcni,brcno->nio", input_side, grad_side, preferred_element_type=jnp.float32
        )

    g_real = back_multiply(g_shaped[0], weights[0]) + back_multiply(g_shaped[1], weights[1])
    g_imag = back_multiply(g_shaped[1], weights[0]) - back_multiply(g_shaped[0], weights[1])
    g_w_real = weight_multiply(shaped[0], g_shaped[0]) + weight_multiply(shaped[1], g_shaped[1])
    g_w_imag = weight_multiply(shaped[0], g_shaped[1]) - weight_multiply(shaped[1], g_shaped[0])
    g_bias = jnp.stack(
        [jnp.sum(grad_now.astype(jnp.float32), axis=(0, 1, 2)) for grad_now in grads_low]
    )
    full_dims = pieces[0].shape
    return (
        (g_real.reshape(full_dims), g_imag.reshape(full_dims)),
        jnp.stack([g_w_real, g_w_imag]),
        g_bias,
    )


def halo_rows(values):
    return with_halo(values, (("lat", 1),), 1)


def rows_conv(source_low, weight3, bias):
    padded = halo_rows(source_low)
    row_count = source_low.shape[1]
    window = jnp.concatenate(
        [padded[:, offset : offset + row_count] for offset in range(3)], axis=-1
    )
    flat_weight = weight3.reshape(-1, weight3.shape[-1])
    result = jnp.einsum("brci,io->brco", window, flat_weight, preferred_element_type=jnp.float32)
    return (result + bias.astype(jnp.float32), window)


def rows_back(grad_low, weight3, need_source):
    g_bias = jnp.sum(grad_low.astype(jnp.float32), axis=(0, 1, 2))
    if not need_source:
        return (g_bias, None)
    padded = halo_rows(grad_low)
    row_count = grad_low.shape[1]
    window_back = jnp.concatenate(
        [padded[:, 2 - offset : 2 - offset + row_count] for offset in range(3)], axis=-1
    )
    flipped = jnp.transpose(weight3, (0, 2, 1)).reshape(-1, weight3.shape[1])
    g_source = jnp.einsum("brco,oi->brci", window_back, flipped, preferred_element_type=jnp.float32)
    return (g_bias, g_source)


def conv_weight_grad(terms_list, weight3):
    window = jnp.concatenate([terms_now[0] for terms_now in terms_list], axis=0)
    grads_low = jnp.concatenate([terms_now[1] for terms_now in terms_list], axis=0)
    return jnp.einsum(
        "brci,brco->io", window, grads_low, preferred_element_type=jnp.float32
    ).reshape(weight3.shape)


def layer_forward(state, params_now):
    spec_w, spec_b, norm_vals, mlp_pair, mlp_bias = params_now
    normed, first_saved = norm_forward(state, norm_vals[0], norm_vals[1])
    spectrum = transform((normed.astype(jnp.bfloat16),), 2, -1.0, False)
    spectrum = transform(to_low(spectrum), 1, -1.0, False)
    mixed_in = to_low(spectrum)
    inner = block_mix(mixed_in, spec_w[0], spec_b[0])
    activated = to_low(tuple((exact_gelu(piece_now) for piece_now in inner)))
    outer = block_mix(activated, spec_w[1], spec_b[1])
    spectrum = transform(to_low(outer), 1, 1.0, False)
    spatial = transform(to_low(spectrum), 2, 1.0, True)[0]
    mixed = state + spatial + normed
    second, second_saved = norm_forward(mixed, norm_vals[2], norm_vals[3])
    hidden_in = second.astype(jnp.bfloat16)
    before = (
        jnp.einsum("brcd,fd->brcf", hidden_in, mlp_pair[0], preferred_element_type=jnp.float32)
        + mlp_bias[:FF]
    )
    hidden = exact_gelu(before).astype(jnp.bfloat16)
    result = (
        jnp.einsum("brcf,fd->brcd", hidden, mlp_pair[1], preferred_element_type=jnp.float32)
        + mlp_bias[FF:]
    )
    return (
        mixed + result,
        (first_saved, mixed_in, inner, activated, second_saved, hidden_in, before, hidden),
    )


def layer_backward(upstream, cache, params_now):
    spec_w, spec_b, norm_vals, mlp_pair, mlp_bias = params_now
    first_saved, mixed_in, inner, activated, second_saved, hidden_in, before, hidden = cache
    grad_out = upstream.astype(jnp.bfloat16)
    g_down_bias = jnp.sum(grad_out.astype(jnp.float32), axis=(0, 1, 2))
    g_hidden = jnp.einsum(
        "brcd,fd->brcf", grad_out, mlp_pair[1], preferred_element_type=jnp.float32
    )
    g_before = gelu_back(before, g_hidden).astype(jnp.bfloat16)
    g_up_bias = jnp.sum(g_before.astype(jnp.float32), axis=(0, 1, 2))
    g_second = jnp.einsum(
        "brcf,fd->brcd", g_before, mlp_pair[0], preferred_element_type=jnp.float32
    )
    g_norm_in, g_gain_two, g_shift_two = norm_backward(g_second, second_saved, norm_vals[2])
    g_mixed = upstream + g_norm_in
    g_spectrum = transform((g_mixed.astype(jnp.bfloat16),), 2, -1.0, False)
    g_outer = to_low(transform(to_low(g_spectrum), 1, -1.0, False))
    g_activated, g_w_outer, g_b_outer = block_back(g_outer, activated, spec_w[1])
    g_inner = to_low(
        tuple((gelu_back(piece_now, grad_now) for piece_now, grad_now in zip(inner, g_activated)))
    )
    g_mixed_in, g_w_inner, g_b_inner = block_back(g_inner, mixed_in, spec_w[0])
    g_spectrum = transform(to_low(g_mixed_in), 1, 1.0, False)
    g_normed = transform(to_low(g_spectrum), 2, 1.0, True)[0] + g_mixed
    g_state_norm, g_gain_one, g_shift_one = norm_backward(g_normed, first_saved, norm_vals[0])
    layer_grads = (
        jnp.stack([g_w_inner, g_w_outer]),
        jnp.stack([g_b_inner, g_b_outer]),
        jnp.stack([g_gain_one, g_shift_one, g_gain_two, g_shift_two]),
        jnp.concatenate([g_up_bias, g_down_bias]),
    )
    return (g_mixed + g_state_norm, layer_grads, (hidden, grad_out, g_before, hidden_in))


def body(pixels, targets, mask, lat_rows, adam_params, adam_m, adam_v, mlp_weights, mlp_momentum):
    flat_low = lax.all_gather(adam_params.astype(jnp.bfloat16), ("lat", "lon"), axis=0, tiled=True)
    mlp_low = lax.all_gather(mlp_weights.astype(jnp.bfloat16), "lon", axis=2, tiled=True)
    embed_w, head_w, spec_w, embed_b, head_b, spec_b, norm_params, mlp_b = unpack(flat_low)
    row_count = pixels.shape[1]
    lat_total = lax.axis_size("lat") * row_count
    row_weight = jnp.sin(math.pi * (lat_rows.astype(jnp.float32) + 0.5) / lat_total)
    weight_map = row_weight[None, :, None] * mask.astype(jnp.float32)
    weight_sum = lax.psum(jnp.sum(weight_map), ("lat", "lon"))
    loss_scale = 2.0 / (STEPS * PIX * weight_sum)

    def params_at(depth_idx):
        return (
            spec_w[depth_idx],
            spec_b[depth_idx],
            norm_params[depth_idx].astype(jnp.float32),
            mlp_low[depth_idx],
            mlp_b[depth_idx].astype(jnp.float32),
        )

    current = pixels
    saved_steps = []
    loss_local = jnp.zeros((), jnp.float32)
    for roll_idx in range(STEPS):
        state, embed_window = rows_conv(current.astype(jnp.bfloat16), embed_w, embed_b)
        caches = []
        for depth_idx in range(L):
            state, cache_now = layer_forward(state, params_at(depth_idx))
            caches.append(cache_now)
        predicted, head_window = rows_conv(state.astype(jnp.bfloat16), head_w, head_b)
        differ = predicted - targets[roll_idx].astype(jnp.float32)
        loss_local = loss_local + jnp.sum(weight_map[..., None] * differ * differ)
        saved_steps.append(
            (embed_window, caches, head_window, weight_map[..., None] * differ * loss_scale)
        )
        current = predicted
    g_embed_b = jnp.zeros(embed_b.shape, jnp.float32)
    g_head_b = jnp.zeros(head_b.shape, jnp.float32)
    head_terms = []
    embed_terms = []
    mlp_terms = [[] for unused in range(L)]
    g_layers = [None] * L
    carried = None
    for roll_idx in reversed(range(STEPS)):
        embed_window, caches, head_window, loss_grad = saved_steps[roll_idx]
        upstream = loss_grad if carried is None else loss_grad + carried
        upstream_low = upstream.astype(jnp.bfloat16)
        head_terms.append((head_window, upstream_low))
        grad_b, grad_state = rows_back(upstream_low, head_w, True)
        g_head_b = g_head_b + grad_b
        for depth_idx in reversed(range(L)):
            grad_state, layer_grads, mlp_now = layer_backward(
                grad_state, caches[depth_idx], params_at(depth_idx)
            )
            mlp_terms[depth_idx].append(mlp_now)
            if g_layers[depth_idx] is None:
                g_layers[depth_idx] = layer_grads
            else:
                g_layers[depth_idx] = jax.tree.map(jnp.add, g_layers[depth_idx], layer_grads)
        state_low = grad_state.astype(jnp.bfloat16)
        embed_terms.append((embed_window, state_low))
        grad_b, carried = rows_back(state_low, embed_w, roll_idx > 0)
        g_embed_b = g_embed_b + grad_b
    g_embed_w = conv_weight_grad(embed_terms, embed_w)
    g_head_w = conv_weight_grad(head_terms, head_w)
    mlp_grads = []
    for depth_idx in range(L):
        joined = [
            jnp.concatenate([terms_now[member] for terms_now in mlp_terms[depth_idx]], axis=0)
            for member in range(4)
        ]
        g_up = jnp.einsum("brcf,brcd->fd", joined[2], joined[3], preferred_element_type=jnp.float32)
        g_down = jnp.einsum(
            "brcf,brcd->fd", joined[0], joined[1], preferred_element_type=jnp.float32
        )
        mlp_grads.append(jnp.stack([g_up, g_down]))
    full_mlp = jnp.stack(mlp_grads)
    stacked = [
        jnp.stack([g_layers[depth_idx][member] for depth_idx in range(L)]) for member in range(4)
    ]
    flat_grad = jnp.concatenate(
        [
            g_embed_w.reshape(-1),
            g_head_w.reshape(-1),
            stacked[0].reshape(-1),
            g_embed_b,
            g_head_b,
            stacked[1].reshape(-1),
            stacked[2].reshape(-1),
            stacked[3].reshape(-1),
        ]
    )
    lon_count = lax.axis_size("lon")
    lat_count = lax.axis_size("lat")
    dev_count = lon_count * lat_count
    per_block = full_mlp.shape[2] // dev_count
    mlp_rows = (
        full_mlp.reshape(L, 2, lon_count, lat_count, per_block, D)
        .transpose(3, 2, 0, 1, 4, 5)
        .reshape(dev_count, -1)
    )
    flat_rows = flat_grad.reshape(dev_count, -1)
    flat_width = flat_rows.shape[1]
    summed = lax.psum_scatter(
        jnp.concatenate([flat_rows, mlp_rows], axis=1),
        ("lat", "lon"),
        scatter_dimension=0,
        tiled=True,
    )[0]
    flat_piece = summed[:flat_width]
    mlp_piece = summed[flat_width:].reshape(L, 2, per_block, D)
    local_square = jnp.sum(flat_piece * flat_piece) + jnp.sum(mlp_piece * mlp_piece)
    loss_total, square_sum = lax.psum(
        (loss_local / (STEPS * PIX * weight_sum), local_square), ("lat", "lon")
    )
    mlp_grad = lax.all_gather(mlp_piece.astype(jnp.bfloat16), "lat", axis=2, tiled=True).astype(
        mlp_piece.dtype
    )
    grad_norm = jnp.sqrt(square_sum)
    factor = jnp.minimum(1.0, CLIP_LEVEL / (grad_norm + 1e-06))
    clipped = flat_piece * factor
    first_new = BETA_FIRST * adam_m + (1.0 - BETA_FIRST) * clipped
    second_new = BETA_SECOND * adam_v + (1.0 - BETA_SECOND) * clipped * clipped
    count_value = float(STEP_NUM)
    first_hat = first_new / (1.0 - BETA_FIRST**count_value)
    second_hat = second_new / (1.0 - BETA_SECOND**count_value)
    adam_new = adam_params - ADAM_RATE * (
        first_hat / (jnp.sqrt(second_hat) + 1e-08) + DECAY_RATE * adam_params
    )
    momentum_new = MOMENT_KEEP * mlp_momentum + mlp_grad * factor
    ortho = momentum_new
    for ns_idx in range(NS_STEPS):
        partial_gram = jnp.einsum("lkfd,lkfe->lkde", ortho, ortho, precision=HIGH_PREC)
        square = lax.psum(partial_gram.astype(jnp.bfloat16), "lon").astype(jnp.float32)
        if ns_idx == 0:
            trace_val = jnp.trace(square, axis1=2, axis2=3)
            inverse = 1.0 / (jnp.sqrt(trace_val) + 1e-07)
            ortho = ortho * inverse[:, :, None, None]
            square = square * (inverse * inverse)[:, :, None, None]
        poly = POLY_COEF[1] * square + POLY_COEF[2] * jnp.einsum(
            "lkde,lkef->lkdf", square, square, precision=HIGH_PREC
        )
        ortho = POLY_COEF[0] * ortho + jnp.einsum(
            "lkfd,lkde->lkfe", ortho, poly, precision=HIGH_PREC
        )
    mlp_new = mlp_weights * (1.0 - MUON_RATE * DECAY_RATE) - MUON_RATE * (FF / D) ** 0.5 * ortho
    return (adam_new, first_new, second_new, mlp_new, momentum_new, loss_total, grad_norm)


def solution(mesh):
    placed = (
        P(None, "lat", "lon", None),
        P(None, None, "lat", "lon", None),
        P(None, "lat", "lon"),
        P("lat"),
        P(("lat", "lon")),
        P(("lat", "lon")),
        P(("lat", "lon")),
        P(None, None, "lon", None),
        P(None, None, "lon", None),
    )
    return jax.shard_map(
        body,
        mesh=mesh,
        in_specs=placed,
        out_specs=(
            P(("lat", "lon")),
            P(("lat", "lon")),
            P(("lat", "lon")),
            P(None, None, "lon", None),
            P(None, None, "lon", None),
            P(),
            P(),
        ),
        check_vma=False,
    )
```

profile of v0, /device:TPU:0, one launch (start us, length us, event | category | flops | bytes accessed | tf_op | source)
XLA Modules:
  0.0 4633.7 jit_solution(8975585872070440740)
XLA Ops:
  35.9 311.3 %all-reduce.12.cloned.1.call-done = bf16[6510080]{0:T(1024)(128)(2,1)} async-done(((bf16[6510080]{0:T(1024)(128)(2,1)}), bf16[6510080]{0:T(1024)(128)(2,1)}) %all-reduce.12.cloned.1.call-update) | async-done | bytes 13020176
  347.2 9.7 fusion.1477
  356.9 11.1 reshape.1246
  381.8 8.7 all_to_all.1896
  681.0 8.0 all_to_all.1897
  855.6 7.6 reshape.1345
  991.3 12.0 reshape.1261
  1031.2 8.1 all_to_all.1898
  1203.0 7.5 reshape.1359
  1303.0 9.5 all_to_all.1899
  1341.1 8.0 all_to_all.1900
  1455.2 7.6 all-to-all-done.48
  1509.8 7.5 reshape.1373
  1645.4 38.2 psum.35
  1694.2 12.0 reshape.1212
  1706.2 8.9 copy.1569
  1740.0 8.0 all_to_all.1901
  1853.4 8.8 all-to-all-done.61
  1941.2 11.1 reshape.1214
  1952.4 9.0 copy.1679
  2438.2 8.0 convolution_bitcast_fusion
  2446.2 13.0 reshape_reshape.14
  2471.0 8.0 fusion.79
  2493.1 7.8 fusion.83
  2544.1 7.6 all-to-all-done.89
  2742.1 7.9 fusion.71
  2774.7 7.6 fusion.75
  2796.3 28.4 copy_bitcast_fusion
  2879.6 35.8 reshape.1221
  3069.6 9.2 convolution_bitcast_fusion.1
  3078.7 13.2 reshape_reshape.13
  3091.9 9.8 constant_dynamic-update-slice_fusion.6
  3101.7 9.8 constant_dynamic-update-slice_fusion.5
  3117.5 33.2 reshape.1220
  3150.7 42.5 pad_maximum_fusion
  3193.3 921.3 %all-reduce.14.cloned.1.call-done = f32[32,498352]{1,0:T(8,128)} async-done(((f32[32,498352]{1,0:T(8,128)}), f32[32,498352]{1,0:T(8,128)}) %all-reduce.14.cloned.1.call-update) | async-done | bytes 63789072
  4114.5 14.3 convert_reduce_fusion.4
  4143.7 41.0 all-reduce.2
  4185.4 23.9 all-gather.5.cloned.1.call-done
  4219.4 47.8 %convolution_convert_fusion.1 = bf16[2,2,768,768]{3,2,1,0:T(8,128)(2,1)} fusion(f32[2,2,768,768]{3,2,1,0:T(8,128)S(1)} %multiply_add_fusion.1), kind=kOutput, calls=%fused_computation.74 | convolution fusion | flops 21745631232 | bytes 14155776 | tf_op jit(solution)/shard_map/lkfd,lkfe->lkde/dot_general | solution.py:450
  4267.4 8.7 multiply_reduce_fusion.1
  4276.1 83.2 %all-reduce.8.cloned.1.call-done = bf16[2,2,768,768]{3,2,1,0:T(8,128)(2,1)} async-done(((bf16[2,2,768,768]{3,2,1,0:T(8,128)(2,1)}), bf16[2,2,768,768]{3,2,1,0:T(8,128)(2,1)}) %all-reduce.8.cloned.1.call-update) | async-done | bytes 4718608 | tf_op jit(solution)/shard_map/psum | solution.py:451
  4363.5 28.2 fusion
  4391.8 28.8 multiply_add_fusion
  4424.2 47.9 %convolution_convert_fusion = bf16[2,2,768,768]{3,2,1,0:T(8,128)(2,1)} fusion(f32[2,2,768,768]{3,2,1,0:T(8,128)S(1)} %multiply_add_fusion), kind=kOutput, calls=%fused_computation.73 | convolution fusion | flops 21745631232 | bytes 14155776 | tf_op jit(solution)/shard_map/lkfd,lkfe->lkde/dot_general | solution.py:450
  4475.6 90.6 %all-reduce.10.cloned.1.call-done = bf16[2,2,768,768]{3,2,1,0:T(8,128)(2,1)} async-done(((bf16[2,2,768,768]{3,2,1,0:T(8,128)(2,1)}), bf16[2,2,768,768]{3,2,1,0:T(8,128)(2,1)}) %all-reduce.10.cloned.1.call-update) | async-done | bytes 4718608 | tf_op jit(solution)/shard_map/psum | solution.py:451
  4566.2 11.2 fusion.1494
  4577.4 47.4 %multiply_subtract_fusion = f32[2,2,768,768]{3,2,1,0:T(8,128)} fusion(f32[2,2,768,768]{3,2,1,0:T(8,128)} %copy-done.1, f32[2,2,768,768]{3,2,1,0:T(8,128)} %param.16, f32[2,2,768,768]{3,2,1,0:T(8,128)} %fusion.1494, bf16[2,2,768,768]{3,2,1,0:T(8,128)(2,1)} %all-reduce.10.cloned.1.call-done), kind=kOutput, calls=%fused_computation.11 | convolution fusion | flops 21764505600 | bytes 42467328 | tf_op jit(solution)/shard_map/lkfd,lkde->lkfe/dot_general | solution.py:460
  (1621 shorter events, 2457.0 us)
Async XLA Ops:
  8.0 339.2 %all-reduce.12.cloned.1.call-start = ((), (), s32[]{:S(2)}) async-start(), calls=%async_computation.116 | async-start | bytes 26042368
  21.3 633.7 %all-gather.3.cloned.1.call-start = ((), (), s32[]{:S(2)}) async-start(), calls=%async_computation.112 | async-start | bytes 23592960 | tf_op jit(solution)/shard_map/all_gather | solution.py:320
  439.2 20.0 all-to-all-start.4
  536.7 17.0 all-to-all-start.7
  608.8 17.4 all-to-all-start.10
  728.5 16.5 all-to-all-start.16
  745.0 17.9 all-to-all-start.18
  831.4 18.2 all-to-all-start.22
  849.6 18.1 all-to-all-start.21
  922.8 17.5 all-to-all-start.24
  985.8 17.5 collective-permute-start.2
  1078.6 16.5 all-to-all-start.30
  1095.1 17.0 all-to-all-start.32
  1196.8 18.2 all-to-all-start.35
  1269.8 17.8 all-to-all-start.38
  1404.8 17.0 all-to-all-start.46
  1487.1 16.7 all-to-all-start.50
  1503.8 18.0 all-to-all-start.49
  1576.8 19.8 all-to-all-start.52
  1639.9 44.4 collective-permute-start.6
  1641.9 42.4 collective-permute-start.7
  1689.8 25.3 collective-permute-start.8
  1693.8 21.4 collective-permute-start.9
  1804.0 17.6 all-to-all-start.60
  1891.1 17.0 all-to-all-start.63
  1937.1 37.0 all-to-all-start.65
  1990.0 17.9 all-to-all-start.66
  2109.8 19.3 all-to-all-start.72
  2129.1 22.1 all-to-all-start.74
  2222.0 23.3 all-to-all-start.77
  2274.4 17.2 all-to-all-start.79
  2307.6 21.0 all-to-all-start.80
  2434.7 32.2 all-to-all-start.87
  2466.9 19.8 all-to-all-start.86
  2486.7 25.1 all-to-all-start.88
  2569.0 21.3 all-to-all-start.92
  2590.4 20.0 all-to-all-start.91
  2670.0 18.2 all-to-all-start.94
  2771.2 18.7 all-to-all-start.101
  2790.0 42.4 all-to-all-start.100
  2873.8 42.6 all-to-all-start.103
  2933.7 22.3 all-to-all-start.106
  2956.0 17.9 all-to-all-start.105
  3028.0 17.4 all-to-all-start.108
  3060.8 1053.8 %all-reduce.14.cloned.1.call-start = ((), (), s32[]{:S(2)}) async-start(), calls=%async_computation.117 | async-start | bytes 127598592
  3193.2 1016.0 %all-gather.5.cloned.1.call-start = ((), (), s32[]{:S(2)}) async-start(), calls=%async_computation.113 | async-start | bytes 5308416 | tf_op jit(solution)/shard_map/all_gather | solution.py:433
  4130.2 229.1 %all-reduce.8.cloned.1.call-start = ((), (), s32[]{:S(2)}) async-start(), calls=%async_computation.114 | async-start | bytes 9437184 | tf_op jit(solution)/shard_map/psum | solution.py:451
  4267.2 299.0 %all-reduce.10.cloned.1.call-start = ((), (), s32[]{:S(2)}) async-start(), calls=%async_computation.115 | async-start | bytes 9437184 | tf_op jit(solution)/shard_map/psum | solution.py:451
  (360 other events, 17169.6 us)
Sparse Core Ops, SparseCore 0:
  21.4 325.7 all-reduce.11
  3193.4 921.1 all-reduce.13
Sparse Core Ops, SparseCore 1:
  35.8 117.8 all-gather.2
  4130.3 78.9 all-gather.4
  4267.3 92.0 all-reduce.7
  4472.2 93.9 all-reduce.9
where the time goes:
time: 4670 us; the launch traced here: 4630 us
  waiting for transfers between devices  1680 us (36%)
  local copies, waits for them, and re-layouts  1550 us (33%)
  matrix products  528 us (11%)
  starting transfers between devices  521 us (11%)
  other arithmetic  195 us (4%)
  blocking collectives  129 us (3%)
    unnamed x8, waiting for transfers between devices  1230 us
    unnamed x684, local copies, waits for them, and re-layouts  733 us
    all_to_all x32, starting transfers between devices, turn_transform(): lax.all_to_all(for_sending(pieces), 'lat', split_axis=3, concat_axis=1, t...  177 us
    psum x2, waiting for transfers between devices, body(): lax.psum(partial_gram.astype(jnp.bfloat16), 'lon').astype(jnp.float32)  174 us
    all_to_all x48, local copies, waits for them, and re-layouts, turn_transform(): lax.all_to_all(for_sending(pieces), 'lon', split_axis=3, concat_axis=2, t...  164 us
    all_to_all x32, starting transfers between devices, turn_transform(): lax.all_to_all(for_sending(narrow), 'lat', split_axis=1, concat_axis=3, t...  158 us
    all_to_all x32, waiting for transfers between devices, turn_transform(): lax.all_to_all(for_sending(narrow), 'lat', split_axis=1, concat_axis=3, t...  156 us
    all_to_all x64, local copies, waits for them, and re-layouts, turn_transform(): lax.all_to_all(for_sending(pieces), 'lat', split_axis=3, concat_axis=1, t...  142 us
  transfers between devices with their start and end apart: 126, of which 50 were waited for; matrix products, arithmetic and copies ran while one was open for 25% of the time, Pallas kernels for 0%

commit v1 on v0

--- a/solution.py
+++ b/solution.py
@@ -1,8 +1,14 @@
+import functools
 import math
 
 import jax
+import ml_dtypes
+import numpy as np
 import jax.numpy as jnp
 from jax import lax
+from jax.experimental import pallas as pl
+from jax.experimental.pallas import tpu as pltpu
+from jax.sharding import Mesh
 from jax.sharding import PartitionSpec as P
 
 D = 768
@@ -464,30 +470,1029 @@
     return (adam_new, first_new, second_new, mlp_new, momentum_new, loss_total, grad_norm)
 
 
+ROWS = 48
+COLS = 48
+GROUP = 16
+OWN = 3
+TOK = ROWS * OWN
+HALF_TOK = TOK // 2
+PAIRS = 12
+LANES = 128
+WIDE = NB * LANES
+FREQ = PAIRS * 96
+NARROW = jnp.bfloat16
+WINDOW = 212
+EMBED_AT = 2
+Z_AXES = ("zh", "zl")
+EMBED_SIZE = 3 * PIX * D
+SUB_AXES = ("zh", "zl", "x", "y", "c")
+LAT_AXES = ("zh", "zl", "x")
+LON_AXES = ("y", "c")
+ITEM_AXES = ("zl", "x", "y", "c")
+
+
+def shift_tables():
+    table = np.zeros((3, TOK, TOK), np.float32)
+    spots = np.arange(TOK)
+    for offset in range(3):
+        table[offset, spots, (spots + OWN * (offset - 1)) % TOK] = 1.0
+    return table
+
+
+def row_table():
+    table = np.zeros((TOK, TOK), np.float64)
+    rows = np.arange(ROWS)
+    for pair in range(2 * PAIRS):
+        if pair == 0:
+            waves = (np.ones(ROWS), np.cos(np.pi * rows))
+        else:
+            angle = 2.0 * np.pi * (pair * rows % ROWS) / ROWS
+            waves = (np.cos(angle), np.sin(angle))
+        for part in range(2):
+            for own in range(OWN):
+                table[pair * 6 + part * OWN + own, rows * OWN + own] = waves[part]
+    return table / math.sqrt(ROWS)
+
+
+def column_tables():
+    freq = np.arange(COLS)[:, None]
+    table = np.zeros((2, 192, 128), np.float64)
+    for source in range(GROUP):
+        quad, lon = source // 4, source % 4
+        for own in range(OWN):
+            column = lon * 12 + quad * OWN + own
+            angle = 2.0 * np.pi * (freq[:, 0] * column % COLS) / COLS
+            cosine, sine = np.cos(angle), np.sin(angle)
+            first, second = source * 8 + own, source * 8 + OWN + own
+            table[0, 0:48, first] = cosine
+            table[0, 96:144, first] = -sine
+            table[0, 48:96, second] = cosine
+            table[0, 144:192, second] = -sine
+            table[1, 0:48, first] = cosine
+            table[1, 48:96, first] = cosine
+            table[1, 96:144, first] = -sine
+            table[1, 144:192, first] = -sine
+            table[1, 0:48, second] = -sine
+            table[1, 48:96, second] = sine
+            table[1, 96:144, second] = -cosine
+            table[1, 144:192, second] = cosine
+    return table / math.sqrt(COLS)
+
+
+def spread_table():
+    table = np.zeros((384, 512), np.float32)
+    spots = np.arange(384)
+    table[spots, spots // BS * LANES + spots % BS] = 1.0
+    return table
+
+
+def two_terms(table):
+    high = table.astype(ml_dtypes.bfloat16)
+    low = (table - high.astype(np.float64)).astype(ml_dtypes.bfloat16)
+    return np.stack([high, low])
+
+
+def dot(left, right):
+    return lax.dot_general(left, right, (((1,), (0,)), ((), ())), preferred_element_type=jnp.float32)
+
+
+def dot_nt(left, right):
+    return lax.dot_general(left, right, (((1,), (1,)), ((), ())), preferred_element_type=jnp.float32)
+
+
+def dot_tn(left, right):
+    return lax.dot_general(left, right, (((0,), (0,)), ((), ())), preferred_element_type=jnp.float32)
+
+
+def normalize(values):
+    center = values - jnp.mean(values, axis=-1, keepdims=True)
+    inverse = lax.rsqrt(jnp.mean(center * center, axis=-1, keepdims=True) + NORM_EPS)
+    return center * inverse, inverse
+
+
+def normalize_back(upstream, scaled, inverse, gain):
+    inner = upstream * gain
+    return inverse * (
+        inner
+        - jnp.mean(inner, axis=-1, keepdims=True)
+        - scaled * jnp.mean(inner * scaled, axis=-1, keepdims=True)
+    )
+
+
+def column_sum(values):
+    return jnp.sum(values, axis=0, keepdims=True)
+
+
+def bell(values):
+    return 0.5 * (1.0 + lax.erf(values * math.sqrt(0.5)))
+
+
+def bell_slope(values, area):
+    return area + values * jnp.exp(-0.5 * values * values) * (1.0 / math.sqrt(2.0 * math.pi))
+
+
+def send_rows(low, spread_ref, row_ref, out_ref):
+    wide = jnp.concatenate(
+        [dot(low[:, :384], spread_ref[...]), dot(low[:, 384:], spread_ref[...])], axis=1
+    ).astype(NARROW)
+    turned = dot(row_ref[0], wide) + dot(row_ref[1], wide)
+    for side in range(2):
+        for block in range(NB):
+            out_ref[side * NB + block] = turned[
+                side * HALF_TOK : (side + 1) * HALF_TOK, block * LANES : (block + 1) * LANES
+            ].astype(NARROW)
+
+
+def take_rows(in_ref, spread_ref, row_back_ref):
+    sides = []
+    for side in range(2):
+        sides.append(
+            jnp.concatenate(
+                [in_ref[side * NB + block].astype(jnp.float32) for block in range(NB)], axis=1
+            )
+        )
+    wide = jnp.concatenate(sides, axis=0).astype(NARROW)
+    low = jnp.concatenate(
+        [dot_nt(wide[:, :512], spread_ref[...]), dot_nt(wide[:, 512:], spread_ref[...])], axis=1
+    ).astype(NARROW)
+    return dot(row_back_ref[0], low) + dot(row_back_ref[1], low)
+
+
+def fetch(sources, held_ref, sems):
+    copies = [pltpu.make_async_copy(src, held_ref.at[i], sems.at[i]) for i, src in enumerate(sources)]
+    for copy in copies:
+        copy.start()
+    return copies
+
+
+def thirds(w_ref, size):
+    return [w_ref.at[pl.ds(i * size, size)] for i in range(3)]
+
+
+def embed_kernel(src_ref, shift_ref, bias_ref, norm_ref, spread_ref, row_ref, w_ref,
+                 state_ref, send_ref, held_ref, sems):
+    copies = fetch(thirds(w_ref, PIX), held_ref, sems)
+    src = src_ref[...]
+    state = bias_ref[...]
+    for offset in range(3):
+        moved = src if offset == 1 else dot(shift_ref[offset], src).astype(NARROW)
+        copies[offset].wait()
+        state = state + dot(moved, held_ref[offset])
+    state_ref[...] = state
+    scaled, _unused = normalize(state)
+    normed = scaled * norm_ref[0:1] + norm_ref[1:2]
+    send_rows(normed.astype(NARROW), spread_ref, row_ref, send_ref)
+
+
+def turn_columns(wide_ref, col_ref, pair):
+    kind = 0 if pair == 0 else 1
+    low = wide_ref[:, 6 * pair : 6 * pair + 8, :].reshape(128, 128).astype(NARROW)
+    both = dot(col_ref[0, kind], low) + dot(col_ref[1, kind], low)
+    return jnp.concatenate([both[:96], both[96:]], axis=1).astype(NARROW)
+
+
+def back_columns(wide_ref, col_back_ref, pair, low):
+    kind = 0 if pair == 0 else 1
+    both = jnp.concatenate([low[:, :128], low[:, 128:]], axis=0)
+    back = dot(col_back_ref[0, kind], both) + dot(col_back_ref[1, kind], both)
+    wide_ref[:, 6 * pair : 6 * pair + 8, :] = back.reshape(16, 8, 128)
+
+
+def spec_kernel(
+    in_ref, col_ref, col_back_ref, w_ref, b_ref, out_ref, mixed_ref, wide_ref, wide_out_ref
+):
+    wide_ref[:, :HALF_TOK, :] = in_ref[...].astype(jnp.float32)
+    wide_ref[:, HALF_TOK:, :] = jnp.zeros((16, 8, 128), jnp.float32)
+    for chunk in range(4):
+        pairs = range(chunk * 3, chunk * 3 + 3)
+        mixed = jnp.concatenate([turn_columns(wide_ref, col_ref, pair) for pair in pairs], axis=0)
+        mixed_ref[chunk * 288 : (chunk + 1) * 288, :] = mixed
+        inner = dot(mixed, w_ref[0]) + b_ref[0:1]
+        act = (inner * bell(inner)).astype(NARROW)
+        outer = (dot(act, w_ref[1]) + b_ref[1:2]).astype(NARROW)
+        for place, pair in enumerate(pairs):
+            back_columns(wide_out_ref, col_back_ref, pair, outer[place * 96 : place * 96 + 96])
+    out_ref[...] = wide_out_ref[:, :HALF_TOK, :].astype(NARROW)
+
+
+def spec_back_kernel(
+    in_ref, col_ref, col_back_ref, w_ref, b_ref, mixed_ref,
+    out_ref, gw_ref, gb_ref, wide_ref, wide_out_ref,
+):
+    wide_ref[:, :HALF_TOK, :] = in_ref[...].astype(jnp.float32)
+    wide_ref[:, HALF_TOK:, :] = jnp.zeros((16, 8, 128), jnp.float32)
+    for chunk in range(4):
+        pairs = range(chunk * 3, chunk * 3 + 3)
+        g_outer = jnp.concatenate([turn_columns(wide_ref, col_ref, pair) for pair in pairs], axis=0)
+        mixed = mixed_ref[chunk * 288 : (chunk + 1) * 288, :]
+        inner = dot(mixed, w_ref[0]) + b_ref[0:1]
+        area = bell(inner)
+        act = (inner * area).astype(NARROW)
+        g_inner = (bell_slope(inner, area) * dot_nt(g_outer, w_ref[1])).astype(NARROW)
+        g_mixed = dot_nt(g_inner, w_ref[0]).astype(NARROW)
+        first, second = dot_tn(mixed, g_inner), dot_tn(act, g_outer)
+        sums = jnp.concatenate(
+            [column_sum(g_inner.astype(jnp.float32)), column_sum(g_outer.astype(jnp.float32))], axis=0
+        )
+        if chunk == 0:
+            gw_ref[0], gw_ref[1], gb_ref[...] = first, second, sums
+        else:
+            gw_ref[0] += first
+            gw_ref[1] += second
+            gb_ref[...] += sums
+        for place, pair in enumerate(pairs):
+            back_columns(wide_out_ref, col_back_ref, pair, g_mixed[place * 96 : place * 96 + 96])
+    out_ref[...] = wide_out_ref[:, :HALF_TOK, :].astype(NARROW)
+
+
+def mlp_kernel(has_next, in_ref, state_ref, norm_ref, next_norm_ref, up_b_ref, down_b_ref,
+               spread_ref, row_ref, row_back_ref, w0_ref, w1_ref, w2_ref, w3_ref, *rest):
+    held_ref, sems = rest[-2:]
+    mixed_ref, hidden_in_ref, before_ref, hidden_ref, out_ref = rest[:5]
+    copies = fetch((w0_ref, w1_ref, w2_ref, w3_ref), held_ref, sems)
+    spatial = take_rows(in_ref, spread_ref, row_back_ref)
+    state = state_ref[...]
+    scaled, _unused = normalize(state)
+    mixed = state + spatial + (scaled * norm_ref[0:1] + norm_ref[1:2])
+    mixed_ref[...] = mixed
+    again, _unused = normalize(mixed)
+    hidden_in = (again * norm_ref[2:3] + norm_ref[3:4]).astype(NARROW)
+    hidden_in_ref[...] = hidden_in
+    out = mixed + down_b_ref[...]
+    for part in range(4):
+        spot = slice(part * D, (part + 1) * D)
+        copies[part].wait()
+        before = dot_nt(hidden_in, held_ref[part, 0]) + up_b_ref[:, spot]
+        before_ref[:, spot] = before
+        hidden = (before * bell(before)).astype(NARROW)
+        hidden_ref[:, spot] = hidden
+        out = out + dot(hidden, held_ref[part, 1])
+    out_ref[...] = out
+    if has_next:
+        scaled, _unused = normalize(out)
+        normed = scaled * next_norm_ref[0:1] + next_norm_ref[1:2]
+        send_rows(normed.astype(NARROW), spread_ref, row_ref, rest[5])
+
+
+def head_kernel(state_ref, shift_ref, bias_ref, target_ref, weight_ref, w_ref,
+                low_ref, pred_ref, grad_ref, loss_ref, held_ref, sems):
+    copies = fetch(thirds(w_ref, D), held_ref, sems)
+    low = state_ref[...].astype(NARROW)
+    low_ref[...] = low
+    predicted = bias_ref[...]
+    for offset in range(3):
+        moved = low if offset == 1 else dot(shift_ref[offset], low).astype(NARROW)
+        copies[offset].wait()
+        predicted = predicted + dot(moved, held_ref[offset])
+    pred_ref[...] = predicted.astype(NARROW)
+    differ = predicted - target_ref[...].astype(jnp.float32)
+    loss_ref[...] = column_sum(weight_ref[:, 0:1] * differ * differ)
+    grad_ref[...] = weight_ref[:, 1:2] * differ
+
+
+def head_back_kernel(grad_ref, shift_ref, w_ref, low_ref, sum_ref, out_ref, held_ref, sems):
+    copies = fetch(thirds(w_ref, D), held_ref, sems)
+    low = grad_ref[...].astype(NARROW)
+    low_ref[...] = low
+    sum_ref[...] = column_sum(low.astype(jnp.float32))
+    total = None
+    for offset in range(3):
+        moved = low if offset == 1 else dot(shift_ref[2 - offset], low).astype(NARROW)
+        copies[offset].wait()
+        part = dot_nt(moved, held_ref[offset])
+        total = part if total is None else total + part
+    out_ref[...] = total
+
+
+def embed_back_kernel(low_ref, shift_ref, add_ref, w_ref, out_ref, held_ref, sems):
+    copies = fetch(thirds(w_ref, PIX), held_ref, sems)
+    low = low_ref[...]
+    total = add_ref[...]
+    for offset in range(3):
+        moved = low if offset == 1 else dot(shift_ref[2 - offset], low).astype(NARROW)
+        copies[offset].wait()
+        total = total + dot_nt(moved, held_ref[offset])
+    out_ref[...] = total
+
+
+def mlp_back_kernel(up_ref, before_ref, mixed_ref, norm_ref, spread_ref, row_ref,
+                    w0_ref, w1_ref, w2_ref, w3_ref,
+                    grad_out_ref, g_before_ref, g_mixed_ref, g_up_b_ref, sums_ref, send_ref,
+                    held_ref, sems):
+    copies = fetch((w0_ref, w1_ref, w2_ref, w3_ref), held_ref, sems)
+    upstream = up_ref[...]
+    grad_out = upstream.astype(NARROW)
+    grad_out_ref[...] = grad_out
+    sums_ref[0:1] = column_sum(grad_out.astype(jnp.float32))
+    g_second = None
+    for part in range(4):
+        spot = slice(part * D, (part + 1) * D)
+        before = before_ref[:, spot]
+        slope = bell_slope(before, bell(before))
+        copies[part].wait()
+        g_before = (slope * dot_nt(grad_out, held_ref[part, 1])).astype(NARROW)
+        g_before_ref[:, spot] = g_before
+        g_up_b_ref[:, spot] = column_sum(g_before.astype(jnp.float32))
+        now = dot(g_before, held_ref[part, 0])
+        g_second = now if g_second is None else g_second + now
+    scaled, inverse = normalize(mixed_ref[...])
+    sums_ref[1:2] = column_sum(g_second * scaled)
+    sums_ref[2:3] = column_sum(g_second)
+    g_mixed = upstream + normalize_back(g_second, scaled, inverse, norm_ref[2:3])
+    g_mixed_ref[...] = g_mixed
+    send_rows(g_mixed.astype(NARROW), spread_ref, row_ref, send_ref)
+
+
+def norm_back_kernel(in_ref, g_mixed_ref, state_ref, norm_ref, spread_ref, row_back_ref,
+                     out_ref, low_ref, sums_ref):
+    g_mixed = g_mixed_ref[...]
+    g_normed = take_rows(in_ref, spread_ref, row_back_ref) + g_mixed
+    scaled, inverse = normalize(state_ref[...])
+    out = g_mixed + normalize_back(g_normed, scaled, inverse, norm_ref[0:1])
+    out_ref[...] = out
+    low = out.astype(NARROW)
+    low_ref[...] = low
+    sums_ref[0:1] = column_sum(g_normed * scaled)
+    sums_ref[1:2] = column_sum(g_normed)
+    sums_ref[2:3] = column_sum(low.astype(jnp.float32))
+
+
+def muon_kernel(level_ref, momentum_ref, weight_ref, change_ref, out_ref):
+    momentum = momentum_ref[...]
+    ortho = POLY_COEF[0] * POLY_COEF[0] * level_ref[pl.program_id(0)] * momentum
+    ortho = ortho + dot(momentum.astype(NARROW), change_ref[...])
+    out_ref[...] = weight_ref[...] * (1.0 - MUON_RATE * DECAY_RATE) - MUON_RATE * (FF / D) ** 0.5 * ortho
+
+
+def launch(kernel, name, out_dims, operands, far=(), far_out=False, near=(), scratch=(), limit=28):
+    anywhere = pl.BlockSpec(memory_space=pl.ANY)
+    local = pl.BlockSpec(memory_space=pltpu.VMEM)
+    in_specs = []
+    for i in range(len(operands)):
+        if i in near:
+            in_specs.append(pl.BlockSpec(memory_space=pltpu.SMEM))
+        else:
+            in_specs.append(anywhere if i in far else local)
+    return pl.pallas_call(
+        kernel,
+        name=name,
+        out_shape=[jax.ShapeDtypeStruct(dims, kind) for dims, kind in out_dims],
+        in_specs=in_specs,
+        out_specs=[anywhere if far_out else local for unused in out_dims],
+        scratch_shapes=list(scratch),
+        compiler_params=pltpu.CompilerParams(vmem_limit_bytes=limit * 1024 * 1024),
+    )(*operands)
+
+
+def exchange(values):
+    return lax.all_to_all(values, ITEM_AXES, split_axis=0, concat_axis=0, tiled=True)
+
+
+def total_over(values, axes):
+    count = lax.axis_size(axes)
+    spread = jnp.broadcast_to(jnp.pad(values, (0, LANES - values.shape[0])), (count, 1, LANES))
+    got = lax.all_to_all(spread, axes, split_axis=0, concat_axis=0, tiled=True)
+    return jnp.sum(got, axis=(0, 1))[: values.shape[0]]
+
+
+KINDS = {"embed": (D, 6), "head": (PIX, 10), "rest": (LANES, 1)}
+
+
+def kind_ranges(total):
+    edges = (0, EMBED_SIZE, 2 * EMBED_SIZE, total)
+    return dict(zip(KINDS, zip(edges[:-1], edges[1:])))
+
+
+def window_pieces(index, width, total):
+    found = []
+    for kind, (low, high) in kind_ranges(total).items():
+        begin, end = max(index * width, low), min((index + 1) * width, high)
+        if begin >= end:
+            continue
+        row, tiles = KINDS[kind]
+        first = (begin - low) // (8 * row)
+        last = -(-(end - low) // (8 * row))
+        found.append([kind, first, last, 0, begin, end])
+    spot = {"embed": EMBED_AT, "head": 0, "rest": 0}
+    kinds = [piece[0] for piece in found]
+    for piece in found:
+        piece[3] = spot[piece[0]]
+    if kinds == ["embed", "head"]:
+        used = (found[1][2] - found[1][1]) * 10
+        found[0][3] = EMBED_AT + -(-(used - EMBED_AT) // 6) * 6
+    if kinds == ["head", "rest"]:
+        found[1][3] = (found[0][2] - found[0][1]) * 10
+    for piece in found:
+        assert piece[3] + (piece[2] - piece[1]) * KINDS[piece[0]][1] <= WINDOW
+    return found
+
+
+def form_tables(width, total, count):
+    starts = {kind: np.zeros(count, np.int32) for kind in KINDS}
+    lows = {kind: np.zeros(count, np.int32) for kind in KINDS}
+    highs = {kind: np.zeros(count, np.int32) for kind in KINDS}
+    for index in range(count):
+        for kind, first, last, tile, begin, end in window_pieces(index, width, total):
+            row, tiles = KINDS[kind]
+            base = EMBED_AT if kind == "embed" else 0
+            own = begin - kind_ranges(total)[kind][0] - first * 8 * row
+            lows[kind][index] = begin - index * width
+            highs[kind][index] = end - index * width
+            starts[kind][index] = (tile - base) * 8 * LANES + own - lows[kind][index]
+    return starts, lows, highs
+
+
+def form_tiles(kind):
+    if kind == "embed":
+        return EMBED_AT, (WINDOW - EMBED_AT) // 6
+    return (0, WINDOW // 10) if kind == "head" else (0, WINDOW)
+
+
+def own_window(own, device, width, total, count):
+    starts, lows, highs = form_tables(width, total, count)
+    spot = jnp.arange(width, dtype=jnp.int32)
+    window = jnp.zeros((WINDOW, 8, LANES), jnp.float32)
+    for kind, (row, tiles) in KINDS.items():
+        start, low, high = (jnp.asarray(t[kind])[device] for t in (starts, lows, highs))
+        first, groups = form_tiles(kind)
+        length = groups * tiles * 8 * LANES
+        held = jnp.where((spot >= low) & (spot < high), own, 0.0)
+        held = jnp.pad(held, (length, length))
+        form = lax.dynamic_slice(held, (length - start,), (length,))
+        form = form.reshape(groups, 8, tiles, LANES).transpose(0, 2, 1, 3).reshape(-1, 8, LANES)
+        window = window + jnp.pad(form, ((first, WINDOW - first - groups * tiles), (0, 0), (0, 0)))
+    return window.astype(NARROW)
+
+
+def own_range(window, device, width, total, count):
+    starts, lows, highs = form_tables(width, total, count)
+    spot = jnp.arange(width, dtype=jnp.int32)
+    result = jnp.zeros((width,), jnp.float32)
+    for kind, (row, tiles) in KINDS.items():
+        start, low, high = (jnp.asarray(t[kind])[device] for t in (starts, lows, highs))
+        first, groups = form_tiles(kind)
+        form = window[first : first + groups * tiles].reshape(groups, tiles, 8, LANES)
+        form = jnp.pad(form.transpose(0, 2, 1, 3).reshape(-1), (width, width))
+        held = lax.dynamic_slice(form, (width + start,), (width,))
+        result = jnp.where((spot >= low) & (spot < high), held, result)
+    return result
+
+
+def join_plan(kind, width, total, count):
+    pieces = []
+    for index in range(count):
+        for piece in window_pieces(index, width, total):
+            if piece[0] == kind:
+                pieces.append((index,) + tuple(piece[1:4]))
+    single, double = [], []
+    for place, (index, first, last, tile) in enumerate(pieces):
+        if place:
+            shared = pieces[place - 1][2]
+            before = pieces[place - 1]
+            if shared > first:
+                double.append((first, shared, before[0], before[3], before[1], index, tile))
+        else:
+            shared = first
+        follow = pieces[place + 1][1] if place + 1 < len(pieces) else last
+        begin, end = max(first, shared), min(last, follow)
+        if begin < end:
+            single.append((begin, end, index, tile, first))
+    return single, double
+
+
+def join_kernel(tiles, single, double, got_ref, out_ref, left_ref, right_ref, sems, left_sems, right_sems):
+    copies = []
+    for place, (begin, end, index, tile, first) in enumerate(single):
+        source = got_ref.at[index, pl.ds(tile + (begin - first) * tiles, (end - begin) * tiles)]
+        target = out_ref.at[pl.ds(begin * tiles, (end - begin) * tiles)]
+        copies.append(pltpu.make_async_copy(source, target, sems.at[place]))
+    loads = []
+    for place, (begin, end, before, before_tile, before_first, index, tile) in enumerate(double):
+        size = (end - begin) * tiles
+        source = got_ref.at[before, pl.ds(before_tile + (begin - before_first) * tiles, size)]
+        loads.append(pltpu.make_async_copy(source, left_ref.at[place, pl.ds(0, size)], left_sems.at[place]))
+        source = got_ref.at[index, pl.ds(tile, size)]
+        loads.append(pltpu.make_async_copy(source, right_ref.at[place, pl.ds(0, size)], right_sems.at[place]))
+    for copy in loads + copies:
+        copy.start()
+    for copy in loads:
+        copy.wait()
+    stores = []
+    for place, (begin, end, *unused) in enumerate(double):
+        size = (end - begin) * tiles
+        total = left_ref[place, :size].astype(jnp.float32) + right_ref[place, :size].astype(jnp.float32)
+        left_ref[place, :size] = total.astype(NARROW)
+        target = out_ref.at[pl.ds(begin * tiles, size)]
+        stores.append(pltpu.make_async_copy(left_ref.at[place, pl.ds(0, size)], target, left_sems.at[place]))
+        stores[-1].start()
+    for copy in copies + stores:
+        copy.wait()
+
+
+def join_windows(got, kind, width, total, count):
+    row, tiles = KINDS[kind]
+    low, high = kind_ranges(total)[kind]
+    single, double = join_plan(kind, width, total, count)
+    groups = -(-(high - low) // (8 * row))
+    deep = max([(d[1] - d[0]) * tiles for d in double] + [1])
+    held = pltpu.VMEM((max(len(double), 1), deep, 8, LANES), NARROW)
+    sem = pltpu.SemaphoreType.DMA
+    (out,) = launch(
+        functools.partial(join_kernel, tiles, single, double), "join_" + kind,
+        [((groups * tiles, 8, LANES), NARROW)], [got], far=(0,), far_out=True,
+        scratch=(held, held, sem((max(len(single), 1),)), sem((max(len(double), 1),)), sem((max(len(double), 1),))),
+    )
+    return out.reshape(groups, tiles, 8, LANES).transpose(0, 2, 1, 3).reshape(groups * 8, row)
+
+
+def pack_plan(width, total, count):
+    plan = []
+    for index in range(count):
+        for kind, first, last, tile, begin, end in window_pieces(index, width, total):
+            tiles = KINDS[kind][1]
+            if kind == "rest":
+                plan.append((index, 6, first, last - first, tile))
+                continue
+            size = (PIX if kind == "embed" else D) // 8
+            while first < last:
+                source = first // size
+                stop = min(last, (source + 1) * size)
+                number = source + (0 if kind == "embed" else 3)
+                plan.append((index, number, (first - source * size) * tiles, (stop - first) * tiles, tile))
+                tile += (stop - first) * tiles
+                first = stop
+    return plan
+
+
+def pack_kernel(plan, place_ref, *refs):
+    sources, (keep_ref, send_ref, sems) = refs[:7], refs[7:]
+    x, y, c = place_ref[0], place_ref[1], place_ref[2]
+    ends = []
+    for number, (index, source, begin, size, tile) in enumerate(plan):
+        plane, side, depth, core = index // 8, index // 4 % 2, index // 2 % 2, index % 2
+        spot = (plane, (side + x) % 2, (depth + y) % 2, pl.ds(tile, size))
+        from_ref = sources[source].at[pl.ds(begin, size)]
+        keep = pltpu.make_async_copy(from_ref, keep_ref.at[spot], sems.at[number])
+        send = pltpu.make_async_copy(from_ref, send_ref.at[spot], sems.at[number])
+
+        @pl.when(c == core)
+        def _():
+            keep.start()
+
+        @pl.when(c != core)
+        def _():
+            send.start()
+
+        ends.append(keep)
+    for copy in ends:
+        copy.wait()
+
+
+def tiles_of(values):
+    rows, columns = values.shape
+    split = values.reshape(rows // 8, 8, columns // LANES, LANES)
+    return split.transpose(0, 2, 1, 3).reshape(-1, 8, LANES)
+
+
+def swap(values, axis):
+    return lax.ppermute(values, axis, [(0, 1), (1, 0)])
+
+
+def add_low(left, right):
+    return (left.astype(jnp.float32) + right.astype(jnp.float32)).astype(NARROW)
+
+
+def chip_sum(kept, x_dim, y_dim, cut_dim):
+    half = kept.shape[cut_dim] // 2
+
+    def side(values, dim, which):
+        return lax.index_in_dim(values, which, dim, keepdims=True)
+
+    parts = []
+    for start, order in ((0, ((x_dim, "x"), (y_dim, "y"))), (half, ((y_dim, "y"), (x_dim, "x")))):
+        value = lax.slice_in_dim(kept, start, start + half, axis=cut_dim)
+        for dim, axis in order:
+            value = add_low(side(value, dim, 0), swap(side(value, dim, 1), axis))
+        parts.append(value)
+    return jnp.concatenate(parts, axis=cut_dim)
+
+
+def line_sum(parts, owners):
+    plane = lax.axis_index(Z_AXES)
+
+    def pick(number):
+        return lax.dynamic_index_in_dim(
+            parts, jnp.clip(number - owners[0], 0, len(owners) - 1), 0, keepdims=False
+        )
+
+    total = pick(plane).astype(jnp.float32)
+    for mirror in (False, True):
+        here = 3 - plane if mirror else plane
+        moving = None
+        for step in (1, 2, 3):
+            pairs = []
+            for spot in range(3):
+                number = 4 - step + spot
+                owner = 3 - number if mirror else number
+                if number > 3 or owner not in owners:
+                    continue
+                pairs.append((3 - spot, 2 - spot) if mirror else (spot, spot + 1))
+            if not pairs:
+                continue
+            number = 4 - step + here
+            value = pick(3 - number if mirror else number)
+            if moving is not None:
+                value = add_low(value, moving)
+            moving = lax.ppermute(value, Z_AXES, pairs)
+        total = total + moving.astype(jnp.float32)
+    return total
+
+
+def plane_sum(values):
+    rows = values.shape[0]
+    core = lax.axis_index("c")
+    halves = values.reshape(2, rows // 2, values.shape[1])
+    kept = lax.dynamic_index_in_dim(halves, core, 0, keepdims=False)
+    sent = lax.dynamic_index_in_dim(halves, 1 - core, 0, keepdims=False).astype(NARROW)
+    kept = kept + swap(sent, "c").astype(jnp.float32)
+    quarter = rows // 4
+    parts = []
+    for start, order in ((0, ("x", "y")), (quarter, ("y", "x"))):
+        value = kept[start : start + quarter]
+        for axis in order:
+            low = value.astype(NARROW)
+            value = low.astype(jnp.float32) + swap(low, axis).astype(jnp.float32)
+        parts.append(value)
+    mine = jnp.concatenate(parts, axis=0).astype(NARROW)
+    other = swap(mine, "c")
+    first = jnp.where(core == 0, mine, other)
+    second = jnp.where(core == 0, other, mine)
+    return jnp.concatenate([first, second], axis=0).astype(jnp.float32)
+
+
+def line_gather(own):
+    plane = lax.axis_index(Z_AXES)
+    below, above = [], []
+    value = own
+    for step in (1, 2, 3):
+        value = lax.ppermute(value, Z_AXES, [(i, i + 1) for i in range(step - 1, 3)])
+        below.append(value)
+    value = own
+    for step in (1, 2, 3):
+        value = lax.ppermute(value, Z_AXES, [(i, i - 1) for i in range(1, 5 - step)])
+        above.append(value)
+    stack = jnp.stack(below[::-1] + [own] + above)
+    return lax.dynamic_slice_in_dim(stack, 3 - plane, 4, 0)
+
+
+def unpack_rest(rest):
+    found = []
+    offset = 0
+    for dims in ((L, 2, 2, NB, BS, BS), (D,), (PIX,), (L, 2, 2, D), (L, 4, D), (L, FF + D)):
+        amount = math.prod(dims)
+        found.append(rest[offset : offset + amount].reshape(dims))
+        offset += amount
+    return found
+
+
+def fast_body(pixels, targets, mask, lat_rows, adam_params, adam_m, adam_v, mlp_weights, mlp_momentum):
+    lat_index, lon_index = lax.axis_index(LAT_AXES), lax.axis_index(LON_AXES)
+    device = lax.axis_index(SUB_AXES)
+    devices = lax.axis_size(SUB_AXES)
+    width = adam_params.shape[0]
+    total = width * devices
+    low_side = lax.axis_index("zl") == 0
+    x, y, c = lax.axis_index("x"), lax.axis_index("y"), lax.axis_index("c")
+    block = lax.axis_index(("x", "y", "c"))
+    shifts = jnp.asarray(shift_tables(), NARROW)
+    row_fwd = jnp.asarray(two_terms(row_table()))
+    row_back = jnp.asarray(two_terms(row_table().T))
+    col_fwd = jnp.asarray(two_terms(column_tables()))
+    col_back = jnp.asarray(two_terms(column_tables().transpose(0, 2, 1)))
+    col_fwd = jnp.where(low_side, col_fwd, col_fwd[:, 1:2])
+    col_back = jnp.where(low_side, col_back, col_back[:, 1:2])
+    spread = jnp.asarray(spread_table(), NARROW)
+
+    def to_items(values):
+        rest = values.shape[4:]
+        lead, items, rows, cols = values.shape[:4]
+        split = values.reshape((lead, items, rows, 4, OWN) + rest)
+        order = (1, 3, 0, 2, 4) + tuple(range(5, 5 + len(rest)))
+        packed = split.transpose(order).reshape((items * 4, lead * rows * OWN) + rest)
+        got = lax.all_to_all(packed, LAT_AXES, split_axis=0, concat_axis=0, tiled=True)
+        got = got.reshape((items * 4, lead, rows * OWN) + rest)
+        return jnp.moveaxis(got, 1, 0).reshape((lead, TOK) + rest)
+
+    windows = lax.all_gather(own_window(adam_params, device, width, total, devices), SUB_AXES)
+    turned_w = jnp.roll(mlp_weights, mlp_weights.shape[2] // 2, axis=2)
+    mlp_own = jnp.where(x == 0, mlp_weights, turned_w).astype(NARROW)
+    mlp_low = []
+    for depth in range(L):
+        own = mlp_own[depth]
+        if depth:
+            own, windows = lax.optimization_barrier((own, windows))
+        across_y = swap(own, "y")
+        mlp_low.append((own, across_y, swap(own, "c"), swap(across_y, "c")))
+    source = to_items(pixels[None])[0]
+    wanted = to_items(targets)
+    row_weight = jnp.sin(math.pi * (lat_rows.astype(jnp.float32) + 0.5) / ROWS)
+    weight_local = row_weight[None, :, None] * mask.astype(jnp.float32)
+    weights = to_items(weight_local[None])[0]
+    weight_sum = total_over(jnp.sum(weight_local)[None], SUB_AXES)[0]
+    loss_scale = 2.0 / (STEPS * PIX * weight_sum)
+    weight_pair = jnp.stack([weights, weights * loss_scale], axis=1)
+
+    embed_w = join_windows(windows, "embed", width, total, devices)
+    head_w = join_windows(windows, "head", width, total, devices)
+    rest = join_windows(windows, "rest", width, total, devices).reshape(-1)
+    spec_w, embed_b, head_b, spec_b, norm_params, mlp_b = unpack_rest(rest)
+    embed_b, head_b = embed_b.astype(jnp.float32)[None], head_b.astype(jnp.float32)[None]
+    norms = norm_params.astype(jnp.float32)
+    mlp_b = mlp_b.astype(jnp.float32)
+
+    def by_place(values):
+        values = jnp.where(y == 0, values, values[:, ::-1])
+        values = jnp.where(c == 0, values, values[:, :, ::-1])
+        return jnp.where(x == 0, values, values[:, :, :, ::-1])
+
+    up_b = by_place(mlp_b[:, :FF].reshape(L, 2, 2, 2, -1)).transpose(0, 2, 1, 3, 4).reshape(L, 1, FF)
+    down_b = mlp_b[:, None, FF:]
+    gap = LANES - BS
+    own_w = lax.dynamic_index_in_dim(spec_w, block, 3, keepdims=False)
+    own_w = jnp.pad(own_w, ((0, 0),) * 3 + ((0, gap), (0, gap)))
+    real, imag = own_w[:, :, 0], own_w[:, :, 1]
+    pair_w = jnp.concatenate(
+        [jnp.concatenate([real, imag], axis=-1), jnp.concatenate([-imag, real], axis=-1)], axis=-2
+    )
+    own_b = lax.dynamic_slice_in_dim(spec_b, block * BS, BS, 3).astype(jnp.float32)
+    pair_b = jnp.pad(own_b, ((0, 0),) * 3 + ((0, gap),)).reshape(L, 2, 2 * LANES)
+
+    f32 = jnp.float32
+    payload = ((GROUP, HALF_TOK, LANES), NARROW)
+    state_f32 = ((TOK, D), f32)
+    wide = pltpu.VMEM((GROUP, HALF_TOK + 8, LANES), f32)
+    sem = pltpu.SemaphoreType.DMA
+    held_mlp = (pltpu.VMEM((4, 2, D, D), NARROW), sem((4,)))
+    held_embed = (pltpu.VMEM((3, PIX, D), NARROW), sem((3,)))
+    held_head = (pltpu.VMEM((3, D, PIX), NARROW), sem((3,)))
+
+    current = source
+    saved = []
+    loss_sums = []
+    for roll_idx in range(STEPS):
+        state, sent = launch(
+            embed_kernel, "embed", [state_f32, payload],
+            [current, shifts, embed_b, norms[0], spread, row_fwd, embed_w], far=(6,),
+            scratch=held_embed,
+        )
+        layers = []
+        for depth in range(L):
+            got = exchange(sent)
+            out, mixed_in = launch(
+                spec_kernel, "spec", [payload, ((FREQ, 2 * LANES), NARROW)],
+                [got, col_fwd, col_back, pair_w[depth], pair_b[depth]], scratch=(wide, wide),
+            )
+            got = exchange(out)
+            has_next = depth + 1 < L
+            outs = [state_f32, ((TOK, D), NARROW), ((TOK, FF), f32), ((TOK, FF), NARROW), state_f32]
+            results = launch(
+                functools.partial(mlp_kernel, has_next), "mlp", outs + [payload] * has_next,
+                [got, state, norms[depth], norms[min(depth + 1, L - 1)], up_b[depth], down_b[depth],
+                 spread, row_fwd, row_back, *mlp_low[depth]], far=(9, 10, 11, 12), scratch=held_mlp,
+            )
+            layers.append((state, mixed_in) + tuple(results[:4]))
+            state = results[4]
+            if has_next:
+                sent = results[5]
+        low, predicted, loss_grad, loss_part = launch(
+            head_kernel, "head",
+            [((TOK, D), NARROW), ((TOK, PIX), NARROW), ((TOK, PIX), f32), ((1, PIX), f32)],
+            [state, shifts, head_b, wanted[roll_idx], weight_pair, head_w], far=(5,),
+            scratch=held_head,
+        )
+        loss_sums.append(loss_part)
+        saved.append((current, layers, low, loss_grad))
+        current = predicted
+
+    rows_own = mlp_momentum.shape[2] // 2
+    half_ff = FF // 2
+
+    def joined(terms, member):
+        return jnp.concatenate([now[member] for now in terms], axis=0)
+
+    def mlp_sends(depth):
+        g_before, hidden_in, hidden, grad_out = (joined(mlp_terms[depth], m) for m in range(4))
+        pairs = ((g_before, hidden_in), (hidden, grad_out))
+        return pairs, [swap(dot_tn(a[:, half_ff:], b).astype(NARROW), "c") for a, b in pairs]
+
+    def mlp_chip(pairs, got):
+        kept = [
+            (dot_tn(a[:, :half_ff], b) + sent.astype(f32)).astype(NARROW)
+            for (a, b), sent in zip(pairs, got)
+        ]
+        kept = jnp.stack(kept).reshape(2, 2, 2, rows_own, D)
+        return chip_sum(kept, 2, 1, 3).reshape(2, rows_own, D)
+
+    def mlp_line(depth, kept):
+        return line_sum(kept, [2 * depth, 2 * depth + 1])
+
+    head_terms, embed_terms = [], []
+    mlp_terms = [[] for unused in range(L)]
+    spec_terms = [[] for unused in range(L)]
+    sum_terms = [[] for unused in range(L)]
+    head_sums, embed_sums = [], []
+    upstream = None
+    for roll_idx in reversed(range(STEPS)):
+        current, layers, low, loss_grad = saved[roll_idx]
+        upstream = loss_grad if upstream is None else upstream
+        upstream_low, head_sum, grad_state = launch(
+            head_back_kernel, "head_back",
+            [((TOK, PIX), NARROW), ((1, PIX), f32), state_f32], [upstream, shifts, head_w],
+            far=(2,), scratch=held_head,
+        )
+        head_terms.append((low, upstream_low))
+        head_sums.append(head_sum)
+        for depth in reversed(range(L)):
+            state, mixed_in, mixed, hidden_in, before, hidden = layers[depth]
+            grad_out, g_before, g_mixed, g_up_b, sums_two, sent = launch(
+                mlp_back_kernel, "mlp_back",
+                [((TOK, D), NARROW), ((TOK, FF), NARROW), state_f32, ((1, FF), f32), ((3, D), f32),
+                 payload],
+                [grad_state, before, mixed, norms[depth], spread, row_fwd, *mlp_low[depth]],
+                far=(6, 7, 8, 9), scratch=held_mlp,
+            )
+            got = exchange(sent)
+            if roll_idx == 0 and depth == 0:
+                last_chip, got = lax.optimization_barrier((mlp_chip(*last_sends), got))
+            out, g_pair, g_pair_b = launch(
+                spec_back_kernel, "spec_back",
+                [payload, ((2, 2 * LANES, 2 * LANES), f32), ((2, 2 * LANES), f32)],
+                [got, col_fwd, col_back, pair_w[depth], pair_b[depth], mixed_in],
+                scratch=(wide, wide),
+            )
+            got = exchange(out)
+            if roll_idx == 0 and depth == 0:
+                mlp_second, got = lax.optimization_barrier((mlp_line(L - 1, last_chip), got))
+            grad_state, state_low, sums_one = launch(
+                norm_back_kernel, "norm_back", [state_f32, ((TOK, D), NARROW), ((3, D), f32)],
+                [got, g_mixed, state, norms[depth], spread, row_back],
+            )
+            mlp_terms[depth].append((g_before, hidden_in, hidden, grad_out))
+            if roll_idx == 0 and depth == L - 1:
+                pairs, sends = mlp_sends(depth)
+                grad_state, *sends = lax.optimization_barrier((grad_state, *sends))
+                last_sends = (pairs, sends)
+            spec_terms[depth].append((g_pair, g_pair_b))
+            sum_terms[depth].append((sums_one, sums_two, g_up_b))
+        embed_terms.append((current, state_low))
+        embed_sums.append(sums_one[2])
+        if roll_idx:
+            (upstream,) = launch(
+                embed_back_kernel, "embed_back", [((TOK, PIX), f32)],
+                [state_low, shifts, saved[roll_idx - 1][3], embed_w], far=(3,), scratch=held_embed,
+            )
+
+    mlp_first = mlp_line(0, mlp_chip(*mlp_sends(0)))
+    mlp_mine = jnp.where(lax.axis_index("zh") == 0, mlp_first, mlp_second)
+
+    def moved_pair(values, amount):
+        return jnp.concatenate([jnp.roll(now, amount, axis=0) for now in values], axis=0)
+
+    embed_src = joined(embed_terms, 0)
+    head_up = joined(head_terms, 1)
+    g_embed = [
+        dot_tn(embed_src, moved_pair([now[1] for now in embed_terms], OWN * (o - 1))).astype(NARROW)
+        for o in range(3)
+    ]
+    g_head = [
+        dot_tn(moved_pair([now[0] for now in head_terms], -OWN * (o - 1)), head_up).astype(NARROW)
+        for o in range(3)
+    ]
+    g_spec, g_spec_b, g_norm, g_mlp_b = [], [], [], []
+    for depth in range(L):
+        pair_sum = sum(now[0] for now in spec_terms[depth]).reshape(2, 2, LANES, 2, LANES)
+        pair_sum = pair_sum[:, :, :BS, :, :BS]
+        g_real = pair_sum[:, 0, :, 0] + pair_sum[:, 1, :, 1]
+        g_imag = pair_sum[:, 0, :, 1] - pair_sum[:, 1, :, 0]
+        g_spec.append(jnp.stack([g_real, g_imag], axis=1))
+        g_spec_b.append(sum(now[1] for now in spec_terms[depth]).reshape(2, 2, LANES)[:, :, :BS])
+        one = sum(now[0] for now in sum_terms[depth])
+        two = sum(now[1] for now in sum_terms[depth])
+        g_norm.append(jnp.stack([one[0], one[1], two[1], two[2]]))
+        up_sum = sum(now[2] for now in sum_terms[depth]).reshape(1, 2, 2, 2, -1)
+        up_sum = by_place(up_sum.transpose(0, 2, 1, 3, 4)).reshape(-1)
+        g_mlp_b.append(jnp.concatenate([up_sum, two[0]]))
+    full_spec = jnp.zeros((L, 2, 2, NB, BS, BS), NARROW)
+    full_spec = lax.dynamic_update_slice_in_dim(
+        full_spec, jnp.stack(g_spec).astype(NARROW)[:, :, :, None], block, 3
+    )
+    full_spec_b = lax.dynamic_update_slice_in_dim(
+        jnp.zeros((L, 2, 2, D), f32), jnp.stack(g_spec_b), block * BS, 3
+    )
+    small = jnp.concatenate(
+        [sum(embed_sums), sum(head_sums)[0], full_spec_b.reshape(-1),
+         jnp.stack(g_norm).reshape(-1), jnp.stack(g_mlp_b).reshape(-1)]
+    ).astype(NARROW)
+    rest_grad = jnp.concatenate([full_spec.reshape(-1), small])
+    rest_grad = jnp.pad(rest_grad, (0, -rest_grad.shape[0] % (8 * LANES))).reshape(-1, 8, LANES)
+    plan = pack_plan(width, total, devices)
+    window_set = ((4, 2, 2, WINDOW, 8, LANES), NARROW)
+    kept, sent = launch(
+        functools.partial(pack_kernel, plan), "pack", [window_set, window_set],
+        [jnp.stack([x, y, c])] + [tiles_of(g) for g in g_embed + g_head] + [rest_grad],
+        near=(0,), far_out=True, scratch=(sem((len(plan),)),), limit=8,
+    )
+    kept = chip_sum(add_low(kept, swap(sent, "c")), 1, 2, 3).reshape(4, WINDOW, 8, LANES)
+    flat_piece = own_range(line_sum(kept, [0, 1, 2, 3]), device, width, total, devices)
+    local = jnp.stack(
+        [jnp.sum(flat_piece * flat_piece) + jnp.sum(mlp_mine * mlp_mine),
+         sum(jnp.sum(now) for now in loss_sums)]
+    )
+    square_sum, loss_total = total_over(local, SUB_AXES)
+    loss_total = loss_total / (STEPS * PIX * weight_sum)
+    grad_norm = jnp.sqrt(square_sum)
+    factor = jnp.minimum(1.0, CLIP_LEVEL / (grad_norm + 1e-06))
+
+    mlp_grad = lax.all_gather(mlp_mine.astype(NARROW), LAT_AXES, axis=0, tiled=True)
+    mlp_grad = mlp_grad.reshape(mlp_momentum.shape).astype(f32)
+    momentum_new = MOMENT_KEEP * mlp_momentum + mlp_grad * factor
+
+    held = mlp_momentum.reshape(2 * L * 2, rows_own, D)
+    held = lax.dynamic_index_in_dim(held, lat_index, 0, keepdims=False)
+    mine_new = MOMENT_KEEP * held + mlp_mine * factor
+    high = lax.Precision.HIGH
+    gram = plane_sum(lax.dot_general(mine_new, mine_new, (((0,), (0,)), ((), ())), precision=high))
+    inverse = 1.0 / (jnp.sqrt(jnp.trace(gram)) + 1e-07)
+    lead, mid, last = POLY_COEF
+    square = gram * (inverse * inverse)
+    mul = functools.partial(jnp.dot, precision=high)
+    poly_one = mid * square + last * mul(square, square)
+    turned = mul(square, poly_one)
+    square_two = lead * lead * square + 2.0 * lead * turned + mul(turned, poly_one)
+    poly_two = mid * square_two + last * mul(square_two, square_two)
+    change = lead * (poly_one + poly_two) + mul(poly_one, poly_two)
+    level_high = inverse.astype(NARROW)
+    level_mid = (inverse - level_high.astype(f32)).astype(NARROW)
+    level_low = (inverse - level_high.astype(f32) - level_mid.astype(f32)).astype(NARROW)
+    extra = jnp.zeros((8, D), NARROW)
+    extra = extra.at[0, 0].set(level_high).at[0, 1].set(level_mid).at[0, 2].set(level_low)
+    change = lax.dynamic_slice_in_dim((change * inverse).astype(NARROW), c * (D // 2), D // 2, 0)
+    gathered = line_gather(jnp.concatenate([change, extra], axis=0))
+    levels = jnp.sum(gathered[:, D // 2, :3].astype(f32), axis=-1)
+    gathered = gathered[:, : D // 2]
+    other = swap(gathered, "c")
+    changes = jnp.concatenate(
+        [jnp.where(c == 0, gathered, other), jnp.where(c == 0, other, gathered)], axis=1
+    )
+    (mlp_new,) = pl.pallas_call(
+        muon_kernel,
+        name="muon",
+        grid=(2 * L, 2),
+        out_shape=[jax.ShapeDtypeStruct((2 * L, D, D), f32)],
+        in_specs=[pl.BlockSpec(memory_space=pltpu.SMEM)]
+        + [pl.BlockSpec((None, rows_own, D), lambda m, h: (m, h, 0))] * 2
+        + [pl.BlockSpec((None, D, D), lambda m, h: (m, 0, 0))],
+        out_specs=[pl.BlockSpec((None, rows_own, D), lambda m, h: (m, h, 0))],
+        compiler_params=pltpu.CompilerParams(vmem_limit_bytes=28 * 1024 * 1024),
+    )(levels, momentum_new.reshape(2 * L, D, D), mlp_weights.reshape(2 * L, D, D), changes)
+    mlp_new = mlp_new.reshape(mlp_weights.shape)
+
+    clipped = flat_piece * factor
+    first_new = BETA_FIRST * adam_m + (1.0 - BETA_FIRST) * clipped
+    second_new = BETA_SECOND * adam_v + (1.0 - BETA_SECOND) * clipped * clipped
+    count_value = float(STEP_NUM)
+    first_hat = first_new / (1.0 - BETA_FIRST**count_value)
+    second_hat = second_new / (1.0 - BETA_SECOND**count_value)
+    adam_new = adam_params - ADAM_RATE * (
+        first_hat / (jnp.sqrt(second_hat) + 1e-08) + DECAY_RATE * adam_params
+    )
+    return (adam_new, first_new, second_new, mlp_new, momentum_new, loss_total, grad_norm)
+
+
 def solution(mesh):
-    placed = (
-        P(None, "lat", "lon", None),
-        P(None, None, "lat", "lon", None),
-        P(None, "lat", "lon"),
-        P("lat"),
-        P(("lat", "lon")),
-        P(("lat", "lon")),
-        P(("lat", "lon")),
-        P(None, None, "lon", None),
-        P(None, None, "lon", None),
-    )
+    if tuple(mesh.shape.items()) == (("lat", 8), ("lon", 4)):
+        fine = Mesh(mesh.devices.reshape(2, 2, 2, 2, 2), SUB_AXES)
+        return placed(fast_body, fine, LAT_AXES, LON_AXES)
+    return placed(body, mesh, ("lat",), ("lon",))
+
+
+def placed(step, mesh, lat, lon):
+    flat = P(lat + lon)
+    halves = P(None, None, lon, None)
     return jax.shard_map(
-        body,
+        step,
         mesh=mesh,
-        in_specs=placed,
-        out_specs=(
-            P(("lat", "lon")),
-            P(("lat", "lon")),
-            P(("lat", "lon")),
-            P(None, None, "lon", None),
-            P(None, None, "lon", None),
-            P(),
-            P(),
+        in_specs=(
+            P(None, lat, lon, None),
+            P(None, None, lat, lon, None),
+            P(None, lat, lon),
+            P(lat),
+            flat,
+            flat,
+            flat,
+            halves,
+            halves,
         ),
+        out_specs=(flat, flat, flat, halves, halves, P(), P()),
         check_vma=False,
     )

time: 4670 us -> 1130 us (0.24)
  local copies, waits for them, and re-layouts: 1550 us -> 197 us
  waiting for transfers between devices: 1680 us -> 409 us
  matrix products: 528 us -> 54.1 us
  starting transfers between devices: 521 us -> 164 us
  Pallas kernels: 0 us -> 136 us
  blocking collectives: 129 us -> 24 us
  other arithmetic: 195 us -> 103 us
    unnamed x8 -> x2, waiting for transfers between devices: 1230 us -> 0.03 us
    unnamed x684 -> x431, local copies, waits for them, and re-layouts: 733 us -> 103 us
    dot_general x227 -> x20, matrix products: 528 us -> 54.1 us  [the longest x14 33 us: dot_tn(): lax.dot_general(left, right, (((0,), (0,)), ((), ())), preferred_element_...]
    all_to_all x144 -> x4, local copies, waits for them, and re-layouts: 427 us -> 3.41 us  [to_items(): lax.all_to_all(packed, LAT_AXES, split_axis=0, concat_axis=0, tiled=True)]
    all_to_all x106 -> x19, starting transfers between devices: 489 us -> 78.5 us  [the longest x14 58.1 us: exchange(): lax.all_to_all(values, ITEM_AXES, split_axis=0, concat_axis=0, tiled=True)]
    ppermute x14 -> x50, waiting for transfers between devices: 12.5 us -> 265 us  [the longest x30 170 us: swap(): return lax.ppermute(values, axis, [(0, 1), (1, 0)])]
    convert_element_type x110 -> x2, local copies, waits for them, and re-layouts: 188 us -> 0.09 us  [the longest x1 0.07 us: plane_sum(): lax.dynamic_index_in_dim(halves, 1 - core, 0, keepdims=False).astype(NARROW)]
    psum x2 -> x0, waiting for transfers between devices: 174 us -> none  [body(): lax.psum(partial_gram.astype(jnp.bfloat16), 'lon').astype(jnp.float32)]
  transfers between devices with their start and end apart: 126 -> 71, of which waited for: 50 -> 42; matrix products, arithmetic and copies ran while one was open for 25% -> 15% of each run, Pallas kernels for 0% -> 4%
where the time goes in v1:
time: 1130 us; the launch traced here: 1120 us
  waiting for transfers between devices  409 us (36%)
  local copies, waits for them, and re-layouts  197 us (17%)
  starting transfers between devices  164 us (15%)
  Pallas kernels  136 us (12%)
  other arithmetic  103 us (9%)
  matrix products  54.1 us (5%)
  between operations  33.6 us (3%)
  blocking collectives  24 us (2%)
    ppermute x30, waiting for transfers between devices, swap(): return lax.ppermute(values, axis, [(0, 1), (1, 0)])  170 us
    pallas_call x31, Pallas kernels, launch(): pl.pallas_call(kernel, name=name, out_shape=[jax.ShapeDtypeStruct(dims, k...  127 us
    unnamed x431, local copies, waits for them, and re-layouts  103 us
    all_to_all x14, waiting for transfers between devices, exchange(): lax.all_to_all(values, ITEM_AXES, split_axis=0, concat_axis=0, tiled=True)  67.6 us
    ppermute x3, waiting for transfers between devices, line_gather(): lax.ppermute(value, Z_AXES, [(i, i - 1) for i in range(1, 5 - step)])  67.4 us
    all_to_all x14, starting transfers between devices, exchange(): lax.all_to_all(values, ITEM_AXES, split_axis=0, concat_axis=0, tiled=True)  58.1 us
    ppermute x14, starting transfers between devices, line_sum(): moving = lax.ppermute(value, Z_AXES, pairs)  52.6 us
    dot_general x14, matrix products, dot_tn(): lax.dot_general(left, right, (((0,), (0,)), ((), ())), preferred_element_...  33 us
  transfers between devices with their start and end apart: 71, of which 42 were waited for; matrix products, arithmetic and copies ran while one was open for 15% of the time, Pallas kernels for 4%

profile of v1, /device:TPU:0, one launch (start us, length us, event | category | flops | bytes accessed | tf_op | source)
XLA Modules:
  0.0 1119.2 jit_solution(8542174925399271638)
XLA Ops:
  21.2 5.6 fusion.56
  32.2 6.5 fusion.149
  38.7 6.3 fusion
  59.3 19.1 %all-to-all-done = bf16[8,18,1280]{2,1,0:T(8,128)(2,1)S(1)} async-done(((bf16[8,18,1280]{2,1,0:T(8,128)(2,1)}), bf16[8,18,1280]{2,1,0:T(8,128)(2,1)S(1)}, u32[]{:S(2)}, u32[]{:S(2)}) %all-to-all-start) | async-done | bytes 368672 | tf_op jit(solution)/shard_map/all_to_all | solution.py:1182
  83.2 39.4 %collective-permute-done.w1_ref = bf16[2,768,768]{2,1,0:T(8,128)(2,1)} collective-permute-done((bf16[2,768,768]{2,1,0:T(8,128)(2,1)}, bf16[2,768,768]{2,1,0:T(8,128)(2,1)}, u32[]{:S(2)}, u32[]{:S(2)}) %collective-permute-start) | collective-permute-done | bytes 2359328 | tf_op jit(solution)/shard_map/ppermute | solution.py:1058
  122.6 29.8 %all-gather.6.cloned.1.call-done = bf16[6784,8,128]{2,1,0:T(8,128)(2,1)} async-done(((bf16[212,8,128]{2,1,0:T(8,128)(2,1)}), bf16[6784,8,128]{2,1,0:T(8,128)(2,1)}) %all-gather.6.cloned.1.call-update) | async-done | bytes 13893648 | tf_op jit(solution)/shard_map/all_gather | solution.py:1186
  189.3 30.3 %all-to-all-done.1.in_ref = bf16[16,72,128]{2,1,0:T(8,128)(2,1)} async-done(((bf16[16,72,128]{2,1,0:T(8,128)(2,1)}), bf16[16,72,128]{2,1,0:T(8,128)(2,1)}, u32[]{:S(2)}, u32[]{:S(2)}) %all-to-all-start.1) | async-done | bytes 294944 | tf_op jit(solution)/shard_map/all_to_all | solution.py:848
  248.6 6.8 mlp.4
  260.6 7.4 all-to-all-done.5
  307.5 6.9 mlp.5
  324.8 13.1 %all_to_all.109.in_ref = bf16[16,72,128]{2,1,0:T(8,128)(2,1)S(1)} all-to-all(bf16[16,72,128]{2,1,0:T(8,128)(2,1)S(1)} %get-tuple-element.155), channel_id=1, replica_groups=mesh['zh'=2,'zl'=2,'x'=2,'y'=2,'c'=2] {'zl','x','y','c'}, dimensions={0} | all-to-all | bytes 589824 | tf_op jit(solution)/shard_map/all_to_all | solution.py:848
  340.4 10.9 all_to_all.110.in_ref
  351.3 5.8 mlp.6
  385.6 5.1 all-to-all-done.11.in_ref
  391.8 6.8 mlp.7
  407.1 6.9 mlp_back.4
  440.7 5.0 all-to-all-done.13.in_ref
  449.7 6.1 mlp_back.5
  465.6 5.1 all-to-all-done.14.in_ref
  482.8 5.2 all-to-all-done.15.in_ref
  506.3 6.9 mlp_back.6
  540.7 5.5 all-to-all-start.17
  571.2 6.8 mlp_back.7
  583.4 12.3 %collective-permute-done.10 = bf16[2,1,2,192,768]{4,3,2,1,0:T(8,128)(2,1)} collective-permute-done((bf16[2,1,2,192,768]{4,3,2,1,0:T(8,128)(2,1)}, bf16[2,1,2,192,768]{4,3,2,1,0:T(8,128)(2,1)}, u32[]{:S(2)}, u32[]{:S(2)}) %collective-permute-start.10) | collective-permute-done | bytes 1179680 | tf_op jit(solution)/shard_map/ppermute | solution.py:1058
  604.5 9.0 collective-permute-done.11
  634.6 5.2 collective-permute-start.13
  673.0 9.1 pack.1
  689.2 7.9 collective-permute-done.28
  708.6 9.7 add_convert_fusion
  727.3 5.5 collective-permute-done.31
  736.1 51.5 %collective-permute-done.29 = bf16[2,2,1,192,768]{4,3,2,1,0:T(8,128)(2,1)} collective-permute-done((bf16[2,2,1,192,768]{4,3,2,1,0:T(8,128)(2,1)}, bf16[2,2,1,192,768]{4,3,2,1,0:T(8,128)(2,1)}, u32[]{:S(2)}, u32[]{:S(2)}) %collective-permute-start.29) | collective-permute-done | bytes 1179680 | tf_op jit(solution)/shard_map/ppermute | solution.py:1058
  800.3 5.3 collective-permute-done.30
  807.3 13.7 %collective-permute-done.18 = bf16[4,1,1,106,8,128]{5,4,3,2,1,0:T(8,128)(2,1)S(1)} collective-permute-done((bf16[4,1,1,106,8,128]{5,4,3,2,1,0:T(8,128)(2,1)S(1)}, bf16[4,1,1,106,8,128]{5,4,3,2,1,0:T(8,128)(2,1)S(1)}, u32[]{:S(2)}, u32[]{:S(2)}) %collective-permute-start.18) | collective-permute-done | bytes 868384 | tf_op jit(solution)/shard_map/ppermute | solution.py:1058
  822.5 15.6 %collective-permute-start.21 = (bf16[212,8,128]{2,1,0:T(8,128)(2,1)}, bf16[212,8,128]{2,1,0:T(8,128)(2,1)}, u32[]{:S(2)}, u32[]{:S(2)}) collective-permute-start(bf16[212,8,128]{2,1,0:T(8,128)(2,1)} %get-tuple-element.266), channel_id=1, source_target_pairs={{0,8},{1,9},{2,10},{3,11},{4,12},{5,13},{6,14},{7,15}} | collective-permute-start | bytes 1302536 | tf_op jit(solution)/shard_map/ppermute | solution.py:1106
  850.3 5.2 collective-permute-start.22
  867.4 9.4 collective-permute-start.23
  882.5 5.8 collective-permute-done.26
  894.8 6.8 multiply_reduce_fusion.1
  907.0 7.0 all-to-all-done.20
  922.7 8.1 collective-permute-done.38
  933.2 5.9 collective-permute-done.39
  970.8 12.2 %collective-permute-done.43 = bf16[392,768]{1,0:T(8,128)(2,1)S(1)} collective-permute-done((bf16[392,768]{1,0:T(8,128)(2,1)S(1)}, bf16[392,768]{1,0:T(8,128)(2,1)S(1)}, u32[]{:S(2)}, u32[]{:S(2)}) %collective-permute-start.43) | collective-permute-done | bytes 602144 | tf_op jit(solution)/shard_map/ppermute | solution.py:1138
  989.8 28.6 %collective-permute-done.47 = bf16[392,768]{1,0:T(8,128)(2,1)S(1)} collective-permute-done((bf16[392,768]{1,0:T(8,128)(2,1)S(1)}, bf16[392,768]{1,0:T(8,128)(2,1)S(1)}, u32[]{:S(2)}, u32[]{:S(2)}) %collective-permute-start.47) | collective-permute-done | bytes 602144 | tf_op jit(solution)/shard_map/ppermute | solution.py:1142
  1021.1 35.4 %collective-permute-done.48 = bf16[392,768]{1,0:T(8,128)(2,1)S(1)} collective-permute-done((bf16[392,768]{1,0:T(8,128)(2,1)S(1)}, bf16[392,768]{1,0:T(8,128)(2,1)S(1)}, u32[]{:S(2)}, u32[]{:S(2)}) %collective-permute-start.48) | collective-permute-done | bytes 602144 | tf_op jit(solution)/shard_map/ppermute | solution.py:1142
  1063.2 10.9 all-gather.4.cloned.1.call-done
  1074.1 6.7 convert_multiply_fusion
  1080.8 11.3 %multiply_add_fusion = f32[2,2,768,768]{3,2,1,0:T(8,128)} fusion(f32[2,2,768,768]{3,2,1,0:T(8,128)} %bitcast.339, f32[2,2,768,768]{3,2,1,0:T(8,128)} %param.47), kind=kLoop, calls=%fused_computation.4 | loop fusion | flops 4718592 | bytes 28311552 | tf_op jit(solution)/shard_map/add | solution.py:1418
  1101.2 8.4 muon.1
  (822 shorter events, 531.9 us)
Async XLA Ops:
  7.2 145.2 %all-gather.6.cloned.1.call-start = ((), (), s32[]{:S(2)}) async-start(), calls=%async_computation.22 | async-start | bytes 14327808 | tf_op jit(solution)/shard_map/all_gather | solution.py:1186
  47.6 75.0 %collective-permute-start = (bf16[2,768,768]{2,1,0:T(8,128)(2,1)}, bf16[2,768,768]{2,1,0:T(8,128)(2,1)}, u32[]{:S(2)}, u32[]{:S(2)}) collective-permute-start(bf16[2,768,768]{2,1,0:T(8,128)(2,1)} %get-tuple-element.260.w0_ref), channel_id=1, source_target_pairs={{0,2},{2,0},{1,3},{3,1},{4,6},{6,4},{5,7},{7,5},{8,10},{10,8},{9,1... | collective-permute-start | bytes 7077896 | tf_op jit(solution)/shard_map/ppermute | solution.py:1058
  50.8 196.8 %collective-permute-start.1 = (bf16[2,768,768]{2,1,0:T(8,128)(2,1)}, bf16[2,768,768]{2,1,0:T(8,128)(2,1)}, u32[]{:S(2)}, u32[]{:S(2)}) collective-permute-start(bf16[2,768,768]{2,1,0:T(8,128)(2,1)} %get-tuple-element.260.w0_ref), channel_id=1, source_target_pairs={{0,1},{1,0},{2,3},{3,2},{4,5},{5,4},{6,7},{7,6},{8,9},{9,8},{10,11... | collective-permute-start | bytes 7077896 | tf_op jit(solution)/shard_map/ppermute | solution.py:1058
  51.9 26.5 %all-to-all-start = ((bf16[8,18,1280]{2,1,0:T(8,128)(2,1)}), bf16[8,18,1280]{2,1,0:T(8,128)(2,1)S(1)}, u32[]{:S(2)}, u32[]{:S(2)}) async-start(bf16[8,18,1280]{2,1,0:T(8,128)(2,1)} %copy.166), calls=%async_computation | async-start | bytes 983040 | tf_op jit(solution)/shard_map/all_to_all | solution.py:1182
  78.4 106.5 %all-to-all-start.6 = ((f32[8,1,18]{2,1,0:T(1,128)}), f32[8,1,18]{2,1,0:T(1,128)S(1)}, u32[]{:S(2)}, u32[]{:S(2)}) async-start(f32[8,1,18]{2,1,0:T(1,128)} %copy.178), calls=%async_computation.6 | async-start | bytes 8192 | tf_op jit(solution)/shard_map/all_to_all | solution.py:1182
  122.6 125.0 %collective-permute-start.2 = (bf16[2,768,768]{2,1,0:T(8,128)(2,1)}, bf16[2,768,768]{2,1,0:T(8,128)(2,1)}, u32[]{:S(2)}, u32[]{:S(2)}) collective-permute-start(bf16[2,768,768]{2,1,0:T(8,128)(2,1)} %collective-permute-done.w1_ref), channel_id=1, source_target_pairs={{0,1},{1,0},{2,3},{3,2},{4,5},{5,4},{6,7},{7,6},{8,9},{9,8},{10,11... | collective-permute-start | bytes 7077896 | tf_op jit(solution)/shard_map/ppermute | solution.py:1058
  162.9 84.3 %collective-permute-start.3 = (bf16[2,768,768]{2,1,0:T(8,128)(2,1)}, bf16[2,768,768]{2,1,0:T(8,128)(2,1)}, u32[]{:S(2)}, u32[]{:S(2)}) collective-permute-start(bf16[2,768,768]{2,1,0:T(8,128)(2,1)} %get-tuple-element.152.w0_ref), channel_id=1, source_target_pairs={{0,2},{2,0},{1,3},{3,1},{4,6},{6,4},{5,7},{7,5},{8,10},{10,8},{9,1... | collective-permute-start | bytes 7077896 | tf_op jit(solution)/shard_map/ppermute | solution.py:1058
  184.9 34.7 %all-to-all-start.1 = ((bf16[16,72,128]{2,1,0:T(8,128)(2,1)}), bf16[16,72,128]{2,1,0:T(8,128)(2,1)}, u32[]{:S(2)}, u32[]{:S(2)}) async-start(bf16[16,72,128]{2,1,0:T(8,128)(2,1)} %copy-done.94), calls=%async_computation.1 | async-start | bytes 589824 | tf_op jit(solution)/shard_map/all_to_all | solution.py:848
  241.4 64.8 %collective-permute-start.4 = (bf16[2,768,768]{2,1,0:T(8,128)(2,1)}, bf16[2,768,768]{2,1,0:T(8,128)(2,1)}, u32[]{:S(2)}, u32[]{:S(2)}) collective-permute-start(bf16[2,768,768]{2,1,0:T(8,128)(2,1)} %get-tuple-element.152.w0_ref), channel_id=1, source_target_pairs={{0,1},{1,0},{2,3},{3,2},{4,5},{5,4},{6,7},{7,6},{8,9},{9,8},{10,11... | collective-permute-start | bytes 7077896 | tf_op jit(solution)/shard_map/ppermute | solution.py:1058
  242.9 25.1 %all-to-all-start.5 = ((bf16[8,36,1280]{2,1,0:T(8,128)(2,1)}), bf16[8,36,1280]{2,1,0:T(8,128)(2,1)}, u32[]{:S(2)}, u32[]{:S(2)}) async-start(bf16[8,36,1280]{2,1,0:T(8,128)(2,1)} %copy.173), calls=%async_computation.5 | async-start | bytes 1638400 | tf_op jit(solution)/shard_map/all_to_all | solution.py:1182
  247.2 59.1 %collective-permute-start.5 = (bf16[2,768,768]{2,1,0:T(8,128)(2,1)}, bf16[2,768,768]{2,1,0:T(8,128)(2,1)}, u32[]{:S(2)}, u32[]{:S(2)}) collective-permute-start(bf16[2,768,768]{2,1,0:T(8,128)(2,1)} %collective-permute-done.3.w1_ref), channel_id=1, source_target_pairs={{0,1},{1,0},{2,3},{3,2},{4,5},{5,4},{6,7},{7,6},{8,9},{9,8},{10,11... | collective-permute-start | bytes 7077896 | tf_op jit(solution)/shard_map/ppermute | solution.py:1058
  285.3 21.0 %all-to-all-start.4 = ((bf16[16,72,128]{2,1,0:T(8,128)(2,1)}), bf16[16,72,128]{2,1,0:T(8,128)(2,1)}, u32[]{:S(2)}, u32[]{:S(2)}) async-start(bf16[16,72,128]{2,1,0:T(8,128)(2,1)} %copy-done.95), calls=%async_computation.4 | async-start | bytes 589824 | tf_op jit(solution)/shard_map/all_to_all | solution.py:848
  378.0 12.8 %all-to-all-start.11 = ((bf16[16,72,128]{2,1,0:T(8,128)(2,1)}), bf16[16,72,128]{2,1,0:T(8,128)(2,1)}, u32[]{:S(2)}, u32[]{:S(2)}) async-start(bf16[16,72,128]{2,1,0:T(8,128)(2,1)} %get-tuple-element.159), calls=%async_computation.11 | async-start | bytes 589824 | tf_op jit(solution)/shard_map/all_to_all | solution.py:848
  517.7 39.0 %collective-permute-start.6 = (bf16[1536,768]{1,0:T(8,128)(2,1)}, bf16[1536,768]{1,0:T(8,128)(2,1)}, u32[]{:S(2)}, u32[]{:S(2)}) collective-permute-start(bf16[1536,768]{1,0:T(8,128)(2,1)} %convolution_convert_fusion.9), channel_id=1, source_target_pairs={{0,1},{1,0},{2,3},{3,2},{4,5},{5,4},{6,7},{7,6},{8,9},{9,8},{10,11... | collective-permute-start | bytes 7077896 | tf_op jit(solution)/shard_map/ppermute | solution.py:1058
  520.7 36.1 %collective-permute-start.7 = (bf16[1536,768]{1,0:T(8,128)(2,1)}, bf16[1536,768]{1,0:T(8,128)(2,1)}, u32[]{:S(2)}, u32[]{:S(2)}) collective-permute-start(bf16[1536,768]{1,0:T(8,128)(2,1)} %convolution_convert_fusion.8), channel_id=1, source_target_pairs={{0,1},{1,0},{2,3},{3,2},{4,5},{5,4},{6,7},{7,6},{8,9},{9,8},{10,11... | collective-permute-start | bytes 7077896 | tf_op jit(solution)/shard_map/ppermute | solution.py:1058
  522.0 14.3 %all-to-all-start.16 = ((bf16[16,72,128]{2,1,0:T(8,128)(2,1)}), bf16[16,72,128]{2,1,0:T(8,128)(2,1)S(1)}, u32[]{:S(2)}, u32[]{:S(2)}) async-start(bf16[16,72,128]{2,1,0:T(8,128)(2,1)} %get-tuple-element.186), calls=%async_computation.16 | async-start | bytes 589824 | tf_op jit(solution)/shard_map/all_to_all | solution.py:848
  540.7 13.6 %all-to-all-start.17 = ((bf16[16,72,128]{2,1,0:T(8,128)(2,1)}), bf16[16,72,128]{2,1,0:T(8,128)(2,1)S(1)}, u32[]{:S(2)}, u32[]{:S(2)}) async-start(bf16[16,72,128]{2,1,0:T(8,128)(2,1)} %copy-done.93), calls=%async_computation.17 | async-start | bytes 589824 | tf_op jit(solution)/shard_map/all_to_all | solution.py:848
  566.2 29.5 %collective-permute-start.10 = (bf16[2,1,2,192,768]{4,3,2,1,0:T(8,128)(2,1)}, bf16[2,1,2,192,768]{4,3,2,1,0:T(8,128)(2,1)}, u32[]{:S(2)}, u32[]{:S(2)}) collective-permute-start(bf16[2,1,2,192,768]{4,3,2,1,0:T(8,128)(2,1)} %pad_maximum_fusion.2), channel_id=1, source_target_pairs={{0,2},{2,0},{1,3},{3,1},{4,6},{6,4},{5,7},{7,5},{8,10},{10,8},{9,1... | collective-permute-start | bytes 3538952 | tf_op jit(solution)/shard_map/ppermute | solution.py:1058
  570.0 30.8 %collective-permute-start.8 = (bf16[2,2,1,192,768]{4,3,2,1,0:T(8,128)(2,1)}, bf16[2,2,1,192,768]{4,3,2,1,0:T(8,128)(2,1)}, u32[]{:S(2)}, u32[]{:S(2)}) collective-permute-start(bf16[2,2,1,192,768]{4,3,2,1,0:T(8,128)(2,1)} %fusion.15), channel_id=1, source_target_pairs={{0,4},{4,0},{1,5},{5,1},{2,6},{6,2},{3,7},{7,3},{8,12},{12,8},{9,1... | collective-permute-start | bytes 3538952 | tf_op jit(solution)/shard_map/ppermute | solution.py:1058
  579.1 37.6 %all-to-all-start.18 = ((bf16[16,72,128]{2,1,0:T(8,128)(2,1)}), bf16[16,72,128]{2,1,0:T(8,128)(2,1)S(1)}, u32[]{:S(2)}, u32[]{:S(2)}) async-start(bf16[16,72,128]{2,1,0:T(8,128)(2,1)} %get-tuple-element.200), calls=%async_computation.18 | async-start | bytes 589824 | tf_op jit(solution)/shard_map/all_to_all | solution.py:848
  597.6 15.9 %collective-permute-start.11 = (bf16[2,1,1,192,768]{4,3,2,1,0:T(8,128)(2,1)S(1)}, bf16[2,1,1,192,768]{4,3,2,1,0:T(8,128)(2,1)S(1)}, u32[]{:S(2)}, u32[]{:S(2)}) collective-permute-start(bf16[2,1,1,192,768]{4,3,2,1,0:T(8,128)(2,1)S(1)} %slice.598), channel_id=1, source_target_pairs={{0,4},{4,0},{1,5},{5,1},{2,6},{6,2},{3,7},{7,3},{8,12},{12,8},{9,1... | collective-permute-start | bytes 1769480 | tf_op jit(solution)/shard_map/ppermute | solution.py:1058
  602.4 13.0 %collective-permute-start.9 = (bf16[2,1,1,192,768]{4,3,2,1,0:T(8,128)(2,1)S(1)}, bf16[2,1,1,192,768]{4,3,2,1,0:T(8,128)(2,1)S(1)}, u32[]{:S(2)}, u32[]{:S(2)}) collective-permute-start(bf16[2,1,1,192,768]{4,3,2,1,0:T(8,128)(2,1)S(1)} %slice.594), channel_id=1, source_target_pairs={{0,2},{2,0},{1,3},{3,1},{4,6},{6,4},{5,7},{7,5},{8,10},{10,8},{9,1... | collective-permute-start | bytes 1769480 | tf_op jit(solution)/shard_map/ppermute | solution.py:1058
  619.0 13.3 %collective-permute-start.12 = (bf16[384,768]{1,0:T(8,128)(2,1)}, bf16[384,768]{1,0:T(8,128)(2,1)}, u32[]{:S(2)}, u32[]{:S(2)}) collective-permute-start(bf16[384,768]{1,0:T(8,128)(2,1)} %get-tuple-element.274), channel_id=1, source_target_pairs={{0,8},{1,9},{2,10},{3,11},{4,12},{5,13},{6,14},{7,15}} | collective-permute-start | bytes 1769480 | tf_op jit(solution)/shard_map/ppermute | solution.py:1106
  634.6 17.4 %collective-permute-start.13 = (bf16[384,768]{1,0:T(8,128)(2,1)}, bf16[384,768]{1,0:T(8,128)(2,1)}, u32[]{:S(2)}, u32[]{:S(2)}) collective-permute-start(bf16[384,768]{1,0:T(8,128)(2,1)} %fusion.23), channel_id=1, source_target_pairs={{0,8},{8,16},{1,9},{9,17},{2,10},{10,18},{3,11},{11,19},{4,12},{12... | collective-permute-start | bytes 1769480 | tf_op jit(solution)/shard_map/ppermute | solution.py:1106
  646.6 13.2 %all-to-all-start.19 = ((bf16[16,72,128]{2,1,0:T(8,128)(2,1)}), bf16[16,72,128]{2,1,0:T(8,128)(2,1)S(1)}, u32[]{:S(2)}, u32[]{:S(2)}) async-start(bf16[16,72,128]{2,1,0:T(8,128)(2,1)} %get-tuple-element.204), calls=%async_computation.19 | async-start | bytes 589824 | tf_op jit(solution)/shard_map/all_to_all | solution.py:848
  682.1 23.6 %collective-permute-start.16 = (bf16[4,2,2,212,8,128]{5,4,3,2,1,0:T(8,128)(2,1)S(1)}, bf16[4,2,2,212,8,128]{5,4,3,2,1,0:T(8,128)(2,1)S(1)}, u32[]{:S(2)}, u32[]{:S(2)}) collective-permute-start(bf16[4,2,2,212,8,128]{5,4,3,2,1,0:T(8,128)(2,1)S(1)} %get-tuple-element.235), channel_id=1, source_target_pairs={{0,1},{1,0},{2,3},{3,2},{4,5},{5,4},{6,7},{7,6},{8,9},{9,8},{10,11... | collective-permute-start | bytes 20840456 | tf_op jit(solution)/shard_map/ppermute | solution.py:1058
  703.8 29.0 %collective-permute-start.31 = (bf16[2,1,2,192,768]{4,3,2,1,0:T(8,128)(2,1)}, bf16[2,1,2,192,768]{4,3,2,1,0:T(8,128)(2,1)S(1)}, u32[]{:S(2)}, u32[]{:S(2)}) collective-permute-start(bf16[2,1,2,192,768]{4,3,2,1,0:T(8,128)(2,1)} %pad_maximum_fusion.1), channel_id=1, source_target_pairs={{0,2},{2,0},{1,3},{3,1},{4,6},{6,4},{5,7},{7,5},{8,10},{10,8},{9,1... | collective-permute-start | bytes 3538952 | tf_op jit(solution)/shard_map/ppermute | solution.py:1058
  721.2 68.2 %collective-permute-start.17 = (bf16[4,1,2,106,8,128]{5,4,3,2,1,0:T(8,128)(2,1)}, bf16[4,1,2,106,8,128]{5,4,3,2,1,0:T(8,128)(2,1)}, u32[]{:S(2)}, u32[]{:S(2)}) collective-permute-start(bf16[4,1,2,106,8,128]{5,4,3,2,1,0:T(8,128)(2,1)} %slice.618), channel_id=1, source_target_pairs={{0,4},{4,0},{1,5},{5,1},{2,6},{6,2},{3,7},{7,3},{8,12},{12,8},{9,1... | collective-permute-start | bytes 5210120 | tf_op jit(solution)/shard_map/ppermute | solution.py:1058
  723.8 63.8 %collective-permute-start.29 = (bf16[2,2,1,192,768]{4,3,2,1,0:T(8,128)(2,1)}, bf16[2,2,1,192,768]{4,3,2,1,0:T(8,128)(2,1)}, u32[]{:S(2)}, u32[]{:S(2)}) collective-permute-start(bf16[2,2,1,192,768]{4,3,2,1,0:T(8,128)(2,1)} %fusion.12), channel_id=1, source_target_pairs={{0,4},{4,0},{1,5},{5,1},{2,6},{6,2},{3,7},{7,3},{8,12},{12,8},{9,1... | collective-permute-start | bytes 3538952 | tf_op jit(solution)/shard_map/ppermute | solution.py:1058
  727.1 66.3 %collective-permute-start.19 = (bf16[4,2,1,106,8,128]{5,4,3,2,1,0:T(8,128)(2,1)}, bf16[4,2,1,106,8,128]{5,4,3,2,1,0:T(8,128)(2,1)}, u32[]{:S(2)}, u32[]{:S(2)}) collective-permute-start(bf16[4,2,1,106,8,128]{5,4,3,2,1,0:T(8,128)(2,1)} %slice.622), channel_id=1, source_target_pairs={{0,2},{2,0},{1,3},{3,1},{4,6},{6,4},{5,7},{7,5},{8,10},{10,8},{9,1... | collective-permute-start | bytes 5210120 | tf_op jit(solution)/shard_map/ppermute | solution.py:1058
  734.3 65.8 %collective-permute-start.32 = (bf16[2,1,1,192,768]{4,3,2,1,0:T(8,128)(2,1)S(1)}, bf16[2,1,1,192,768]{4,3,2,1,0:T(8,128)(2,1)S(1)}, u32[]{:S(2)}, u32[]{:S(2)}) collective-permute-start(bf16[2,1,1,192,768]{4,3,2,1,0:T(8,128)(2,1)S(1)} %slice.640), channel_id=1, source_target_pairs={{0,4},{4,0},{1,5},{5,1},{2,6},{6,2},{3,7},{7,3},{8,12},{12,8},{9,1... | collective-permute-start | bytes 1769480 | tf_op jit(solution)/shard_map/ppermute | solution.py:1058
  789.2 16.3 %collective-permute-start.30 = (bf16[2,1,1,192,768]{4,3,2,1,0:T(8,128)(2,1)S(1)}, bf16[2,1,1,192,768]{4,3,2,1,0:T(8,128)(2,1)S(1)}, u32[]{:S(2)}, u32[]{:S(2)}) collective-permute-start(bf16[2,1,1,192,768]{4,3,2,1,0:T(8,128)(2,1)S(1)} %slice.636), channel_id=1, source_target_pairs={{0,2},{2,0},{1,3},{3,1},{4,6},{6,4},{5,7},{7,5},{8,10},{10,8},{9,1... | collective-permute-start | bytes 1769480 | tf_op jit(solution)/shard_map/ppermute | solution.py:1058
  791.4 29.6 %collective-permute-start.18 = (bf16[4,1,1,106,8,128]{5,4,3,2,1,0:T(8,128)(2,1)S(1)}, bf16[4,1,1,106,8,128]{5,4,3,2,1,0:T(8,128)(2,1)S(1)}, u32[]{:S(2)}, u32[]{:S(2)}) collective-permute-start(bf16[4,1,1,106,8,128]{5,4,3,2,1,0:T(8,128)(2,1)S(1)} %slice.620), channel_id=1, source_target_pairs={{0,2},{2,0},{1,3},{3,1},{4,6},{6,4},{5,7},{7,5},{8,10},{10,8},{9,1... | collective-permute-start | bytes 2605064 | tf_op jit(solution)/shard_map/ppermute | solution.py:1058
  795.4 25.8 %collective-permute-start.20 = (bf16[4,1,1,106,8,128]{5,4,3,2,1,0:T(8,128)(2,1)S(1)}, bf16[4,1,1,106,8,128]{5,4,3,2,1,0:T(8,128)(2,1)S(1)}, u32[]{:S(2)}, u32[]{:S(2)}) collective-permute-start(bf16[4,1,1,106,8,128]{5,4,3,2,1,0:T(8,128)(2,1)S(1)} %slice.624), channel_id=1, source_target_pairs={{0,4},{4,0},{1,5},{5,1},{2,6},{6,2},{3,7},{7,3},{8,12},{12,8},{9,1... | collective-permute-start | bytes 2605064 | tf_op jit(solution)/shard_map/ppermute | solution.py:1058
  806.6 33.0 %collective-permute-start.34 = (bf16[384,768]{1,0:T(8,128)(2,1)S(1)}, bf16[384,768]{1,0:T(8,128)(2,1)S(1)}, u32[]{:S(2)}, u32[]{:S(2)}) collective-permute-start(bf16[384,768]{1,0:T(8,128)(2,1)S(1)} %get-tuple-element.273), channel_id=1, source_target_pairs={{24,16},{25,17},{26,18},{27,19},{28,20},{29,21},{30,22},{31,23}} | collective-permute-start | bytes 1769480 | tf_op jit(solution)/shard_map/ppermute | solution.py:1106
  822.5 25.5 %collective-permute-start.21 = (bf16[212,8,128]{2,1,0:T(8,128)(2,1)}, bf16[212,8,128]{2,1,0:T(8,128)(2,1)}, u32[]{:S(2)}, u32[]{:S(2)}) collective-permute-start(bf16[212,8,128]{2,1,0:T(8,128)(2,1)} %get-tuple-element.266), channel_id=1, source_target_pairs={{0,8},{1,9},{2,10},{3,11},{4,12},{5,13},{6,14},{7,15}} | collective-permute-start | bytes 1302536 | tf_op jit(solution)/shard_map/ppermute | solution.py:1106
  839.8 17.1 %collective-permute-start.35 = (bf16[384,768]{1,0:T(8,128)(2,1)S(1)}, bf16[384,768]{1,0:T(8,128)(2,1)}, u32[]{:S(2)}, u32[]{:S(2)}) collective-permute-start(bf16[384,768]{1,0:T(8,128)(2,1)S(1)} %fusion.19), channel_id=1, source_target_pairs={{24,16},{16,8},{25,17},{17,9},{26,18},{18,10},{27,19},{19,11},{28,... | collective-permute-start | bytes 1769480 | tf_op jit(solution)/shard_map/ppermute | solution.py:1106
  841.3 36.9 %collective-permute-start.33 = (bf16[384,768]{1,0:T(8,128)(2,1)}, bf16[384,768]{1,0:T(8,128)(2,1)}, u32[]{:S(2)}, u32[]{:S(2)}) collective-permute-start(bf16[384,768]{1,0:T(8,128)(2,1)} %get-tuple-element.272), channel_id=1, source_target_pairs={{0,8},{1,9},{2,10},{3,11},{4,12},{5,13},{6,14},{7,15}} | collective-permute-start | bytes 1769480 | tf_op jit(solution)/shard_map/ppermute | solution.py:1106
  850.3 15.7 %collective-permute-start.22 = (bf16[212,8,128]{2,1,0:T(8,128)(2,1)}, bf16[212,8,128]{2,1,0:T(8,128)(2,1)}, u32[]{:S(2)}, u32[]{:S(2)}) collective-permute-start(bf16[212,8,128]{2,1,0:T(8,128)(2,1)} %get-tuple-element.264), channel_id=1, source_target_pairs={{0,8},{8,16},{1,9},{9,17},{2,10},{10,18},{3,11},{11,19},{4,12},{12... | collective-permute-start | bytes 1302536 | tf_op jit(solution)/shard_map/ppermute | solution.py:1106
  858.1 20.1 %collective-permute-start.36 = (bf16[384,768]{1,0:T(8,128)(2,1)S(1)}, bf16[384,768]{1,0:T(8,128)(2,1)}, u32[]{:S(2)}, u32[]{:S(2)}) collective-permute-start(bf16[384,768]{1,0:T(8,128)(2,1)S(1)} %fusion.20), channel_id=1, source_target_pairs={{16,8},{8,0},{17,9},{9,1},{18,10},{10,2},{19,11},{11,3},{20,12},{1... | collective-permute-start | bytes 1769480 | tf_op jit(solution)/shard_map/ppermute | solution.py:1106
  867.4 15.1 %collective-permute-start.23 = (bf16[212,8,128]{2,1,0:T(8,128)(2,1)S(1)}, bf16[212,8,128]{2,1,0:T(8,128)(2,1)S(1)}, u32[]{:S(2)}, u32[]{:S(2)}) collective-permute-start(bf16[212,8,128]{2,1,0:T(8,128)(2,1)S(1)} %get-tuple-element.262), channel_id=1, source_target_pairs={{0,8},{8,16},{16,24},{1,9},{9,17},{17,25},{2,10},{10,18},{18,26},{... | collective-permute-start | bytes 1302536 | tf_op jit(solution)/shard_map/ppermute | solution.py:1106
  906.9 167.2 %all-gather.4.cloned.1.call-start = ((), (), s32[]{:S(2)}) async-start(), calls=%async_computation.21 | async-start | bytes 5308416 | tf_op jit(solution)/shard_map/all_gather | solution.py:1416
  967.0 15.9 %collective-permute-start.43 = (bf16[392,768]{1,0:T(8,128)(2,1)S(1)}, bf16[392,768]{1,0:T(8,128)(2,1)S(1)}, u32[]{:S(2)}, u32[]{:S(2)}) collective-permute-start(bf16[392,768]{1,0:T(8,128)(2,1)S(1)} %pad_maximum_fusion.4), channel_id=1, source_target_pairs={{0,8},{8,16},{16,24},{1,9},{9,17},{17,25},{2,10},{10,18},{18,26},{... | collective-permute-start | bytes 1806344 | tf_op jit(solution)/shard_map/ppermute | solution.py:1138
  969.5 17.6 %collective-permute-start.46 = (bf16[392,768]{1,0:T(8,128)(2,1)S(1)}, bf16[392,768]{1,0:T(8,128)(2,1)S(1)}, u32[]{:S(2)}, u32[]{:S(2)}) collective-permute-start(bf16[392,768]{1,0:T(8,128)(2,1)S(1)} %pad_maximum_fusion.4), channel_id=1, source_target_pairs={{8,0},{16,8},{24,16},{9,1},{17,9},{25,17},{10,2},{18,10},{26,18},{... | collective-permute-start | bytes 1806344 | tf_op jit(solution)/shard_map/ppermute | solution.py:1142
  987.1 31.4 %collective-permute-start.47 = (bf16[392,768]{1,0:T(8,128)(2,1)S(1)}, bf16[392,768]{1,0:T(8,128)(2,1)S(1)}, u32[]{:S(2)}, u32[]{:S(2)}) collective-permute-start(bf16[392,768]{1,0:T(8,128)(2,1)S(1)} %collective-permute-done.46), channel_id=1, source_target_pairs={{8,0},{16,8},{9,1},{17,9},{10,2},{18,10},{11,3},{19,11},{12,4},{20... | collective-permute-start | bytes 1806344 | tf_op jit(solution)/shard_map/ppermute | solution.py:1142
  988.4 31.3 %collective-permute-start.45 = (bf16[392,768]{1,0:T(8,128)(2,1)S(1)}, bf16[392,768]{1,0:T(8,128)(2,1)}, u32[]{:S(2)}, u32[]{:S(2)}) collective-permute-start(bf16[392,768]{1,0:T(8,128)(2,1)S(1)} %collective-permute-done.44), channel_id=1, source_target_pairs={{16,24},{17,25},{18,26},{19,27},{20,28},{21,29},{22,30},{23,31}} | collective-permute-start | bytes 1806344 | tf_op jit(solution)/shard_map/ppermute | solution.py:1138
  1018.4 38.0 %collective-permute-start.48 = (bf16[392,768]{1,0:T(8,128)(2,1)S(1)}, bf16[392,768]{1,0:T(8,128)(2,1)S(1)}, u32[]{:S(2)}, u32[]{:S(2)}) collective-permute-start(bf16[392,768]{1,0:T(8,128)(2,1)S(1)} %collective-permute-done.47), channel_id=1, source_target_pairs={{8,0},{9,1},{10,2},{11,3},{12,4},{13,5},{14,6},{15,7}} | collective-permute-start | bytes 1806344 | tf_op jit(solution)/shard_map/ppermute | solution.py:1142
  1059.8 33.2 %collective-permute-start.49 = (bf16[4,384,768]{2,1,0:T(8,128)(2,1)}, bf16[4,384,768]{2,1,0:T(8,128)(2,1)S(1)}, u32[]{:S(2)}, u32[]{:S(2)}) collective-permute-start(bf16[4,384,768]{2,1,0:T(8,128)(2,1)} %constant_dynamic-slice_fusion.3), channel_id=1, source_target_pairs={{0,1},{1,0},{2,3},{3,2},{4,5},{5,4},{6,7},{7,6},{8,9},{9,8},{10,11... | collective-permute-start | bytes 7077896 | tf_op jit(solution)/shard_map/ppermute | solution.py:1058
  (227 other events, 2412.2 us)
Sparse Core Ops, SparseCore 0:
  32.3 120.0 all-gather.5
  983.7 90.3 all-gather.3

commit v2 on v1

--- a/solution.py
+++ b/solution.py
@@ -626,18 +626,16 @@
 
 
 def thirds(w_ref, size):
-    return [w_ref.at[pl.ds(i * size, size)] for i in range(3)]
+    return [w_ref[i * size : (i + 1) * size] for i in range(3)]
 
 
 def embed_kernel(src_ref, shift_ref, bias_ref, norm_ref, spread_ref, row_ref, w_ref,
-                 state_ref, send_ref, held_ref, sems):
-    copies = fetch(thirds(w_ref, PIX), held_ref, sems)
+                 state_ref, send_ref):
     src = src_ref[...]
     state = bias_ref[...]
-    for offset in range(3):
+    for offset, weight in enumerate(thirds(w_ref, PIX)):
         moved = src if offset == 1 else dot(shift_ref[offset], src).astype(NARROW)
-        copies[offset].wait()
-        state = state + dot(moved, held_ref[offset])
+        state = state + dot(moved, weight)
     state_ref[...] = state
     scaled, _unused = normalize(state)
     normed = scaled * norm_ref[0:1] + norm_ref[1:2]
@@ -735,43 +733,37 @@
 
 
 def head_kernel(state_ref, shift_ref, bias_ref, target_ref, weight_ref, w_ref,
-                low_ref, pred_ref, grad_ref, loss_ref, held_ref, sems):
-    copies = fetch(thirds(w_ref, D), held_ref, sems)
+                low_ref, pred_ref, grad_ref, loss_ref):
     low = state_ref[...].astype(NARROW)
     low_ref[...] = low
     predicted = bias_ref[...]
-    for offset in range(3):
+    for offset, weight in enumerate(thirds(w_ref, D)):
         moved = low if offset == 1 else dot(shift_ref[offset], low).astype(NARROW)
-        copies[offset].wait()
-        predicted = predicted + dot(moved, held_ref[offset])
+        predicted = predicted + dot(moved, weight)
     pred_ref[...] = predicted.astype(NARROW)
     differ = predicted - target_ref[...].astype(jnp.float32)
     loss_ref[...] = column_sum(weight_ref[:, 0:1] * differ * differ)
     grad_ref[...] = weight_ref[:, 1:2] * differ
 
 
-def head_back_kernel(grad_ref, shift_ref, w_ref, low_ref, sum_ref, out_ref, held_ref, sems):
-    copies = fetch(thirds(w_ref, D), held_ref, sems)
+def head_back_kernel(grad_ref, shift_ref, w_ref, low_ref, sum_ref, out_ref):
     low = grad_ref[...].astype(NARROW)
     low_ref[...] = low
     sum_ref[...] = column_sum(low.astype(jnp.float32))
     total = None
-    for offset in range(3):
+    for offset, weight in enumerate(thirds(w_ref, D)):
         moved = low if offset == 1 else dot(shift_ref[2 - offset], low).astype(NARROW)
-        copies[offset].wait()
-        part = dot_nt(moved, held_ref[offset])
+        part = dot_nt(moved, weight)
         total = part if total is None else total + part
     out_ref[...] = total
 
 
-def embed_back_kernel(low_ref, shift_ref, add_ref, w_ref, out_ref, held_ref, sems):
-    copies = fetch(thirds(w_ref, PIX), held_ref, sems)
+def embed_back_kernel(low_ref, shift_ref, add_ref, w_ref, out_ref):
     low = low_ref[...]
     total = add_ref[...]
-    for offset in range(3):
+    for offset, weight in enumerate(thirds(w_ref, PIX)):
         moved = low if offset == 1 else dot(shift_ref[2 - offset], low).astype(NARROW)
-        copies[offset].wait()
-        total = total + dot_nt(moved, held_ref[offset])
+        total = total + dot_nt(moved, weight)
     out_ref[...] = total
 
 
@@ -817,6 +809,29 @@
     sums_ref[2:3] = column_sum(low.astype(jnp.float32))
 
 
+def narrow_kernel(place_ref, in_ref, out_ref):
+    out_ref[...] = in_ref[...].astype(NARROW)
+
+
+def own_quarters(weights, place):
+    size = weights.shape[1] // 4
+
+    def from_spot(m, q, place_ref):
+        return (m, (q // 2 + place_ref[0]) % 2 * 2 + (q % 2 + place_ref[1]) % 2, 0)
+
+    return pl.pallas_call(
+        narrow_kernel,
+        name="narrow",
+        out_shape=jax.ShapeDtypeStruct(weights.shape, NARROW),
+        grid_spec=pltpu.PrefetchScalarGridSpec(
+            num_scalar_prefetch=1,
+            grid=(weights.shape[0], 4),
+            in_specs=[pl.BlockSpec((None, size, D), from_spot)],
+            out_specs=pl.BlockSpec((None, size, D), lambda m, q, place_ref: (m, q, 0)),
+        ),
+    )(place, weights)
+
+
 def muon_kernel(level_ref, momentum_ref, weight_ref, change_ref, out_ref):
     momentum = momentum_ref[...]
     ortho = POLY_COEF[0] * POLY_COEF[0] * level_ref[pl.program_id(0)] * momentum
@@ -824,8 +839,8 @@
     out_ref[...] = weight_ref[...] * (1.0 - MUON_RATE * DECAY_RATE) - MUON_RATE * (FF / D) ** 0.5 * ortho
 
 
-def launch(kernel, name, out_dims, operands, far=(), far_out=False, near=(), scratch=(), limit=28):
-    anywhere = pl.BlockSpec(memory_space=pl.ANY)
+def launch(kernel, name, out_dims, operands, far=(), far_out=False, near=(), scratch=(), limit=16):
+    anywhere = pl.BlockSpec(memory_space=pltpu.HBM)
     local = pl.BlockSpec(memory_space=pltpu.VMEM)
     in_specs = []
     for i in range(len(operands)):
@@ -887,19 +902,20 @@
     return found
 
 
-def form_tables(width, total, count):
-    starts = {kind: np.zeros(count, np.int32) for kind in KINDS}
-    lows = {kind: np.zeros(count, np.int32) for kind in KINDS}
-    highs = {kind: np.zeros(count, np.int32) for kind in KINDS}
+def form_range(kind, device, width, total, count):
+    row, tiles = KINDS[kind]
+    base, edge = kind_ranges(total)[kind]
+    origin = device * width
+    low = jnp.clip(base - origin, 0, width)
+    high = jnp.clip(edge - origin, 0, width)
+    inside = jnp.maximum(origin - base, 0)
+    start = inside % (8 * row) - low
+    first = EMBED_AT if kind == "embed" else 0
     for index in range(count):
-        for kind, first, last, tile, begin, end in window_pieces(index, width, total):
-            row, tiles = KINDS[kind]
-            base = EMBED_AT if kind == "embed" else 0
-            own = begin - kind_ranges(total)[kind][0] - first * 8 * row
-            lows[kind][index] = begin - index * width
-            highs[kind][index] = end - index * width
-            starts[kind][index] = (tile - base) * 8 * LANES + own - lows[kind][index]
-    return starts, lows, highs
+        for piece in window_pieces(index, width, total):
+            if piece[0] == kind and piece[3] != first:
+                start = start + jnp.where(device == index, (piece[3] - first) * 8 * LANES, 0)
+    return start, low, high
 
 
 def form_tiles(kind):
@@ -909,11 +925,10 @@
 
 
 def own_window(own, device, width, total, count):
-    starts, lows, highs = form_tables(width, total, count)
     spot = jnp.arange(width, dtype=jnp.int32)
     window = jnp.zeros((WINDOW, 8, LANES), jnp.float32)
     for kind, (row, tiles) in KINDS.items():
-        start, low, high = (jnp.asarray(t[kind])[device] for t in (starts, lows, highs))
+        start, low, high = form_range(kind, device, width, total, count)
         first, groups = form_tiles(kind)
         length = groups * tiles * 8 * LANES
         held = jnp.where((spot >= low) & (spot < high), own, 0.0)
@@ -921,15 +936,14 @@
         form = lax.dynamic_slice(held, (length - start,), (length,))
         form = form.reshape(groups, 8, tiles, LANES).transpose(0, 2, 1, 3).reshape(-1, 8, LANES)
         window = window + jnp.pad(form, ((first, WINDOW - first - groups * tiles), (0, 0), (0, 0)))
-    return window.astype(NARROW)
+    return window
 
 
 def own_range(window, device, width, total, count):
-    starts, lows, highs = form_tables(width, total, count)
     spot = jnp.arange(width, dtype=jnp.int32)
     result = jnp.zeros((width,), jnp.float32)
     for kind, (row, tiles) in KINDS.items():
-        start, low, high = (jnp.asarray(t[kind])[device] for t in (starts, lows, highs))
+        start, low, high = form_range(kind, device, width, total, count)
         first, groups = form_tiles(kind)
         form = window[first : first + groups * tiles].reshape(groups, tiles, 8, LANES)
         form = jnp.pad(form.transpose(0, 2, 1, 3).reshape(-1), (width, width))
@@ -999,8 +1013,9 @@
     sem = pltpu.SemaphoreType.DMA
     (out,) = launch(
         functools.partial(join_kernel, tiles, single, double), "join_" + kind,
-        [((groups * tiles, 8, LANES), NARROW)], [got], far=(0,), far_out=True,
+        [((groups * tiles, 8, LANES), NARROW)], [got], far=(0,),
         scratch=(held, held, sem((max(len(single), 1),)), sem((max(len(double), 1),)), sem((max(len(double), 1),))),
+        limit=50,
     )
     return out.reshape(groups, tiles, 8, LANES).transpose(0, 2, 1, 3).reshape(groups * 8, row)
 
@@ -1058,23 +1073,40 @@
     return lax.ppermute(values, axis, [(0, 1), (1, 0)])
 
 
-def add_low(left, right):
-    return (left.astype(jnp.float32) + right.astype(jnp.float32)).astype(NARROW)
-
-
-def chip_sum(kept, x_dim, y_dim, cut_dim):
-    half = kept.shape[cut_dim] // 2
-
-    def side(values, dim, which):
-        return lax.index_in_dim(values, which, dim, keepdims=True)
-
-    parts = []
-    for start, order in ((0, ((x_dim, "x"), (y_dim, "y"))), (half, ((y_dim, "y"), (x_dim, "x")))):
-        value = lax.slice_in_dim(kept, start, start + half, axis=cut_dim)
-        for dim, axis in order:
-            value = add_low(side(value, dim, 0), swap(side(value, dim, 1), axis))
-        parts.append(value)
-    return jnp.concatenate(parts, axis=cut_dim)
+def add_low(*values):
+    return sum(v.astype(jnp.float32) for v in values).astype(NARROW)
+
+
+def side(values, dim, which):
+    return lax.index_in_dim(values, which, dim, keepdims=True)
+
+
+def chip_halves(kept, x_dim, y_dim, cut_dim):
+    half = kept[0].shape[cut_dim] // 2
+    ways = ((x_dim, "x"), (y_dim, "y"))
+    return [
+        ([lax.slice_in_dim(v, start, start + half, axis=cut_dim) for v in kept], order)
+        for start, order in ((0, ways), (half, ways[::-1]))
+    ]
+
+
+def chip_stage(halves, stage):
+    result = []
+    for values, order in halves:
+        dim, axis = order[stage]
+        got = swap(add_low(*(side(v, dim, 1) for v in values)), axis)
+        result.append(([add_low(got, *(side(v, dim, 0) for v in values))], order))
+    return result
+
+
+def chip_join(halves, cut_dim):
+    return jnp.concatenate([values[0] for values, order in halves], axis=cut_dim)
+
+
+def held_back(halves, *others):
+    flat = [values[0] for values, order in halves]
+    flat, others = lax.optimization_barrier((flat, others))
+    return [([v], order) for v, (unused, order) in zip(flat, halves)], *others
 
 
 def line_sum(parts, owners):
@@ -1148,7 +1180,7 @@
 def unpack_rest(rest):
     found = []
     offset = 0
-    for dims in ((L, 2, 2, NB, BS, BS), (D,), (PIX,), (L, 2, 2, D), (L, 4, D), (L, FF + D)):
+    for dims in ((D,), (PIX,), (L, 2, 2, D), (L, 4, D), (L, FF + D)):
         amount = math.prod(dims)
         found.append(rest[offset : offset + amount].reshape(dims))
         offset += amount
@@ -1183,16 +1215,19 @@
         got = got.reshape((items * 4, lead, rows * OWN) + rest)
         return jnp.moveaxis(got, 1, 0).reshape((lead, TOK) + rest)
 
-    windows = lax.all_gather(own_window(adam_params, device, width, total, devices), SUB_AXES)
-    turned_w = jnp.roll(mlp_weights, mlp_weights.shape[2] // 2, axis=2)
-    mlp_own = jnp.where(x == 0, mlp_weights, turned_w).astype(NARROW)
+    own = own_window(adam_params, device, width, total, devices).astype(NARROW)
+    windows = lax.all_gather(own, SUB_AXES)
+    own_mask = own_window(jnp.ones((width,), jnp.float32), device, width, total, devices)
+    zl = lax.axis_index("zl")
     mlp_low = []
     for depth in range(L):
-        own = mlp_own[depth]
-        if depth:
-            own, windows = lax.optimization_barrier((own, windows))
-        across_y = swap(own, "y")
-        mlp_low.append((own, across_y, swap(own, "c"), swap(across_y, "c")))
+        own = own_quarters(mlp_weights[depth], jnp.stack([x, zl])).reshape(2, 4, D // 4, D)
+        first = swap(own[:, 0], "y")
+        second = swap(first, "x")
+        others = swap(jnp.stack([first, second]), "zl")
+        across_y = jnp.stack([first, others[0], second, others[1]], axis=1)
+        four = (own, across_y, swap(own, "c"), swap(across_y, "c"))
+        mlp_low.append([chunk.reshape(2, D, D) for chunk in four])
     source = to_items(pixels[None])[0]
     wanted = to_items(targets)
     row_weight = jnp.sin(math.pi * (lat_rows.astype(jnp.float32) + 0.5) / ROWS)
@@ -1204,18 +1239,21 @@
 
     embed_w = join_windows(windows, "embed", width, total, devices)
     head_w = join_windows(windows, "head", width, total, devices)
-    rest = join_windows(windows, "rest", width, total, devices).reshape(-1)
-    spec_w, embed_b, head_b, spec_b, norm_params, mlp_b = unpack_rest(rest)
+    rest = join_windows(windows, "rest", width, total, devices)
+    spec_rows = L * 4 * NB * BS * BS // LANES
+    spec_w = rest[:spec_rows].reshape(L, 2, 2, NB, BS, BS)
+    embed_b, head_b, spec_b, norm_params, mlp_b = unpack_rest(rest[spec_rows:].reshape(-1))
     embed_b, head_b = embed_b.astype(jnp.float32)[None], head_b.astype(jnp.float32)[None]
     norms = norm_params.astype(jnp.float32)
     mlp_b = mlp_b.astype(jnp.float32)
 
     def by_place(values):
-        values = jnp.where(y == 0, values, values[:, ::-1])
-        values = jnp.where(c == 0, values, values[:, :, ::-1])
-        return jnp.where(x == 0, values, values[:, :, :, ::-1])
-
-    up_b = by_place(mlp_b[:, :FF].reshape(L, 2, 2, 2, -1)).transpose(0, 2, 1, 3, 4).reshape(L, 1, FF)
+        for dim, side in ((1, y), (2, c), (3, x), (4, zl)):
+            values = jnp.where(side == 0, values, jnp.flip(values, dim))
+        return values
+
+    up_b = by_place(mlp_b[:, :FF].reshape(L, 2, 2, 2, 2, -1)).transpose(0, 2, 1, 3, 4, 5)
+    up_b = up_b.reshape(L, 1, FF)
     down_b = mlp_b[:, None, FF:]
     gap = LANES - BS
     own_w = lax.dynamic_index_in_dim(spec_w, block, 3, keepdims=False)
@@ -1233,8 +1271,6 @@
     wide = pltpu.VMEM((GROUP, HALF_TOK + 8, LANES), f32)
     sem = pltpu.SemaphoreType.DMA
     held_mlp = (pltpu.VMEM((4, 2, D, D), NARROW), sem((4,)))
-    held_embed = (pltpu.VMEM((3, PIX, D), NARROW), sem((3,)))
-    held_head = (pltpu.VMEM((3, D, PIX), NARROW), sem((3,)))
 
     current = source
     saved = []
@@ -1242,8 +1278,7 @@
     for roll_idx in range(STEPS):
         state, sent = launch(
             embed_kernel, "embed", [state_f32, payload],
-            [current, shifts, embed_b, norms[0], spread, row_fwd, embed_w], far=(6,),
-            scratch=held_embed,
+            [current, shifts, embed_b, norms[0], spread, row_fwd, embed_w],
         )
         layers = []
         for depth in range(L):
@@ -1258,7 +1293,7 @@
             results = launch(
                 functools.partial(mlp_kernel, has_next), "mlp", outs + [payload] * has_next,
                 [got, state, norms[depth], norms[min(depth + 1, L - 1)], up_b[depth], down_b[depth],
-                 spread, row_fwd, row_back, *mlp_low[depth]], far=(9, 10, 11, 12), scratch=held_mlp,
+                 spread, row_fwd, row_back, *mlp_low[depth]], far=(9, 10, 11, 12), scratch=held_mlp, limit=26,
             )
             layers.append((state, mixed_in) + tuple(results[:4]))
             state = results[4]
@@ -1267,8 +1302,7 @@
         low, predicted, loss_grad, loss_part = launch(
             head_kernel, "head",
             [((TOK, D), NARROW), ((TOK, PIX), NARROW), ((TOK, PIX), f32), ((1, PIX), f32)],
-            [state, shifts, head_b, wanted[roll_idx], weight_pair, head_w], far=(5,),
-            scratch=held_head,
+            [state, shifts, head_b, wanted[roll_idx], weight_pair, head_w],
         )
         loss_sums.append(loss_part)
         saved.append((current, layers, low, loss_grad))
@@ -1285,16 +1319,17 @@
         pairs = ((g_before, hidden_in), (hidden, grad_out))
         return pairs, [swap(dot_tn(a[:, half_ff:], b).astype(NARROW), "c") for a, b in pairs]
 
-    def mlp_chip(pairs, got):
+    def mlp_kept(pairs, got):
         kept = [
             (dot_tn(a[:, :half_ff], b) + sent.astype(f32)).astype(NARROW)
             for (a, b), sent in zip(pairs, got)
         ]
-        kept = jnp.stack(kept).reshape(2, 2, 2, rows_own, D)
-        return chip_sum(kept, 2, 1, 3).reshape(2, rows_own, D)
-
-    def mlp_line(depth, kept):
-        return line_sum(kept, [2 * depth, 2 * depth + 1])
+        return jnp.stack(kept).reshape(2, 2, 2, rows_own, D)
+
+    def mlp_joined(halves):
+        halves = chip_join(halves, 3).reshape(2, 2, rows_own // 2, D)
+        halves = jnp.where(zl == 0, halves, jnp.flip(halves, 1))
+        return halves.reshape(2, rows_own, D)
 
     head_terms, embed_terms = [], []
     mlp_terms = [[] for unused in range(L)]
@@ -1308,7 +1343,6 @@
         upstream_low, head_sum, grad_state = launch(
             head_back_kernel, "head_back",
             [((TOK, PIX), NARROW), ((1, PIX), f32), state_f32], [upstream, shifts, head_w],
-            far=(2,), scratch=held_head,
         )
         head_terms.append((low, upstream_low))
         head_sums.append(head_sum)
@@ -1319,11 +1353,16 @@
                 [((TOK, D), NARROW), ((TOK, FF), NARROW), state_f32, ((1, FF), f32), ((3, D), f32),
                  payload],
                 [grad_state, before, mixed, norms[depth], spread, row_fwd, *mlp_low[depth]],
-                far=(6, 7, 8, 9), scratch=held_mlp,
+                far=(6, 7, 8, 9), scratch=held_mlp, limit=26,
             )
+            mlp_terms[depth].append((g_before, hidden_in, hidden, grad_out))
             got = exchange(sent)
+            if roll_idx == 0 and depth == L - 1:
+                last_sends = mlp_sends(depth)
+                last_kept, got = lax.optimization_barrier((mlp_kept(*last_sends), got))
+                last_halves = chip_halves([last_kept], 2, 1, 3)
             if roll_idx == 0 and depth == 0:
-                last_chip, got = lax.optimization_barrier((mlp_chip(*last_sends), got))
+                last_halves, got = held_back(chip_stage(last_halves, 1), got)
             out, g_pair, g_pair_b = launch(
                 spec_back_kernel, "spec_back",
                 [payload, ((2, 2 * LANES, 2 * LANES), f32), ((2, 2 * LANES), f32)],
@@ -1331,17 +1370,12 @@
                 scratch=(wide, wide),
             )
             got = exchange(out)
-            if roll_idx == 0 and depth == 0:
-                mlp_second, got = lax.optimization_barrier((mlp_line(L - 1, last_chip), got))
+            if roll_idx == 0 and depth == L - 1:
+                last_halves, got = held_back(chip_stage(last_halves, 0), got)
             grad_state, state_low, sums_one = launch(
                 norm_back_kernel, "norm_back", [state_f32, ((TOK, D), NARROW), ((3, D), f32)],
                 [got, g_mixed, state, norms[depth], spread, row_back],
             )
-            mlp_terms[depth].append((g_before, hidden_in, hidden, grad_out))
-            if roll_idx == 0 and depth == L - 1:
-                pairs, sends = mlp_sends(depth)
-                grad_state, *sends = lax.optimization_barrier((grad_state, *sends))
-                last_sends = (pairs, sends)
             spec_terms[depth].append((g_pair, g_pair_b))
             sum_terms[depth].append((sums_one, sums_two, g_up_b))
         embed_terms.append((current, state_low))
@@ -1349,11 +1383,13 @@
         if roll_idx:
             (upstream,) = launch(
                 embed_back_kernel, "embed_back", [((TOK, PIX), f32)],
-                [state_low, shifts, saved[roll_idx - 1][3], embed_w], far=(3,), scratch=held_embed,
+                [state_low, shifts, saved[roll_idx - 1][3], embed_w],
             )
 
-    mlp_first = mlp_line(0, mlp_chip(*mlp_sends(0)))
-    mlp_mine = jnp.where(lax.axis_index("zh") == 0, mlp_first, mlp_second)
+    pairs, sends = mlp_sends(0)
+    first_halves = chip_halves([mlp_kept(pairs, sends)], 2, 1, 3)
+    first_halves = chip_stage(chip_stage(first_halves, 0), 1)
+    chips = jnp.concatenate([mlp_joined(first_halves), mlp_joined(last_halves)], axis=0)
 
     def moved_pair(values, amount):
         return jnp.concatenate([jnp.roll(now, amount, axis=0) for now in values], axis=0)
@@ -1379,8 +1415,8 @@
         one = sum(now[0] for now in sum_terms[depth])
         two = sum(now[1] for now in sum_terms[depth])
         g_norm.append(jnp.stack([one[0], one[1], two[1], two[2]]))
-        up_sum = sum(now[2] for now in sum_terms[depth]).reshape(1, 2, 2, 2, -1)
-        up_sum = by_place(up_sum.transpose(0, 2, 1, 3, 4)).reshape(-1)
+        up_sum = sum(now[2] for now in sum_terms[depth]).reshape(1, 2, 2, 2, 2, -1)
+        up_sum = by_place(up_sum.transpose(0, 2, 1, 3, 4, 5)).reshape(-1)
         g_mlp_b.append(jnp.concatenate([up_sum, two[0]]))
     full_spec = jnp.zeros((L, 2, 2, NB, BS, BS), NARROW)
     full_spec = lax.dynamic_update_slice_in_dim(
@@ -1397,15 +1433,19 @@
     rest_grad = jnp.pad(rest_grad, (0, -rest_grad.shape[0] % (8 * LANES))).reshape(-1, 8, LANES)
     plan = pack_plan(width, total, devices)
     window_set = ((4, 2, 2, WINDOW, 8, LANES), NARROW)
+    rest_grad, *sends = lax.optimization_barrier((rest_grad, *sends))
     kept, sent = launch(
         functools.partial(pack_kernel, plan), "pack", [window_set, window_set],
         [jnp.stack([x, y, c])] + [tiles_of(g) for g in g_embed + g_head] + [rest_grad],
         near=(0,), far_out=True, scratch=(sem((len(plan),)),), limit=8,
     )
-    kept = chip_sum(add_low(kept, swap(sent, "c")), 1, 2, 3).reshape(4, WINDOW, 8, LANES)
-    flat_piece = own_range(line_sum(kept, [0, 1, 2, 3]), device, width, total, devices)
+    halves = chip_stage(chip_halves([kept, swap(sent, "c")], 1, 2, 3), 0)
+    halves = chip_stage(halves, 1)
+    mlp_mine = line_sum(chips, [0, 1, 2, 3])
+    flat_window = line_sum(chip_join(halves, 3).reshape(4, WINDOW, 8, LANES), [0, 1, 2, 3])
+    flat_piece = own_range(flat_window, device, width, total, devices)
     local = jnp.stack(
-        [jnp.sum(flat_piece * flat_piece) + jnp.sum(mlp_mine * mlp_mine),
+        [jnp.sum(jnp.where(own_mask > 0, flat_window * flat_window, 0.0)) + jnp.sum(mlp_mine * mlp_mine),
          sum(jnp.sum(now) for now in loss_sums)]
     )
     square_sum, loss_total = total_over(local, SUB_AXES)
@@ -1414,8 +1454,6 @@
     factor = jnp.minimum(1.0, CLIP_LEVEL / (grad_norm + 1e-06))
 
     mlp_grad = lax.all_gather(mlp_mine.astype(NARROW), LAT_AXES, axis=0, tiled=True)
-    mlp_grad = mlp_grad.reshape(mlp_momentum.shape).astype(f32)
-    momentum_new = MOMENT_KEEP * mlp_momentum + mlp_grad * factor
 
     held = mlp_momentum.reshape(2 * L * 2, rows_own, D)
     held = lax.dynamic_index_in_dim(held, lat_index, 0, keepdims=False)
@@ -1437,7 +1475,11 @@
     extra = jnp.zeros((8, D), NARROW)
     extra = extra.at[0, 0].set(level_high).at[0, 1].set(level_mid).at[0, 2].set(level_low)
     change = lax.dynamic_slice_in_dim((change * inverse).astype(NARROW), c * (D // 2), D // 2, 0)
-    gathered = line_gather(jnp.concatenate([change, extra], axis=0))
+    packed = jnp.concatenate([change, extra], axis=0)
+    packed, mlp_grad = lax.optimization_barrier((packed, mlp_grad))
+    gathered = line_gather(packed)
+    mlp_grad = mlp_grad.reshape(mlp_momentum.shape).astype(f32)
+    momentum_new = MOMENT_KEEP * mlp_momentum + mlp_grad * factor
     levels = jnp.sum(gathered[:, D // 2, :3].astype(f32), axis=-1)
     gathered = gathered[:, : D // 2]
     other = swap(gathered, "c")

time: 1130 us -> 1010 us (0.89)
  waiting for transfers between devices: 409 us -> 332 us
  local copies, waits for them, and re-layouts: 197 us -> 173 us
  blocking collectives: 24 us -> 0 us
    all_to_all x3, waiting for transfers between devices: 26.5 us -> 70.1 us  [to_items(): lax.all_to_all(packed, LAT_AXES, split_axis=0, concat_axis=0, tiled=True)]
    ppermute x3, waiting for transfers between devices: 67.4 us -> 24.1 us  [line_gather(): lax.ppermute(value, Z_AXES, [(i, i - 1) for i in range(1, 5 - step)])]
    ppermute x30 -> x34, waiting for transfers between devices: 170 us -> 137 us  [swap(): return lax.ppermute(values, axis, [(0, 1), (1, 0)])]
    all_gather x1, waiting for transfers between devices: 29.8 us -> 0.01 us  [fast_body(): windows = lax.all_gather(own, SUB_AXES)]
    all_to_all x2 -> x0, blocking collectives: 24 us -> none  [exchange(): lax.all_to_all(values, ITEM_AXES, split_axis=0, concat_axis=0, tiled=True)]
    unnamed x431 -> x456, local copies, waits for them, and re-layouts: 103 us -> 83.3 us
    ppermute x14 -> x12, starting transfers between devices: 52.6 us -> 34.6 us  [line_sum(): moving = lax.ppermute(value, Z_AXES, pairs)]
    pallas_call x0 -> x2, Pallas kernels: none -> 14 us  [own_quarters(): pl.pallas_call(narrow_kernel, name='narrow', out_shape=jax.ShapeDtypeStru...]
  transfers between devices with their start and end apart: 71 -> 75, of which waited for: 42 -> 41; matrix products, arithmetic and copies ran while one was open for 15% -> 25% of each run, Pallas kernels for 4% -> 5%
where the time goes in v2:
time: 1010 us; the launch traced here: 999 us
  waiting for transfers between devices  332 us (33%)
  local copies, waits for them, and re-layouts  173 us (17%)
  starting transfers between devices  165 us (16%)
  Pallas kernels  143 us (14%)
  other arithmetic  99.4 us (10%)
  matrix products  60.6 us (6%)
  between operations  25.9 us (3%)
    ppermute x34, waiting for transfers between devices, swap(): return lax.ppermute(values, axis, [(0, 1), (1, 0)])  137 us
    pallas_call x31, Pallas kernels, launch(): pl.pallas_call(kernel, name=name, out_shape=[jax.ShapeDtypeStruct(dims, k...  120 us
    unnamed x456, local copies, waits for them, and re-layouts  83.3 us
    all_to_all x3, waiting for transfers between devices, to_items(): lax.all_to_all(packed, LAT_AXES, split_axis=0, concat_axis=0, tiled=True)  70.1 us
    all_to_all x16, starting transfers between devices, exchange(): lax.all_to_all(values, ITEM_AXES, split_axis=0, concat_axis=0, tiled=True)  64.3 us
    all_to_all x16, waiting for transfers between devices, exchange(): lax.all_to_all(values, ITEM_AXES, split_axis=0, concat_axis=0, tiled=True)  54.6 us
    dot_general x14, matrix products, dot_tn(): lax.dot_general(left, right, (((0,), (0,)), ((), ())), preferred_element_...  38.8 us
    ppermute x34, starting transfers between devices, swap(): return lax.ppermute(values, axis, [(0, 1), (1, 0)])  37.4 us
  transfers between devices with their start and end apart: 75, of which 41 were waited for; matrix products, arithmetic and copies ran while one was open for 25% of the time, Pallas kernels for 5%

profile of v2, /device:TPU:0, one launch (start us, length us, event | category | flops | bytes accessed | tf_op | source)
XLA Modules:
  0.0 998.6 jit_solution(11317178961118671123)
XLA Ops:
  15.6 8.1 slice_bitcast_fusion
  23.7 7.0 narrow.2.w0_ref
  34.9 14.8 %collective-permute-done = bf16[2,192,768]{2,1,0:T(8,128)(2,1)S(1)} collective-permute-done((bf16[2,192,768]{2,1,0:T(8,128)(2,1)S(1)}, bf16[2,192,768]{2,1,0:T(8,128)(2,1)S(1)}, u32[]{:S(2)}, u32[]{:S(2)}) %collective-permute-start) | collective-permute-done | bytes 589856 | tf_op jit(solution)/shard_map/ppermute | solution.py:1073
  50.8 7.0 narrow.3.w0_ref
  61.5 12.1 %collective-permute-done.1 = bf16[2,192,768]{2,1,0:T(8,128)(2,1)S(1)} collective-permute-done((bf16[2,192,768]{2,1,0:T(8,128)(2,1)S(1)}, bf16[2,192,768]{2,1,0:T(8,128)(2,1)S(1)}, u32[]{:S(2)}, u32[]{:S(2)}) %collective-permute-start.1) | collective-permute-done | bytes 589856 | tf_op jit(solution)/shard_map/ppermute | solution.py:1073
  89.2 60.9 %all-to-all-done = bf16[8,18,1280]{2,1,0:T(8,128)(2,1)} async-done(((bf16[8,18,1280]{2,1,0:T(8,128)(2,1)}), bf16[8,18,1280]{2,1,0:T(8,128)(2,1)}, u32[]{:S(2)}, u32[]{:S(2)}) %all-to-all-start) | async-done | bytes 368672 | tf_op jit(solution)/shard_map/all_to_all | solution.py:1214
  165.6 5.9 join_embed.1
  181.1 7.9 all-to-all-done.1.in_ref
  217.0 5.8 mlp.4
  227.1 9.2 all-to-all-done.5
  243.6 4.4 all-to-all-done.3.in_ref
  252.0 4.4 all-to-all-start.4
  260.3 6.0 join_head.1
  266.5 6.9 mlp.5
  281.4 5.2 all-to-all-start.8
  305.7 6.4 all-to-all-done.9.in_ref
  312.1 7.5 mlp.6
  329.7 5.3 all-to-all-done.10.in_ref
  339.0 4.6 all-to-all-start.11
  346.8 5.0 all-to-all-done.11.in_ref
  352.7 6.8 mlp.7
  365.5 6.8 mlp_back.4
  381.4 4.8 all-to-all-done.12.in_ref
  407.3 6.8 mlp_back.5
  423.4 5.3 all-to-all-done.14.in_ref
  461.1 6.9 mlp_back.6
  514.0 4.4 all-to-all-start.17
  524.8 10.7 %collective-permute-done.13 = bf16[2,1,2,192,768]{4,3,2,1,0:T(8,128)(2,1)} collective-permute-done((bf16[2,1,2,192,768]{4,3,2,1,0:T(8,128)(2,1)}, bf16[2,1,2,192,768]{4,3,2,1,0:T(8,128)(2,1)}, u32[]{:S(2)}, u32[]{:S(2)}) %collective-permute-start.13) | collective-permute-done | bytes 1179680 | tf_op jit(solution)/shard_map/ppermute | solution.py:1073
  538.5 11.6 %collective-permute-done.12 = bf16[2,2,1,192,768]{4,3,2,1,0:T(8,128)(2,1)} collective-permute-done((bf16[2,2,1,192,768]{4,3,2,1,0:T(8,128)(2,1)}, bf16[2,2,1,192,768]{4,3,2,1,0:T(8,128)(2,1)}, u32[]{:S(2)}, u32[]{:S(2)}) %collective-permute-start.12) | collective-permute-done | bytes 1179680 | tf_op jit(solution)/shard_map/ppermute | solution.py:1073
  556.0 6.8 mlp_back.7
  601.7 4.4 reshape.576
  615.9 6.2 pack.1
  637.8 23.6 %collective-permute-done.29 = bf16[2,2,1,192,768]{4,3,2,1,0:T(8,128)(2,1)} collective-permute-done((bf16[2,2,1,192,768]{4,3,2,1,0:T(8,128)(2,1)}, bf16[2,2,1,192,768]{4,3,2,1,0:T(8,128)(2,1)}, u32[]{:S(2)}, u32[]{:S(2)}) %collective-permute-start.29) | collective-permute-done | bytes 1179680 | tf_op jit(solution)/shard_map/ppermute | solution.py:1073
  674.1 5.6 collective-permute-done.30
  691.0 24.7 %collective-permute-done.21 = bf16[4,2,1,106,8,128]{5,4,3,2,1,0:T(8,128)(2,1)S(1)} collective-permute-done((bf16[4,2,1,106,8,128]{5,4,3,2,1,0:T(8,128)(2,1)S(1)}, bf16[4,2,1,106,8,128]{5,4,3,2,1,0:T(8,128)(2,1)S(1)}, u32[]{:S(2)}, u32[]{:S(2)}) %collective-permute-start.21) | collective-permute-done | bytes 1736736 | tf_op jit(solution)/shard_map/ppermute | solution.py:1073
  762.5 5.3 collective-permute-start.24
  781.9 5.5 collective-permute-start.25
  799.3 4.7 collective-permute-done.25
  804.0 13.6 %collective-permute-done.28 = bf16[212,8,128]{2,1,0:T(8,128)(2,1)} collective-permute-done((bf16[212,8,128]{2,1,0:T(8,128)(2,1)}, bf16[212,8,128]{2,1,0:T(8,128)(2,1)}, u32[]{:S(2)}, u32[]{:S(2)}) %collective-permute-start.28) | collective-permute-done | bytes 434208 | tf_op jit(solution)/shard_map/ppermute | solution.py:1138
  825.3 7.2 all-to-all-done.20
  833.8 4.6 fusion.21
  844.7 9.8 collective-permute-done.40
  856.8 6.7 collective-permute-done.41
  896.7 12.0 %collective-permute-done.45 = bf16[392,768]{1,0:T(8,128)(2,1)S(1)} collective-permute-done((bf16[392,768]{1,0:T(8,128)(2,1)S(1)}, bf16[392,768]{1,0:T(8,128)(2,1)S(1)}, u32[]{:S(2)}, u32[]{:S(2)}) %collective-permute-start.45) | collective-permute-done | bytes 602144 | tf_op jit(solution)/shard_map/ppermute | solution.py:1170
  919.5 11.4 %collective-permute-done.49 = bf16[392,768]{1,0:T(8,128)(2,1)} collective-permute-done((bf16[392,768]{1,0:T(8,128)(2,1)}, bf16[392,768]{1,0:T(8,128)(2,1)}, u32[]{:S(2)}, u32[]{:S(2)}) %collective-permute-start.49) | collective-permute-done | bytes 602144 | tf_op jit(solution)/shard_map/ppermute | solution.py:1174
  937.4 9.9 collective-permute-done.50
  959.7 11.3 %multiply_add_fusion = f32[2,2,768,768]{3,2,1,0:T(8,128)} fusion(f32[2,2,768,768]{3,2,1,0:T(8,128)} %bitcast.379, f32[2,2,768,768]{3,2,1,0:T(8,128)} %param.29), kind=kLoop, calls=%fused_computation.1 | loop fusion | flops 4718592 | bytes 28311552 | tf_op jit(solution)/shard_map/add | solution.py:1482
  980.9 8.4 muon.1
  (871 shorter events, 532.5 us)
Async XLA Ops:
  7.2 153.9 %all-gather.6.cloned.1.call-start = ((), (), s32[]{:S(2)}) async-start(), calls=%async_computation.22 | async-start | bytes 14327808 | tf_op jit(solution)/shard_map/all_gather | solution.py:1219
  31.9 17.8 %collective-permute-start = (bf16[2,192,768]{2,1,0:T(8,128)(2,1)S(1)}, bf16[2,192,768]{2,1,0:T(8,128)(2,1)S(1)}, u32[]{:S(2)}, u32[]{:S(2)}) collective-permute-start(bf16[2,192,768]{2,1,0:T(8,128)(2,1)S(1)} %slice_bitcast_fusion.7), channel_id=1, source_target_pairs={{0,2},{2,0},{1,3},{3,1},{4,6},{6,4},{5,7},{7,5},{8,10},{10,8},{9,1... | collective-permute-start | bytes 1769480 | tf_op jit(solution)/shard_map/ppermute | solution.py:1073
  49.7 23.8 %collective-permute-start.1 = (bf16[2,192,768]{2,1,0:T(8,128)(2,1)S(1)}, bf16[2,192,768]{2,1,0:T(8,128)(2,1)S(1)}, u32[]{:S(2)}, u32[]{:S(2)}) collective-permute-start(bf16[2,192,768]{2,1,0:T(8,128)(2,1)S(1)} %collective-permute-done), channel_id=1, source_target_pairs={{0,4},{4,0},{1,5},{5,1},{2,6},{6,2},{3,7},{7,3},{8,12},{12,8},{9,1... | collective-permute-start | bytes 1769480 | tf_op jit(solution)/shard_map/ppermute | solution.py:1073
  58.9 23.1 %collective-permute-start.5 = (bf16[2,192,768]{2,1,0:T(8,128)(2,1)S(1)}, bf16[2,192,768]{2,1,0:T(8,128)(2,1)S(1)}, u32[]{:S(2)}, u32[]{:S(2)}) collective-permute-start(bf16[2,192,768]{2,1,0:T(8,128)(2,1)S(1)} %slice_bitcast_fusion.4), channel_id=1, source_target_pairs={{0,2},{2,0},{1,3},{3,1},{4,6},{6,4},{5,7},{7,5},{8,10},{10,8},{9,1... | collective-permute-start | bytes 1769480 | tf_op jit(solution)/shard_map/ppermute | solution.py:1073
  74.7 83.2 %collective-permute-start.2 = (bf16[2,2,192,768]{3,2,1,0:T(8,128)(2,1)}, bf16[2,2,192,768]{3,2,1,0:T(8,128)(2,1)}, u32[]{:S(2)}, u32[]{:S(2)}) collective-permute-start(bf16[2,2,192,768]{3,2,1,0:T(8,128)(2,1)} %pad_maximum_fusion.5), channel_id=1, source_target_pairs={{0,8},{8,0},{1,9},{9,1},{2,10},{10,2},{3,11},{11,3},{4,12},{12,4},... | collective-permute-start | bytes 3538952 | tf_op jit(solution)/shard_map/ppermute | solution.py:1073
  76.2 139.8 %collective-permute-start.3 = (bf16[2,4,192,768]{3,2,1,0:T(8,128)(2,1)}, bf16[2,4,192,768]{3,2,1,0:T(8,128)(2,1)}, u32[]{:S(2)}, u32[]{:S(2)}) collective-permute-start(bf16[2,4,192,768]{3,2,1,0:T(8,128)(2,1)} %bitcast.22), channel_id=1, source_target_pairs={{0,1},{1,0},{2,3},{3,2},{4,5},{5,4},{6,7},{7,6},{8,9},{9,8},{10,11... | collective-permute-start | bytes 7077896 | tf_op jit(solution)/shard_map/ppermute | solution.py:1073
  76.2 190.2 %collective-permute-start.8 = (bf16[2,4,192,768]{3,2,1,0:T(8,128)(2,1)}, bf16[2,4,192,768]{3,2,1,0:T(8,128)(2,1)}, u32[]{:S(2)}, u32[]{:S(2)}) collective-permute-start(bf16[2,4,192,768]{3,2,1,0:T(8,128)(2,1)} %bitcast.38), channel_id=1, source_target_pairs={{0,1},{1,0},{2,3},{3,2},{4,5},{5,4},{6,7},{7,6},{8,9},{9,8},{10,11... | collective-permute-start | bytes 7077896 | tf_op jit(solution)/shard_map/ppermute | solution.py:1073
  77.8 72.2 %all-to-all-start = ((bf16[8,18,1280]{2,1,0:T(8,128)(2,1)}), bf16[8,18,1280]{2,1,0:T(8,128)(2,1)}, u32[]{:S(2)}, u32[]{:S(2)}) async-start(bf16[8,18,1280]{2,1,0:T(8,128)(2,1)} %copy.196), calls=%async_computation | async-start | bytes 983040 | tf_op jit(solution)/shard_map/all_to_all | solution.py:1214
  82.1 72.7 %collective-permute-start.6 = (bf16[2,192,768]{2,1,0:T(8,128)(2,1)S(1)}, bf16[2,192,768]{2,1,0:T(8,128)(2,1)S(1)}, u32[]{:S(2)}, u32[]{:S(2)}) collective-permute-start(bf16[2,192,768]{2,1,0:T(8,128)(2,1)S(1)} %collective-permute-done.5), channel_id=1, source_target_pairs={{0,4},{4,0},{1,5},{5,1},{2,6},{6,2},{3,7},{7,3},{8,12},{12,8},{9,1... | collective-permute-start | bytes 1769480 | tf_op jit(solution)/shard_map/ppermute | solution.py:1073
  150.1 27.1 %all-to-all-start.6 = ((f32[8,1,18]{2,1,0:T(1,128)}), f32[8,1,18]{2,1,0:T(1,128)S(1)}, u32[]{:S(2)}, u32[]{:S(2)}) async-start(f32[8,1,18]{2,1,0:T(1,128)} %copy.216), calls=%async_computation.6 | async-start | bytes 8192 | tf_op jit(solution)/shard_map/all_to_all | solution.py:1214
  155.9 47.4 %collective-permute-start.7 = (bf16[2,2,192,768]{3,2,1,0:T(8,128)(2,1)}, bf16[2,2,192,768]{3,2,1,0:T(8,128)(2,1)}, u32[]{:S(2)}, u32[]{:S(2)}) collective-permute-start(bf16[2,2,192,768]{3,2,1,0:T(8,128)(2,1)} %pad_maximum_fusion.6), channel_id=1, source_target_pairs={{0,8},{8,0},{1,9},{9,1},{2,10},{10,2},{3,11},{11,3},{4,12},{12,4},... | collective-permute-start | bytes 3538952 | tf_op jit(solution)/shard_map/ppermute | solution.py:1073
  161.1 54.9 %collective-permute-start.4 = (bf16[2,4,192,768]{3,2,1,0:T(8,128)(2,1)}, bf16[2,4,192,768]{3,2,1,0:T(8,128)(2,1)}, u32[]{:S(2)}, u32[]{:S(2)}) collective-permute-start(bf16[2,4,192,768]{3,2,1,0:T(8,128)(2,1)} %pad_maximum_fusion.2), channel_id=1, source_target_pairs={{0,1},{1,0},{2,3},{3,2},{4,5},{5,4},{6,7},{7,6},{8,9},{9,8},{10,11... | collective-permute-start | bytes 7077896 | tf_op jit(solution)/shard_map/ppermute | solution.py:1073
  207.6 58.9 %collective-permute-start.9 = (bf16[2,4,192,768]{3,2,1,0:T(8,128)(2,1)}, bf16[2,4,192,768]{3,2,1,0:T(8,128)(2,1)}, u32[]{:S(2)}, u32[]{:S(2)}) collective-permute-start(bf16[2,4,192,768]{3,2,1,0:T(8,128)(2,1)} %pad_maximum_fusion.3), channel_id=1, source_target_pairs={{0,1},{1,0},{2,3},{3,2},{4,5},{5,4},{6,7},{7,6},{8,9},{9,8},{10,11... | collective-permute-start | bytes 7077896 | tf_op jit(solution)/shard_map/ppermute | solution.py:1073
  211.4 25.0 %all-to-all-start.5 = ((bf16[8,36,1280]{2,1,0:T(8,128)(2,1)}), bf16[8,36,1280]{2,1,0:T(8,128)(2,1)}, u32[]{:S(2)}, u32[]{:S(2)}) async-start(bf16[8,36,1280]{2,1,0:T(8,128)(2,1)} %copy.211), calls=%async_computation.5 | async-start | bytes 1638400 | tf_op jit(solution)/shard_map/all_to_all | solution.py:1214
  471.0 21.8 %collective-permute-start.10 = (bf16[1536,768]{1,0:T(8,128)(2,1)}, bf16[1536,768]{1,0:T(8,128)(2,1)}, u32[]{:S(2)}, u32[]{:S(2)}) collective-permute-start(bf16[1536,768]{1,0:T(8,128)(2,1)} %convolution_convert_fusion.9), channel_id=1, source_target_pairs={{0,1},{1,0},{2,3},{3,2},{4,5},{5,4},{6,7},{7,6},{8,9},{9,8},{10,11... | collective-permute-start | bytes 7077896 | tf_op jit(solution)/shard_map/ppermute | solution.py:1073
  473.9 22.1 %collective-permute-start.11 = (bf16[1536,768]{1,0:T(8,128)(2,1)}, bf16[1536,768]{1,0:T(8,128)(2,1)}, u32[]{:S(2)}, u32[]{:S(2)}) collective-permute-start(bf16[1536,768]{1,0:T(8,128)(2,1)} %convolution_convert_fusion.8), channel_id=1, source_target_pairs={{0,1},{1,0},{2,3},{3,2},{4,5},{5,4},{6,7},{7,6},{8,9},{9,8},{10,11... | collective-permute-start | bytes 7077896 | tf_op jit(solution)/shard_map/ppermute | solution.py:1073
  474.4 27.3 %all-to-all-start.16 = ((bf16[16,72,128]{2,1,0:T(8,128)(2,1)}), bf16[16,72,128]{2,1,0:T(8,128)(2,1)S(1)}, u32[]{:S(2)}, u32[]{:S(2)}) async-start(bf16[16,72,128]{2,1,0:T(8,128)(2,1)} %get-tuple-element.190), calls=%async_computation.16 | async-start | bytes 589824 | tf_op jit(solution)/shard_map/all_to_all | solution.py:863
  504.2 31.3 %collective-permute-start.13 = (bf16[2,1,2,192,768]{4,3,2,1,0:T(8,128)(2,1)}, bf16[2,1,2,192,768]{4,3,2,1,0:T(8,128)(2,1)}, u32[]{:S(2)}, u32[]{:S(2)}) collective-permute-start(bf16[2,1,2,192,768]{4,3,2,1,0:T(8,128)(2,1)} %slice.535), channel_id=1, source_target_pairs={{0,2},{2,0},{1,3},{3,1},{4,6},{6,4},{5,7},{7,5},{8,10},{10,8},{9,1... | collective-permute-start | bytes 3538952 | tf_op jit(solution)/shard_map/ppermute | solution.py:1073
  514.0 39.0 %all-to-all-start.17 = ((bf16[16,72,128]{2,1,0:T(8,128)(2,1)}), bf16[16,72,128]{2,1,0:T(8,128)(2,1)S(1)}, u32[]{:S(2)}, u32[]{:S(2)}) async-start(bf16[16,72,128]{2,1,0:T(8,128)(2,1)} %copy-done.82), calls=%async_computation.17 | async-start | bytes 589824 | tf_op jit(solution)/shard_map/all_to_all | solution.py:863
  518.4 31.7 %collective-permute-start.12 = (bf16[2,2,1,192,768]{4,3,2,1,0:T(8,128)(2,1)}, bf16[2,2,1,192,768]{4,3,2,1,0:T(8,128)(2,1)}, u32[]{:S(2)}, u32[]{:S(2)}) collective-permute-start(bf16[2,2,1,192,768]{4,3,2,1,0:T(8,128)(2,1)} %slice.533), channel_id=1, source_target_pairs={{0,4},{4,0},{1,5},{5,1},{2,6},{6,2},{3,7},{7,3},{8,12},{12,8},{9,1... | collective-permute-start | bytes 3538952 | tf_op jit(solution)/shard_map/ppermute | solution.py:1073
  563.6 27.6 %all-to-all-start.18 = ((bf16[16,72,128]{2,1,0:T(8,128)(2,1)}), bf16[16,72,128]{2,1,0:T(8,128)(2,1)S(1)}, u32[]{:S(2)}, u32[]{:S(2)}) async-start(bf16[16,72,128]{2,1,0:T(8,128)(2,1)} %get-tuple-element.202), calls=%async_computation.18 | async-start | bytes 589824 | tf_op jit(solution)/shard_map/all_to_all | solution.py:863
  569.7 17.0 %collective-permute-start.15 = (bf16[2,1,1,192,768]{4,3,2,1,0:T(8,128)(2,1)}, bf16[2,1,1,192,768]{4,3,2,1,0:T(8,128)(2,1)}, u32[]{:S(2)}, u32[]{:S(2)}) collective-permute-start(bf16[2,1,1,192,768]{4,3,2,1,0:T(8,128)(2,1)} %slice.539), channel_id=1, source_target_pairs={{0,4},{4,0},{1,5},{5,1},{2,6},{6,2},{3,7},{7,3},{8,12},{12,8},{9,1... | collective-permute-start | bytes 1769480 | tf_op jit(solution)/shard_map/ppermute | solution.py:1073
  578.0 36.4 %collective-permute-start.17 = (bf16[1536,768]{1,0:T(8,128)(2,1)}, bf16[1536,768]{1,0:T(8,128)(2,1)}, u32[]{:S(2)}, u32[]{:S(2)}) collective-permute-start(bf16[1536,768]{1,0:T(8,128)(2,1)} %convolution_convert_fusion.6), channel_id=1, source_target_pairs={{0,1},{1,0},{2,3},{3,2},{4,5},{5,4},{6,7},{7,6},{8,9},{9,8},{10,11... | collective-permute-start | bytes 7077896 | tf_op jit(solution)/shard_map/ppermute | solution.py:1073
  580.9 33.5 %collective-permute-start.16 = (bf16[1536,768]{1,0:T(8,128)(2,1)}, bf16[1536,768]{1,0:T(8,128)(2,1)}, u32[]{:S(2)}, u32[]{:S(2)}) collective-permute-start(bf16[1536,768]{1,0:T(8,128)(2,1)} %convolution_convert_fusion.7), channel_id=1, source_target_pairs={{0,1},{1,0},{2,3},{3,2},{4,5},{5,4},{6,7},{7,6},{8,9},{9,8},{10,11... | collective-permute-start | bytes 7077896 | tf_op jit(solution)/shard_map/ppermute | solution.py:1073
  598.5 293.4 %all-gather.4.cloned.1.call-start = ((), (), s32[]{:S(2)}) async-start(), calls=%async_computation.21 | async-start | bytes 5308416 | tf_op jit(solution)/shard_map/all_gather | solution.py:1456
  625.0 43.7 %collective-permute-start.18 = (bf16[4,2,2,212,8,128]{5,4,3,2,1,0:T(8,128)(2,1)}, bf16[4,2,2,212,8,128]{5,4,3,2,1,0:T(8,128)(2,1)}, u32[]{:S(2)}, u32[]{:S(2)}) collective-permute-start(bf16[4,2,2,212,8,128]{5,4,3,2,1,0:T(8,128)(2,1)} %get-tuple-element.244), channel_id=1, source_target_pairs={{0,1},{1,0},{2,3},{3,2},{4,5},{5,4},{6,7},{7,6},{8,9},{9,8},{10,11... | collective-permute-start | bytes 20840456 | tf_op jit(solution)/shard_map/ppermute | solution.py:1073
  632.7 28.7 %collective-permute-start.29 = (bf16[2,2,1,192,768]{4,3,2,1,0:T(8,128)(2,1)}, bf16[2,2,1,192,768]{4,3,2,1,0:T(8,128)(2,1)}, u32[]{:S(2)}, u32[]{:S(2)}) collective-permute-start(bf16[2,2,1,192,768]{4,3,2,1,0:T(8,128)(2,1)} %fusion.10), channel_id=1, source_target_pairs={{0,4},{4,0},{1,5},{5,1},{2,6},{6,2},{3,7},{7,3},{8,12},{12,8},{9,1... | collective-permute-start | bytes 3538952 | tf_op jit(solution)/shard_map/ppermute | solution.py:1073
  635.8 29.8 %collective-permute-start.31 = (bf16[2,1,2,192,768]{4,3,2,1,0:T(8,128)(2,1)}, bf16[2,1,2,192,768]{4,3,2,1,0:T(8,128)(2,1)}, u32[]{:S(2)}, u32[]{:S(2)}) collective-permute-start(bf16[2,1,2,192,768]{4,3,2,1,0:T(8,128)(2,1)} %fusion.9), channel_id=1, source_target_pairs={{0,2},{2,0},{1,3},{3,1},{4,6},{6,4},{5,7},{7,5},{8,10},{10,8},{9,1... | collective-permute-start | bytes 3538952 | tf_op jit(solution)/shard_map/ppermute | solution.py:1073
  663.2 16.5 %collective-permute-start.30 = (bf16[2,1,1,192,768]{4,3,2,1,0:T(8,128)(2,1)S(1)}, bf16[2,1,1,192,768]{4,3,2,1,0:T(8,128)(2,1)S(1)}, u32[]{:S(2)}, u32[]{:S(2)}) collective-permute-start(bf16[2,1,1,192,768]{4,3,2,1,0:T(8,128)(2,1)S(1)} %slice.673), channel_id=1, source_target_pairs={{0,2},{2,0},{1,3},{3,1},{4,6},{6,4},{5,7},{7,5},{8,10},{10,8},{9,1... | collective-permute-start | bytes 1769480 | tf_op jit(solution)/shard_map/ppermute | solution.py:1073
  667.1 16.3 %collective-permute-start.32 = (bf16[2,1,1,192,768]{4,3,2,1,0:T(8,128)(2,1)S(1)}, bf16[2,1,1,192,768]{4,3,2,1,0:T(8,128)(2,1)S(1)}, u32[]{:S(2)}, u32[]{:S(2)}) collective-permute-start(bf16[2,1,1,192,768]{4,3,2,1,0:T(8,128)(2,1)S(1)} %slice.677), channel_id=1, source_target_pairs={{0,4},{4,0},{1,5},{5,1},{2,6},{6,2},{3,7},{7,3},{8,12},{12,8},{9,1... | collective-permute-start | bytes 1769480 | tf_op jit(solution)/shard_map/ppermute | solution.py:1073
  670.6 45.2 %collective-permute-start.21 = (bf16[4,2,1,106,8,128]{5,4,3,2,1,0:T(8,128)(2,1)S(1)}, bf16[4,2,1,106,8,128]{5,4,3,2,1,0:T(8,128)(2,1)S(1)}, u32[]{:S(2)}, u32[]{:S(2)}) collective-permute-start(bf16[4,2,1,106,8,128]{5,4,3,2,1,0:T(8,128)(2,1)S(1)} %add_convert_fusion.5), channel_id=1, source_target_pairs={{0,2},{2,0},{1,3},{3,1},{4,6},{6,4},{5,7},{7,5},{8,10},{10,8},{9,1... | collective-permute-start | bytes 5210120 | tf_op jit(solution)/shard_map/ppermute | solution.py:1073
  672.8 46.8 %collective-permute-start.19 = (bf16[4,1,2,106,8,128]{5,4,3,2,1,0:T(8,128)(2,1)S(1)}, bf16[4,1,2,106,8,128]{5,4,3,2,1,0:T(8,128)(2,1)S(1)}, u32[]{:S(2)}, u32[]{:S(2)}) collective-permute-start(bf16[4,1,2,106,8,128]{5,4,3,2,1,0:T(8,128)(2,1)S(1)} %add_convert_fusion.7), channel_id=1, source_target_pairs={{0,4},{4,0},{1,5},{5,1},{2,6},{6,2},{3,7},{7,3},{8,12},{12,8},{9,1... | collective-permute-start | bytes 5210120 | tf_op jit(solution)/shard_map/ppermute | solution.py:1073
  685.4 41.0 %collective-permute-start.33 = (bf16[384,768]{1,0:T(8,128)(2,1)}, bf16[384,768]{1,0:T(8,128)(2,1)}, u32[]{:S(2)}, u32[]{:S(2)}) collective-permute-start(bf16[384,768]{1,0:T(8,128)(2,1)} %get-tuple-element.268), channel_id=1, source_target_pairs={{0,8},{1,9},{2,10},{3,11},{4,12},{5,13},{6,14},{7,15}} | collective-permute-start | bytes 1769480 | tf_op jit(solution)/shard_map/ppermute | solution.py:1138
  689.6 36.8 %collective-permute-start.36 = (bf16[384,768]{1,0:T(8,128)(2,1)}, bf16[384,768]{1,0:T(8,128)(2,1)}, u32[]{:S(2)}, u32[]{:S(2)}) collective-permute-start(bf16[384,768]{1,0:T(8,128)(2,1)} %get-tuple-element.269), channel_id=1, source_target_pairs={{24,16},{25,17},{26,18},{27,19},{28,20},{29,21},{30,22},{31,23}} | collective-permute-start | bytes 1769480 | tf_op jit(solution)/shard_map/ppermute | solution.py:1138
  718.0 20.3 %collective-permute-start.22 = (bf16[4,1,1,106,8,128]{5,4,3,2,1,0:T(8,128)(2,1)S(1)}, bf16[4,1,1,106,8,128]{5,4,3,2,1,0:T(8,128)(2,1)}, u32[]{:S(2)}, u32[]{:S(2)}) collective-permute-start(bf16[4,1,1,106,8,128]{5,4,3,2,1,0:T(8,128)(2,1)S(1)} %slice.663), channel_id=1, source_target_pairs={{0,4},{4,0},{1,5},{5,1},{2,6},{6,2},{3,7},{7,3},{8,12},{12,8},{9,1... | collective-permute-start | bytes 2605064 | tf_op jit(solution)/shard_map/ppermute | solution.py:1073
  723.2 20.2 %collective-permute-start.20 = (bf16[4,1,1,106,8,128]{5,4,3,2,1,0:T(8,128)(2,1)}, bf16[4,1,1,106,8,128]{5,4,3,2,1,0:T(8,128)(2,1)}, u32[]{:S(2)}, u32[]{:S(2)}) collective-permute-start(bf16[4,1,1,106,8,128]{5,4,3,2,1,0:T(8,128)(2,1)} %slice.659), channel_id=1, source_target_pairs={{0,2},{2,0},{1,3},{3,1},{4,6},{6,4},{5,7},{7,5},{8,10},{10,8},{9,1... | collective-permute-start | bytes 2605064 | tf_op jit(solution)/shard_map/ppermute | solution.py:1073
  729.3 24.0 %collective-permute-start.34 = (bf16[384,768]{1,0:T(8,128)(2,1)}, bf16[384,768]{1,0:T(8,128)(2,1)}, u32[]{:S(2)}, u32[]{:S(2)}) collective-permute-start(bf16[384,768]{1,0:T(8,128)(2,1)} %get-tuple-element.266), channel_id=1, source_target_pairs={{0,8},{8,16},{1,9},{9,17},{2,10},{10,18},{3,11},{11,19},{4,12},{12... | collective-permute-start | bytes 1769480 | tf_op jit(solution)/shard_map/ppermute | solution.py:1138
  733.6 19.7 %collective-permute-start.37 = (bf16[384,768]{1,0:T(8,128)(2,1)}, bf16[384,768]{1,0:T(8,128)(2,1)}, u32[]{:S(2)}, u32[]{:S(2)}) collective-permute-start(bf16[384,768]{1,0:T(8,128)(2,1)} %get-tuple-element.267), channel_id=1, source_target_pairs={{24,16},{16,8},{25,17},{17,9},{26,18},{18,10},{27,19},{19,11},{28,... | collective-permute-start | bytes 1769480 | tf_op jit(solution)/shard_map/ppermute | solution.py:1138
  756.2 15.6 %collective-permute-start.35 = (bf16[384,768]{1,0:T(8,128)(2,1)}, bf16[384,768]{1,0:T(8,128)(2,1)}, u32[]{:S(2)}, u32[]{:S(2)}) collective-permute-start(bf16[384,768]{1,0:T(8,128)(2,1)} %get-tuple-element.264), channel_id=1, source_target_pairs={{0,8},{8,16},{16,24},{1,9},{9,17},{17,25},{2,10},{10,18},{18,26},{... | collective-permute-start | bytes 1769480 | tf_op jit(solution)/shard_map/ppermute | solution.py:1138
  762.5 16.9 %collective-permute-start.24 = (bf16[212,8,128]{2,1,0:T(8,128)(2,1)}, bf16[212,8,128]{2,1,0:T(8,128)(2,1)}, u32[]{:S(2)}, u32[]{:S(2)}) collective-permute-start(bf16[212,8,128]{2,1,0:T(8,128)(2,1)} %get-tuple-element.272), channel_id=1, source_target_pairs={{0,8},{8,16},{1,9},{9,17},{2,10},{10,18},{3,11},{11,19},{4,12},{12... | collective-permute-start | bytes 1302536 | tf_op jit(solution)/shard_map/ppermute | solution.py:1138
  781.9 22.1 %collective-permute-start.25 = (bf16[212,8,128]{2,1,0:T(8,128)(2,1)}, bf16[212,8,128]{2,1,0:T(8,128)(2,1)}, u32[]{:S(2)}, u32[]{:S(2)}) collective-permute-start(bf16[212,8,128]{2,1,0:T(8,128)(2,1)} %get-tuple-element.270), channel_id=1, source_target_pairs={{0,8},{8,16},{16,24},{1,9},{9,17},{17,25},{2,10},{10,18},{18,26},{... | collective-permute-start | bytes 1302536 | tf_op jit(solution)/shard_map/ppermute | solution.py:1138
  787.4 30.2 %collective-permute-start.28 = (bf16[212,8,128]{2,1,0:T(8,128)(2,1)}, bf16[212,8,128]{2,1,0:T(8,128)(2,1)}, u32[]{:S(2)}, u32[]{:S(2)}) collective-permute-start(bf16[212,8,128]{2,1,0:T(8,128)(2,1)} %get-tuple-element.271), channel_id=1, source_target_pairs={{24,16},{16,8},{8,0},{25,17},{17,9},{9,1},{26,18},{18,10},{10,2},{... | collective-permute-start | bytes 1302536 | tf_op jit(solution)/shard_map/ppermute | solution.py:1138
  892.0 16.7 %collective-permute-start.45 = (bf16[392,768]{1,0:T(8,128)(2,1)S(1)}, bf16[392,768]{1,0:T(8,128)(2,1)S(1)}, u32[]{:S(2)}, u32[]{:S(2)}) collective-permute-start(bf16[392,768]{1,0:T(8,128)(2,1)S(1)} %pad_maximum_fusion.10), channel_id=1, source_target_pairs={{0,8},{8,16},{16,24},{1,9},{9,17},{17,25},{2,10},{10,18},{18,26},{... | collective-permute-start | bytes 1806344 | tf_op jit(solution)/shard_map/ppermute | solution.py:1170
  895.4 17.6 %collective-permute-start.48 = (bf16[392,768]{1,0:T(8,128)(2,1)S(1)}, bf16[392,768]{1,0:T(8,128)(2,1)}, u32[]{:S(2)}, u32[]{:S(2)}) collective-permute-start(bf16[392,768]{1,0:T(8,128)(2,1)S(1)} %pad_maximum_fusion.10), channel_id=1, source_target_pairs={{8,0},{16,8},{24,16},{9,1},{17,9},{25,17},{10,2},{18,10},{26,18},{... | collective-permute-start | bytes 1806344 | tf_op jit(solution)/shard_map/ppermute | solution.py:1174
  913.0 17.9 %collective-permute-start.49 = (bf16[392,768]{1,0:T(8,128)(2,1)}, bf16[392,768]{1,0:T(8,128)(2,1)}, u32[]{:S(2)}, u32[]{:S(2)}) collective-permute-start(bf16[392,768]{1,0:T(8,128)(2,1)} %collective-permute-done.48), channel_id=1, source_target_pairs={{8,0},{16,8},{9,1},{17,9},{10,2},{18,10},{11,3},{19,11},{12,4},{20... | collective-permute-start | bytes 1806344 | tf_op jit(solution)/shard_map/ppermute | solution.py:1174
  914.3 18.2 %collective-permute-start.47 = (bf16[392,768]{1,0:T(8,128)(2,1)}, bf16[392,768]{1,0:T(8,128)(2,1)}, u32[]{:S(2)}, u32[]{:S(2)}) collective-permute-start(bf16[392,768]{1,0:T(8,128)(2,1)} %collective-permute-done.46), channel_id=1, source_target_pairs={{16,24},{17,25},{18,26},{19,27},{20,28},{21,29},{22,30},{23,31}} | collective-permute-start | bytes 1806344 | tf_op jit(solution)/shard_map/ppermute | solution.py:1170
  930.9 16.3 %collective-permute-start.50 = (bf16[392,768]{1,0:T(8,128)(2,1)}, bf16[392,768]{1,0:T(8,128)(2,1)S(1)}, u32[]{:S(2)}, u32[]{:S(2)}) collective-permute-start(bf16[392,768]{1,0:T(8,128)(2,1)} %collective-permute-done.49), channel_id=1, source_target_pairs={{8,0},{9,1},{10,2},{11,3},{12,4},{13,5},{14,6},{15,7}} | collective-permute-start | bytes 1806344 | tf_op jit(solution)/shard_map/ppermute | solution.py:1174
  950.6 21.3 %collective-permute-start.51 = (bf16[4,384,768]{2,1,0:T(8,128)(2,1)}, bf16[4,384,768]{2,1,0:T(8,128)(2,1)}, u32[]{:S(2)}, u32[]{:S(2)}) collective-permute-start(bf16[4,384,768]{2,1,0:T(8,128)(2,1)} %constant_dynamic-slice_fusion), channel_id=1, source_target_pairs={{0,1},{1,0},{2,3},{3,2},{4,5},{5,4},{6,7},{7,6},{8,9},{9,8},{10,11... | collective-permute-start | bytes 7077896 | tf_op jit(solution)/shard_map/ppermute | solution.py:1073
  (243 other events, 2635.8 us)
Sparse Core Ops, SparseCore 0:
  15.1 136.3 all-gather.5
  776.3 91.2 all-gather.3

commit v3 on v2

--- a/solution.py
+++ b/solution.py
@@ -482,6 +482,9 @@
 FREQ = PAIRS * 96
 NARROW = jnp.bfloat16
 WINDOW = 212
+MLP_LIMIT = 26
+WINDOW_CUTS = (0, 72, 142, WINDOW)
+MLP_CUTS = (0, 128, 256, 384)
 EMBED_AT = 2
 Z_AXES = ("zh", "zl")
 EMBED_SIZE = 3 * PIX * D
@@ -636,7 +639,7 @@
     for offset, weight in enumerate(thirds(w_ref, PIX)):
         moved = src if offset == 1 else dot(shift_ref[offset], src).astype(NARROW)
         state = state + dot(moved, weight)
-    state_ref[...] = state
+    state_ref.put(state)
     scaled, _unused = normalize(state)
     normed = scaled * norm_ref[0:1] + norm_ref[1:2]
     send_rows(normed.astype(NARROW), spread_ref, row_ref, send_ref)
@@ -664,7 +667,7 @@
     for chunk in range(4):
         pairs = range(chunk * 3, chunk * 3 + 3)
         mixed = jnp.concatenate([turn_columns(wide_ref, col_ref, pair) for pair in pairs], axis=0)
-        mixed_ref[chunk * 288 : (chunk + 1) * 288, :] = mixed
+        mixed_ref.put(mixed, slice(chunk * 288, (chunk + 1) * 288), slice(None))
         inner = dot(mixed, w_ref[0]) + b_ref[0:1]
         act = (inner * bell(inner)).astype(NARROW)
         outer = (dot(act, w_ref[1]) + b_ref[1:2]).astype(NARROW)
@@ -682,7 +685,7 @@
     for chunk in range(4):
         pairs = range(chunk * 3, chunk * 3 + 3)
         g_outer = jnp.concatenate([turn_columns(wide_ref, col_ref, pair) for pair in pairs], axis=0)
-        mixed = mixed_ref[chunk * 288 : (chunk + 1) * 288, :]
+        mixed = mixed_ref()[chunk * 288 : (chunk + 1) * 288, :]
         inner = dot(mixed, w_ref[0]) + b_ref[0:1]
         area = bell(inner)
         act = (inner * area).astype(NARROW)
@@ -709,23 +712,23 @@
     mixed_ref, hidden_in_ref, before_ref, hidden_ref, out_ref = rest[:5]
     copies = fetch((w0_ref, w1_ref, w2_ref, w3_ref), held_ref, sems)
     spatial = take_rows(in_ref, spread_ref, row_back_ref)
-    state = state_ref[...]
+    state = state_ref()[...]
     scaled, _unused = normalize(state)
     mixed = state + spatial + (scaled * norm_ref[0:1] + norm_ref[1:2])
-    mixed_ref[...] = mixed
+    mixed_ref.put(mixed)
     again, _unused = normalize(mixed)
     hidden_in = (again * norm_ref[2:3] + norm_ref[3:4]).astype(NARROW)
-    hidden_in_ref[...] = hidden_in
+    hidden_in_ref.put(hidden_in)
     out = mixed + down_b_ref[...]
     for part in range(4):
         spot = slice(part * D, (part + 1) * D)
         copies[part].wait()
         before = dot_nt(hidden_in, held_ref[part, 0]) + up_b_ref[:, spot]
-        before_ref[:, spot] = before
+        before_ref.put(before, slice(None), spot)
         hidden = (before * bell(before)).astype(NARROW)
-        hidden_ref[:, spot] = hidden
+        hidden_ref.put(hidden, slice(None), spot)
         out = out + dot(hidden, held_ref[part, 1])
-    out_ref[...] = out
+    out_ref.put(out)
     if has_next:
         scaled, _unused = normalize(out)
         normed = scaled * next_norm_ref[0:1] + next_norm_ref[1:2]
@@ -734,21 +737,21 @@
 
 def head_kernel(state_ref, shift_ref, bias_ref, target_ref, weight_ref, w_ref,
                 low_ref, pred_ref, grad_ref, loss_ref):
-    low = state_ref[...].astype(NARROW)
-    low_ref[...] = low
+    low = state_ref()[...].astype(NARROW)
+    low_ref.put(low)
     predicted = bias_ref[...]
     for offset, weight in enumerate(thirds(w_ref, D)):
         moved = low if offset == 1 else dot(shift_ref[offset], low).astype(NARROW)
         predicted = predicted + dot(moved, weight)
     pred_ref[...] = predicted.astype(NARROW)
-    differ = predicted - target_ref[...].astype(jnp.float32)
+    differ = predicted - target_ref()[...].astype(jnp.float32)
+    grad_ref.put(weight_ref[:, 1:2] * differ)
     loss_ref[...] = column_sum(weight_ref[:, 0:1] * differ * differ)
-    grad_ref[...] = weight_ref[:, 1:2] * differ
 
 
 def head_back_kernel(grad_ref, shift_ref, w_ref, low_ref, sum_ref, out_ref):
-    low = grad_ref[...].astype(NARROW)
-    low_ref[...] = low
+    low = grad_ref()[...].astype(NARROW)
+    low_ref.put(low)
     sum_ref[...] = column_sum(low.astype(jnp.float32))
     total = None
     for offset, weight in enumerate(thirds(w_ref, D)):
@@ -760,11 +763,12 @@
 
 def embed_back_kernel(low_ref, shift_ref, add_ref, w_ref, out_ref):
     low = low_ref[...]
-    total = add_ref[...]
+    total = None
     for offset, weight in enumerate(thirds(w_ref, PIX)):
         moved = low if offset == 1 else dot(shift_ref[2 - offset], low).astype(NARROW)
-        total = total + dot_nt(moved, weight)
-    out_ref[...] = total
+        part = dot_nt(moved, weight)
+        total = part if total is None else total + part
+    out_ref.put(add_ref()[...] + total)
 
 
 def mlp_back_kernel(up_ref, before_ref, mixed_ref, norm_ref, spread_ref, row_ref,
@@ -774,32 +778,33 @@
     copies = fetch((w0_ref, w1_ref, w2_ref, w3_ref), held_ref, sems)
     upstream = up_ref[...]
     grad_out = upstream.astype(NARROW)
-    grad_out_ref[...] = grad_out
+    grad_out_ref.put(grad_out)
     sums_ref[0:1] = column_sum(grad_out.astype(jnp.float32))
     g_second = None
     for part in range(4):
         spot = slice(part * D, (part + 1) * D)
-        before = before_ref[:, spot]
+        before = before_ref()[:, spot]
         slope = bell_slope(before, bell(before))
         copies[part].wait()
         g_before = (slope * dot_nt(grad_out, held_ref[part, 1])).astype(NARROW)
-        g_before_ref[:, spot] = g_before
+        g_before_ref.put(g_before, slice(None), spot)
         g_up_b_ref[:, spot] = column_sum(g_before.astype(jnp.float32))
         now = dot(g_before, held_ref[part, 0])
         g_second = now if g_second is None else g_second + now
-    scaled, inverse = normalize(mixed_ref[...])
+    scaled, inverse = normalize(mixed_ref()[...])
     sums_ref[1:2] = column_sum(g_second * scaled)
     sums_ref[2:3] = column_sum(g_second)
     g_mixed = upstream + normalize_back(g_second, scaled, inverse, norm_ref[2:3])
-    g_mixed_ref[...] = g_mixed
+    g_mixed_ref.put(g_mixed)
     send_rows(g_mixed.astype(NARROW), spread_ref, row_ref, send_ref)
 
 
 def norm_back_kernel(in_ref, g_mixed_ref, state_ref, norm_ref, spread_ref, row_back_ref,
                      out_ref, low_ref, sums_ref):
-    g_mixed = g_mixed_ref[...]
-    g_normed = take_rows(in_ref, spread_ref, row_back_ref) + g_mixed
-    scaled, inverse = normalize(state_ref[...])
+    g_normed = take_rows(in_ref, spread_ref, row_back_ref)
+    g_mixed = g_mixed_ref()[...]
+    g_normed = g_normed + g_mixed
+    scaled, inverse = normalize(state_ref()[...])
     out = g_mixed + normalize_back(g_normed, scaled, inverse, norm_ref[0:1])
     out_ref[...] = out
     low = out.astype(NARROW)
@@ -813,21 +818,23 @@
     out_ref[...] = in_ref[...].astype(NARROW)
 
 
-def own_quarters(weights, place):
-    size = weights.shape[1] // 4
+def own_quarters(weights, depth, place):
+    size = weights.shape[2] // 4
 
     def from_spot(m, q, place_ref):
-        return (m, (q // 2 + place_ref[0]) % 2 * 2 + (q % 2 + place_ref[1]) % 2, 0)
+        return (depth, m, (q // 2 + place_ref[0]) % 2 * 2 + q % 2, 0)
 
     return pl.pallas_call(
         narrow_kernel,
         name="narrow",
-        out_shape=jax.ShapeDtypeStruct(weights.shape, NARROW),
+        out_shape=jax.ShapeDtypeStruct((2, 2, 2, size, D), NARROW),
         grid_spec=pltpu.PrefetchScalarGridSpec(
             num_scalar_prefetch=1,
-            grid=(weights.shape[0], 4),
-            in_specs=[pl.BlockSpec((None, size, D), from_spot)],
-            out_specs=pl.BlockSpec((None, size, D), lambda m, q, place_ref: (m, q, 0)),
+            grid=(2, 4),
+            in_specs=[pl.BlockSpec((None, None, size, D), from_spot)],
+            out_specs=pl.BlockSpec(
+                (None, None, None, size, D), lambda m, q, place_ref: (m, q // 2, q % 2, 0, 0)
+            ),
         ),
     )(place, weights)
 
@@ -839,7 +846,39 @@
     out_ref[...] = weight_ref[...] * (1.0 - MUON_RATE * DECAY_RATE) - MUON_RATE * (FF / D) ** 0.5 * ortho
 
 
-def launch(kernel, name, out_dims, operands, far=(), far_out=False, near=(), scratch=(), limit=16):
+class Coming:
+    def __init__(self, far_ref, held_ref, sem):
+        self.held, self.copy = held_ref, pltpu.make_async_copy(far_ref, held_ref, sem)
+        self.copy.start()
+
+    def __call__(self):
+        if self.copy is not None:
+            self.copy.wait()
+        self.copy = None
+        return self.held
+
+
+class Going:
+    def __init__(self, far_ref, held_ref, sems):
+        self.far, self.held, self.sems, self.copies = far_ref, held_ref, sems, []
+
+    def put(self, value, *spot):
+        if spot:
+            self.held[spot] = value
+            source, target = self.held.at[spot], self.far.at[spot]
+        else:
+            self.held[...] = value
+            source, target = self.held, self.far
+        copy = pltpu.make_async_copy(source, target, self.sems.at[len(self.copies)])
+        copy.start()
+        self.copies.append(copy)
+
+
+PIECES = 4
+
+
+def launch(kernel, name, out_dims, operands, far=(), far_out=False, near=(), scratch=(), limit=16,
+           coming=(), going=()):
     anywhere = pl.BlockSpec(memory_space=pltpu.HBM)
     local = pl.BlockSpec(memory_space=pltpu.VMEM)
     in_specs = []
@@ -847,14 +886,44 @@
         if i in near:
             in_specs.append(pl.BlockSpec(memory_space=pltpu.SMEM))
         else:
-            in_specs.append(anywhere if i in far else local)
+            in_specs.append(anywhere if i in far or i in coming else local)
+    sem = pltpu.SemaphoreType.DMA
+    staged = [pltpu.VMEM(operands[i].shape, operands[i].dtype) for i in coming]
+    staged += [pltpu.VMEM(*out_dims[i]) for i in going]
+    staged += [sem((len(coming),))] * bool(coming) + [sem((PIECES,))] * len(going)
+    ins, outs = len(operands), len(out_dims)
+
+    def body(*refs):
+        refs, rest = list(refs[: ins + outs]), refs[ins + outs :]
+        held, rest = rest[: len(staged)], rest[len(staged) :]
+        tail = len(coming) + len(going)
+        for number, i in enumerate(coming):
+            refs[i] = Coming(refs[i], held[number], held[tail].at[number])
+        sent = []
+        for number, i in enumerate(going):
+            sems = held[tail + bool(coming) + number]
+            refs[ins + i] = Going(refs[ins + i], held[len(coming) + number], sems)
+            sent.append(refs[ins + i])
+        kernel(*refs, *rest)
+        for way in sent:
+            for copy in way.copies:
+                copy.wait()
+
+    operands = [
+        pltpu.with_memory_space_constraint(a, pltpu.HBM) if i in far or i in coming else a
+        for i, a in enumerate(operands)
+    ]
+    out_shape = [
+        pltpu.HBM(*dims) if far_out or i in going else jax.ShapeDtypeStruct(*dims)
+        for i, dims in enumerate(out_dims)
+    ]
     return pl.pallas_call(
-        kernel,
+        body,
         name=name,
-        out_shape=[jax.ShapeDtypeStruct(dims, kind) for dims, kind in out_dims],
+        out_shape=out_shape,
         in_specs=in_specs,
-        out_specs=[anywhere if far_out else local for unused in out_dims],
-        scratch_shapes=list(scratch),
+        out_specs=[anywhere if far_out or i in going else local for i in range(outs)],
+        scratch_shapes=staged + list(scratch),
         compiler_params=pltpu.CompilerParams(vmem_limit_bytes=limit * 1024 * 1024),
     )(*operands)
 
@@ -952,70 +1021,113 @@
     return result
 
 
+def gather_windows(own, *early):
+    value, *early = lax.optimization_barrier((jnp.stack([own, swap(own, "zh")]), *early))
+    thirds = []
+    ways = ["x", "y", "zl"]
+    for i in range(3):
+        part = value[:, WINDOW_CUTS[i] : WINDOW_CUTS[i + 1]]
+        for axis in ways[i:] + ways[:i]:
+            part = jnp.stack([part, swap(part, axis)])
+        thirds.append((part, swap(part, "c")))
+    return thirds, *early
+
+
 def join_plan(kind, width, total, count):
+    tiles = KINDS[kind][1]
     pieces = []
     for index in range(count):
         for piece in window_pieces(index, width, total):
             if piece[0] == kind:
-                pieces.append((index,) + tuple(piece[1:4]))
+                pieces.append((index, piece[1] * tiles, piece[2] * tiles, piece[3]))
     single, double = [], []
-    for place, (index, first, last, tile) in enumerate(pieces):
-        if place:
-            shared = pieces[place - 1][2]
-            before = pieces[place - 1]
-            if shared > first:
-                double.append((first, shared, before[0], before[3], before[1], index, tile))
-        else:
-            shared = first
-        follow = pieces[place + 1][1] if place + 1 < len(pieces) else last
-        begin, end = max(first, shared), min(last, follow)
+    for spot, (index, first, last, tile) in enumerate(pieces):
+        begin, end = first, last
+        if spot and pieces[spot - 1][2] > first:
+            before, before_first, begin, before_tile = pieces[spot - 1]
+            double.append((first, begin - first, before, before_tile + first - before_first, index, tile))
+        if spot + 1 < len(pieces):
+            end = min(last, pieces[spot + 1][1])
         if begin < end:
-            single.append((begin, end, index, tile, first))
+            single.append((begin, end - begin, index, tile + begin - first))
     return single, double
 
 
-def join_kernel(tiles, single, double, got_ref, out_ref, left_ref, right_ref, sems, left_sems, right_sems):
-    copies = []
-    for place, (begin, end, index, tile, first) in enumerate(single):
-        source = got_ref.at[index, pl.ds(tile + (begin - first) * tiles, (end - begin) * tiles)]
-        target = out_ref.at[pl.ds(begin * tiles, (end - begin) * tiles)]
-        copies.append(pltpu.make_async_copy(source, target, sems.at[place]))
-    loads = []
-    for place, (begin, end, before, before_tile, before_first, index, tile) in enumerate(double):
-        size = (end - begin) * tiles
-        source = got_ref.at[before, pl.ds(before_tile + (begin - before_first) * tiles, size)]
-        loads.append(pltpu.make_async_copy(source, left_ref.at[place, pl.ds(0, size)], left_sems.at[place]))
-        source = got_ref.at[index, pl.ds(tile, size)]
-        loads.append(pltpu.make_async_copy(source, right_ref.at[place, pl.ds(0, size)], right_sems.at[place]))
-    for copy in loads + copies:
-        copy.start()
-    for copy in loads:
+def by_thirds(size, tile):
+    found = []
+    for third in range(3):
+        begin, end = max(tile, WINDOW_CUTS[third]), min(tile + size, WINDOW_CUTS[third + 1])
+        if begin < end:
+            found.append((third, begin - WINDOW_CUTS[third], end - begin, begin - tile))
+    return found
+
+
+def join_kernel(single, double, place_ref, *refs):
+    sources, (out_ref, left_ref, right_ref, sems) = refs[:6], refs[6:]
+    own = [place_ref[i] for i in range(5)]
+    count = 0
+
+    def start(index, size, tile, target_ref, at):
+        nonlocal count
+        rel = {
+            axis: (index // unit + spot) % 2
+            for axis, unit, spot in zip(SUB_AXES, (16, 8, 4, 2, 1), own)
+        }
+        ways = ["x", "y", "zl"]
+        ends = []
+        for third, begin, amount, offset in by_thirds(size, tile):
+            spots = [rel[axis] for axis in (ways[third:] + ways[:third])[::-1]] + [rel["zh"]]
+            sources_now = sources[2 * third : 2 * third + 2]
+            copies = [
+                pltpu.make_async_copy(
+                    ref.at[(*spots, pl.ds(begin, amount))],
+                    target_ref.at[pl.ds(at + offset, amount)],
+                    sems.at[count],
+                )
+                for ref in sources_now
+            ]
+            count += 1
+
+            @pl.when(rel["c"] == 0)
+            def _():
+                copies[0].start()
+
+            @pl.when(rel["c"] == 1)
+            def _():
+                copies[1].start()
+
+            ends.append(copies[0])
+        return ends
+
+    edges = []
+    for spot, (begin, size, before, before_tile, index, tile) in enumerate(double):
+        edges += start(before, size, before_tile, left_ref.at[spot], 0)
+        edges += start(index, size, tile, right_ref.at[spot], 0)
+    ends = []
+    for begin, size, index, tile in single:
+        ends += start(index, size, tile, out_ref, begin)
+    for copy in edges:
         copy.wait()
-    stores = []
-    for place, (begin, end, *unused) in enumerate(double):
-        size = (end - begin) * tiles
-        total = left_ref[place, :size].astype(jnp.float32) + right_ref[place, :size].astype(jnp.float32)
-        left_ref[place, :size] = total.astype(NARROW)
-        target = out_ref.at[pl.ds(begin * tiles, size)]
-        stores.append(pltpu.make_async_copy(left_ref.at[place, pl.ds(0, size)], target, left_sems.at[place]))
-        stores[-1].start()
-    for copy in copies + stores:
+    for spot, (begin, size, *unused) in enumerate(double):
+        both = left_ref[spot, :size].astype(jnp.float32) + right_ref[spot, :size].astype(jnp.float32)
+        out_ref[begin : begin + size] = both.astype(NARROW)
+    for copy in ends:
         copy.wait()
 
 
-def join_windows(got, kind, width, total, count):
+def join_windows(thirds, place, kind, width, total, count):
     row, tiles = KINDS[kind]
     low, high = kind_ranges(total)[kind]
     single, double = join_plan(kind, width, total, count)
     groups = -(-(high - low) // (8 * row))
-    deep = max([(d[1] - d[0]) * tiles for d in double] + [1])
-    held = pltpu.VMEM((max(len(double), 1), deep, 8, LANES), NARROW)
-    sem = pltpu.SemaphoreType.DMA
+    amount = sum(len(by_thirds(size, tile)) for begin, size, index, tile in single)
+    for begin, size, before, before_tile, index, tile in double:
+        amount += len(by_thirds(size, before_tile)) + len(by_thirds(size, tile))
+    held = pltpu.VMEM((max(len(double), 1), max([d[1] for d in double] + [1]), 8, LANES), NARROW)
     (out,) = launch(
-        functools.partial(join_kernel, tiles, single, double), "join_" + kind,
-        [((groups * tiles, 8, LANES), NARROW)], [got], far=(0,),
-        scratch=(held, held, sem((max(len(single), 1),)), sem((max(len(double), 1),)), sem((max(len(double), 1),))),
-        limit=50,
+        functools.partial(join_kernel, single, double), "join_" + kind,
+        [((groups * tiles, 8, LANES), NARROW)], [place] + [ref for pair in thirds for ref in pair],
+        near=(0,), far=tuple(range(1, 7)), scratch=(held, held, pltpu.SemaphoreType.DMA((amount,))),
     )
     return out.reshape(groups, tiles, 8, LANES).transpose(0, 2, 1, 3).reshape(groups * 8, row)
 
@@ -1041,11 +1153,12 @@
 
 def pack_kernel(plan, place_ref, *refs):
     sources, (keep_ref, send_ref, sems) = refs[:7], refs[7:]
-    x, y, c = place_ref[0], place_ref[1], place_ref[2]
+    zh, zl, x, y, c = (place_ref[i] for i in range(5))
     ends = []
     for number, (index, source, begin, size, tile) in enumerate(plan):
-        plane, side, depth, core = index // 8, index // 4 % 2, index // 2 % 2, index % 2
-        spot = (plane, (side + x) % 2, (depth + y) % 2, pl.ds(tile, size))
+        core = index % 2
+        place = zip((16, 8, 4, 2), (zh, zl, x, y))
+        spot = tuple((index // unit + own) % 2 for unit, own in place) + (pl.ds(tile, size),)
         from_ref = sources[source].at[pl.ds(begin, size)]
         keep = pltpu.make_async_copy(from_ref, keep_ref.at[spot], sems.at[number])
         send = pltpu.make_async_copy(from_ref, send_ref.at[spot], sems.at[number])
@@ -1077,67 +1190,36 @@
     return sum(v.astype(jnp.float32) for v in values).astype(NARROW)
 
 
-def side(values, dim, which):
-    return lax.index_in_dim(values, which, dim, keepdims=True)
-
-
-def chip_halves(kept, x_dim, y_dim, cut_dim):
-    half = kept[0].shape[cut_dim] // 2
-    ways = ((x_dim, "x"), (y_dim, "y"))
+def side(values, dim, which, turn):
+    if turn is None:
+        return lax.index_in_dim(values, which, dim, keepdims=True)
+    return lax.dynamic_slice_in_dim(values, (which + turn) % 2, 1, dim)
+
+
+def chip_parts(kept, ways, cuts, cut_dim):
     return [
-        ([lax.slice_in_dim(v, start, start + half, axis=cut_dim) for v in kept], order)
-        for start, order in ((0, ways), (half, ways[::-1]))
+        ([lax.slice_in_dim(v, cuts[i], cuts[i + 1], axis=cut_dim) for v in kept], ways[i:] + ways[:i])
+        for i in range(3)
     ]
 
 
-def chip_stage(halves, stage):
+def chip_stage(parts, stage):
     result = []
-    for values, order in halves:
-        dim, axis = order[stage]
-        got = swap(add_low(*(side(v, dim, 1) for v in values)), axis)
-        result.append(([add_low(got, *(side(v, dim, 0) for v in values))], order))
+    for values, order in parts:
+        dim, axis, turn = order[stage]
+        got = swap(add_low(*(side(v, dim, 1, turn) for v in values)), axis)
+        result.append(([add_low(got, *(side(v, dim, 0, turn) for v in values))], order))
     return result
 
 
-def chip_join(halves, cut_dim):
-    return jnp.concatenate([values[0] for values, order in halves], axis=cut_dim)
-
-
-def held_back(halves, *others):
-    flat = [values[0] for values, order in halves]
+def chip_join(parts, cut_dim):
+    return jnp.concatenate([values[0] for values, order in parts], axis=cut_dim)
+
+
+def held_back(parts, *others):
+    flat = [values[0] for values, order in parts]
     flat, others = lax.optimization_barrier((flat, others))
-    return [([v], order) for v, (unused, order) in zip(flat, halves)], *others
-
-
-def line_sum(parts, owners):
-    plane = lax.axis_index(Z_AXES)
-
-    def pick(number):
-        return lax.dynamic_index_in_dim(
-            parts, jnp.clip(number - owners[0], 0, len(owners) - 1), 0, keepdims=False
-        )
-
-    total = pick(plane).astype(jnp.float32)
-    for mirror in (False, True):
-        here = 3 - plane if mirror else plane
-        moving = None
-        for step in (1, 2, 3):
-            pairs = []
-            for spot in range(3):
-                number = 4 - step + spot
-                owner = 3 - number if mirror else number
-                if number > 3 or owner not in owners:
-                    continue
-                pairs.append((3 - spot, 2 - spot) if mirror else (spot, spot + 1))
-            if not pairs:
-                continue
-            number = 4 - step + here
-            value = pick(3 - number if mirror else number)
-            if moving is not None:
-                value = add_low(value, moving)
-            moving = lax.ppermute(value, Z_AXES, pairs)
-        total = total + moving.astype(jnp.float32)
-    return total
+    return [([v], order) for v, (unused, order) in zip(flat, parts)], *others
 
 
 def plane_sum(values):
@@ -1215,20 +1297,27 @@
         got = got.reshape((items * 4, lead, rows * OWN) + rest)
         return jnp.moveaxis(got, 1, 0).reshape((lead, TOK) + rest)
 
+    source = to_items(pixels[None])[0]
+    zh, zl = lax.axis_index("zh"), lax.axis_index("zl")
+    place = jnp.stack([zh, zl, x, y, c])
     own = own_window(adam_params, device, width, total, devices).astype(NARROW)
-    windows = lax.all_gather(own, SUB_AXES)
+    quarters = [own_quarters(mlp_weights, depth, x[None]) for depth in range(L)]
+    windows, source, *quarters = gather_windows(own, source, *quarters)
     own_mask = own_window(jnp.ones((width,), jnp.float32), device, width, total, devices)
-    zl = lax.axis_index("zl")
     mlp_low = []
-    for depth in range(L):
-        own = own_quarters(mlp_weights[depth], jnp.stack([x, zl])).reshape(2, 4, D // 4, D)
-        first = swap(own[:, 0], "y")
-        second = swap(first, "x")
-        others = swap(jnp.stack([first, second]), "zl")
-        across_y = jnp.stack([first, others[0], second, others[1]], axis=1)
+    for depth, own in enumerate(quarters):
+        if depth % 2 == 0:
+            first = swap(lax.dynamic_index_in_dim(own[:, 0], zl, 1, keepdims=False), "y")
+            both = jnp.stack([first, swap(first, "x")], axis=1)
+            others = swap(both, "zl")
+            across_y = jnp.where(
+                zl == 0, jnp.stack([both, others], axis=2), jnp.stack([others, both], axis=2)
+            )
+        else:
+            first = swap(own[:, 0], "y")
+            across_y = jnp.stack([first, swap(first, "x")], axis=1)
         four = (own, across_y, swap(own, "c"), swap(across_y, "c"))
         mlp_low.append([chunk.reshape(2, D, D) for chunk in four])
-    source = to_items(pixels[None])[0]
     wanted = to_items(targets)
     row_weight = jnp.sin(math.pi * (lat_rows.astype(jnp.float32) + 0.5) / ROWS)
     weight_local = row_weight[None, :, None] * mask.astype(jnp.float32)
@@ -1237,9 +1326,9 @@
     loss_scale = 2.0 / (STEPS * PIX * weight_sum)
     weight_pair = jnp.stack([weights, weights * loss_scale], axis=1)
 
-    embed_w = join_windows(windows, "embed", width, total, devices)
-    head_w = join_windows(windows, "head", width, total, devices)
-    rest = join_windows(windows, "rest", width, total, devices)
+    embed_w = join_windows(windows, place, "embed", width, total, devices)
+    head_w = join_windows(windows, place, "head", width, total, devices)
+    rest = join_windows(windows, place, "rest", width, total, devices)
     spec_rows = L * 4 * NB * BS * BS // LANES
     spec_w = rest[:spec_rows].reshape(L, 2, 2, NB, BS, BS)
     embed_b, head_b, spec_b, norm_params, mlp_b = unpack_rest(rest[spec_rows:].reshape(-1))
@@ -1248,11 +1337,11 @@
     mlp_b = mlp_b.astype(jnp.float32)
 
     def by_place(values):
-        for dim, side in ((1, y), (2, c), (3, x), (4, zl)):
+        for dim, side in ((1, y), (2, c), (3, x)):
             values = jnp.where(side == 0, values, jnp.flip(values, dim))
         return values
 
-    up_b = by_place(mlp_b[:, :FF].reshape(L, 2, 2, 2, 2, -1)).transpose(0, 2, 1, 3, 4, 5)
+    up_b = by_place(mlp_b[:, :FF].reshape(L, 2, 2, 2, -1)).transpose(0, 2, 1, 3, 4)
     up_b = up_b.reshape(L, 1, FF)
     down_b = mlp_b[:, None, FF:]
     gap = LANES - BS
@@ -1278,7 +1367,7 @@
     for roll_idx in range(STEPS):
         state, sent = launch(
             embed_kernel, "embed", [state_f32, payload],
-            [current, shifts, embed_b, norms[0], spread, row_fwd, embed_w],
+            [current, shifts, embed_b, norms[0], spread, row_fwd, embed_w], going=(0,),
         )
         layers = []
         for depth in range(L):
@@ -1286,6 +1375,7 @@
             out, mixed_in = launch(
                 spec_kernel, "spec", [payload, ((FREQ, 2 * LANES), NARROW)],
                 [got, col_fwd, col_back, pair_w[depth], pair_b[depth]], scratch=(wide, wide),
+                going=(1,),
             )
             got = exchange(out)
             has_next = depth + 1 < L
@@ -1293,7 +1383,8 @@
             results = launch(
                 functools.partial(mlp_kernel, has_next), "mlp", outs + [payload] * has_next,
                 [got, state, norms[depth], norms[min(depth + 1, L - 1)], up_b[depth], down_b[depth],
-                 spread, row_fwd, row_back, *mlp_low[depth]], far=(9, 10, 11, 12), scratch=held_mlp, limit=26,
+                 spread, row_fwd, row_back, *mlp_low[depth]], far=(9, 10, 11, 12), scratch=held_mlp, limit=MLP_LIMIT,
+                coming=(1,), going=(0, 1, 2, 3, 4),
             )
             layers.append((state, mixed_in) + tuple(results[:4]))
             state = results[4]
@@ -1302,7 +1393,7 @@
         low, predicted, loss_grad, loss_part = launch(
             head_kernel, "head",
             [((TOK, D), NARROW), ((TOK, PIX), NARROW), ((TOK, PIX), f32), ((1, PIX), f32)],
-            [state, shifts, head_b, wanted[roll_idx], weight_pair, head_w],
+            [state, shifts, head_b, wanted[roll_idx], weight_pair, head_w], coming=(0, 3), going=(0, 2),
         )
         loss_sums.append(loss_part)
         saved.append((current, layers, low, loss_grad))
@@ -1313,6 +1404,8 @@
 
     def joined(terms, member):
         return jnp.concatenate([now[member] for now in terms], axis=0)
+
+    mlp_ways = [(3, "x", None), (2, "y", None), (1, "zl", zl)]
 
     def mlp_sends(depth):
         g_before, hidden_in, hidden, grad_out = (joined(mlp_terms[depth], m) for m in range(4))
@@ -1325,11 +1418,6 @@
             for (a, b), sent in zip(pairs, got)
         ]
         return jnp.stack(kept).reshape(2, 2, 2, rows_own, D)
-
-    def mlp_joined(halves):
-        halves = chip_join(halves, 3).reshape(2, 2, rows_own // 2, D)
-        halves = jnp.where(zl == 0, halves, jnp.flip(halves, 1))
-        return halves.reshape(2, rows_own, D)
 
     head_terms, embed_terms = [], []
     mlp_terms = [[] for unused in range(L)]
@@ -1343,6 +1431,7 @@
         upstream_low, head_sum, grad_state = launch(
             head_back_kernel, "head_back",
             [((TOK, PIX), NARROW), ((1, PIX), f32), state_f32], [upstream, shifts, head_w],
+            coming=(0,), going=(0,),
         )
         head_terms.append((low, upstream_low))
         head_sums.append(head_sum)
@@ -1353,28 +1442,28 @@
                 [((TOK, D), NARROW), ((TOK, FF), NARROW), state_f32, ((1, FF), f32), ((3, D), f32),
                  payload],
                 [grad_state, before, mixed, norms[depth], spread, row_fwd, *mlp_low[depth]],
-                far=(6, 7, 8, 9), scratch=held_mlp, limit=26,
+                far=(6, 7, 8, 9), scratch=held_mlp, limit=MLP_LIMIT,
+                coming=(1, 2), going=(0, 1, 2),
             )
             mlp_terms[depth].append((g_before, hidden_in, hidden, grad_out))
             got = exchange(sent)
             if roll_idx == 0 and depth == L - 1:
                 last_sends = mlp_sends(depth)
                 last_kept, got = lax.optimization_barrier((mlp_kept(*last_sends), got))
-                last_halves = chip_halves([last_kept], 2, 1, 3)
             if roll_idx == 0 and depth == 0:
-                last_halves, got = held_back(chip_stage(last_halves, 1), got)
+                first_kept, got = lax.optimization_barrier((mlp_kept(*mlp_sends(0)), got))
             out, g_pair, g_pair_b = launch(
                 spec_back_kernel, "spec_back",
                 [payload, ((2, 2 * LANES, 2 * LANES), f32), ((2, 2 * LANES), f32)],
                 [got, col_fwd, col_back, pair_w[depth], pair_b[depth], mixed_in],
-                scratch=(wide, wide),
+                scratch=(wide, wide), coming=(5,),
             )
             got = exchange(out)
-            if roll_idx == 0 and depth == L - 1:
-                last_halves, got = held_back(chip_stage(last_halves, 0), got)
+            if roll_idx == 0 and depth == 0:
+                last_kept, first_kept, got = lax.optimization_barrier((last_kept, first_kept, got))
             grad_state, state_low, sums_one = launch(
                 norm_back_kernel, "norm_back", [state_f32, ((TOK, D), NARROW), ((3, D), f32)],
-                [got, g_mixed, state, norms[depth], spread, row_back],
+                [got, g_mixed, state, norms[depth], spread, row_back], coming=(1, 2),
             )
             spec_terms[depth].append((g_pair, g_pair_b))
             sum_terms[depth].append((sums_one, sums_two, g_up_b))
@@ -1383,13 +1472,11 @@
         if roll_idx:
             (upstream,) = launch(
                 embed_back_kernel, "embed_back", [((TOK, PIX), f32)],
-                [state_low, shifts, saved[roll_idx - 1][3], embed_w],
+                [state_low, shifts, saved[roll_idx - 1][3], embed_w], coming=(2,), going=(0,),
             )
 
-    pairs, sends = mlp_sends(0)
-    first_halves = chip_halves([mlp_kept(pairs, sends)], 2, 1, 3)
-    first_halves = chip_stage(chip_stage(first_halves, 0), 1)
-    chips = jnp.concatenate([mlp_joined(first_halves), mlp_joined(last_halves)], axis=0)
+    mlp_kept_all = jnp.stack([first_kept, last_kept])
+    mlp_parts = chip_stage(chip_parts([mlp_kept_all], mlp_ways, MLP_CUTS, 4), 0)
 
     def moved_pair(values, amount):
         return jnp.concatenate([jnp.roll(now, amount, axis=0) for now in values], axis=0)
@@ -1415,8 +1502,8 @@
         one = sum(now[0] for now in sum_terms[depth])
         two = sum(now[1] for now in sum_terms[depth])
         g_norm.append(jnp.stack([one[0], one[1], two[1], two[2]]))
-        up_sum = sum(now[2] for now in sum_terms[depth]).reshape(1, 2, 2, 2, 2, -1)
-        up_sum = by_place(up_sum.transpose(0, 2, 1, 3, 4, 5)).reshape(-1)
+        up_sum = sum(now[2] for now in sum_terms[depth]).reshape(1, 2, 2, 2, -1)
+        up_sum = by_place(up_sum.transpose(0, 2, 1, 3, 4)).reshape(-1)
         g_mlp_b.append(jnp.concatenate([up_sum, two[0]]))
     full_spec = jnp.zeros((L, 2, 2, NB, BS, BS), NARROW)
     full_spec = lax.dynamic_update_slice_in_dim(
@@ -1432,17 +1519,26 @@
     rest_grad = jnp.concatenate([full_spec.reshape(-1), small])
     rest_grad = jnp.pad(rest_grad, (0, -rest_grad.shape[0] % (8 * LANES))).reshape(-1, 8, LANES)
     plan = pack_plan(width, total, devices)
-    window_set = ((4, 2, 2, WINDOW, 8, LANES), NARROW)
-    rest_grad, *sends = lax.optimization_barrier((rest_grad, *sends))
+    window_set = ((2, 2, 2, 2, WINDOW, 8, LANES), NARROW)
     kept, sent = launch(
         functools.partial(pack_kernel, plan), "pack", [window_set, window_set],
-        [jnp.stack([x, y, c])] + [tiles_of(g) for g in g_embed + g_head] + [rest_grad],
+        [place] + [tiles_of(g) for g in g_embed + g_head] + [rest_grad],
         near=(0,), far_out=True, scratch=(sem((len(plan),)),), limit=8,
     )
-    halves = chip_stage(chip_halves([kept, swap(sent, "c")], 1, 2, 3), 0)
-    halves = chip_stage(halves, 1)
-    mlp_mine = line_sum(chips, [0, 1, 2, 3])
-    flat_window = line_sum(chip_join(halves, 3).reshape(4, WINDOW, 8, LANES), [0, 1, 2, 3])
+    ways = [(2, "x", None), (3, "y", None), (1, "zl", None)]
+    got = swap(sent, "c")
+    mlp_parts, got = held_back(mlp_parts, got)
+    parts = chip_parts([kept, got], ways, WINDOW_CUTS, 4)
+    for stage in range(3):
+        parts = chip_stage(parts, stage)
+        if stage:
+            mlp_parts = chip_stage(mlp_parts, stage)
+    mlp_pair = chip_join(mlp_parts, 4).reshape(2, rows_own, D)
+    mlp_send = jnp.where(zh == 0, mlp_pair[1], mlp_pair[0])
+    mlp_keep = jnp.where(zh == 0, mlp_pair[0], mlp_pair[1])
+    mlp_mine = mlp_keep.astype(f32) + swap(mlp_send, "zh").astype(f32)
+    flat_pair = chip_join(parts, 4).reshape(2, WINDOW, 8, LANES)
+    flat_window = flat_pair[0].astype(f32) + swap(flat_pair[1], "zh").astype(f32)
     flat_piece = own_range(flat_window, device, width, total, devices)
     local = jnp.stack(
         [jnp.sum(jnp.where(own_mask > 0, flat_window * flat_window, 0.0)) + jnp.sum(mlp_mine * mlp_mine),
@@ -1468,18 +1564,34 @@
     turned = mul(square, poly_one)
     square_two = lead * lead * square + 2.0 * lead * turned + mul(turned, poly_one)
     poly_two = mid * square_two + last * mul(square_two, square_two)
-    change = lead * (poly_one + poly_two) + mul(poly_one, poly_two)
+    mine_one, mine_two = (
+        lax.dynamic_slice_in_dim(now, c * (D // 2), D // 2, 0) for now in (poly_one, poly_two)
+    )
+    change = (lead * (mine_one + mine_two) + mul(mine_one, poly_two)) * inverse
     level_high = inverse.astype(NARROW)
     level_mid = (inverse - level_high.astype(f32)).astype(NARROW)
     level_low = (inverse - level_high.astype(f32) - level_mid.astype(f32)).astype(NARROW)
-    extra = jnp.zeros((8, D), NARROW)
-    extra = extra.at[0, 0].set(level_high).at[0, 1].set(level_mid).at[0, 2].set(level_low)
-    change = lax.dynamic_slice_in_dim((change * inverse).astype(NARROW), c * (D // 2), D // 2, 0)
+    column = jnp.arange(D)[None]
+    extra = jnp.where(column == 0, level_high, jnp.where(column == 1, level_mid, level_low))
+    extra = jnp.broadcast_to(extra, (8, D))
+    change = change.astype(NARROW)
     packed = jnp.concatenate([change, extra], axis=0)
     packed, mlp_grad = lax.optimization_barrier((packed, mlp_grad))
     gathered = line_gather(packed)
     mlp_grad = mlp_grad.reshape(mlp_momentum.shape).astype(f32)
     momentum_new = MOMENT_KEEP * mlp_momentum + mlp_grad * factor
+    clipped = flat_piece * factor
+    first_new = BETA_FIRST * adam_m + (1.0 - BETA_FIRST) * clipped
+    second_new = BETA_SECOND * adam_v + (1.0 - BETA_SECOND) * clipped * clipped
+    count_value = float(STEP_NUM)
+    first_hat = first_new / (1.0 - BETA_FIRST**count_value)
+    second_hat = second_new / (1.0 - BETA_SECOND**count_value)
+    adam_new = adam_params - ADAM_RATE * (
+        first_hat / (jnp.sqrt(second_hat) + 1e-08) + DECAY_RATE * adam_params
+    )
+    gathered, momentum_new, adam_new, first_new, second_new = lax.optimization_barrier(
+        (gathered, momentum_new, adam_new, first_new, second_new)
+    )
     levels = jnp.sum(gathered[:, D // 2, :3].astype(f32), axis=-1)
     gathered = gathered[:, : D // 2]
     other = swap(gathered, "c")
@@ -1499,15 +1611,6 @@
     )(levels, momentum_new.reshape(2 * L, D, D), mlp_weights.reshape(2 * L, D, D), changes)
     mlp_new = mlp_new.reshape(mlp_weights.shape)
 
-    clipped = flat_piece * factor
-    first_new = BETA_FIRST * adam_m + (1.0 - BETA_FIRST) * clipped
-    second_new = BETA_SECOND * adam_v + (1.0 - BETA_SECOND) * clipped * clipped
-    count_value = float(STEP_NUM)
-    first_hat = first_new / (1.0 - BETA_FIRST**count_value)
-    second_hat = second_new / (1.0 - BETA_SECOND**count_value)
-    adam_new = adam_params - ADAM_RATE * (
-        first_hat / (jnp.sqrt(second_hat) + 1e-08) + DECAY_RATE * adam_params
-    )
     return (adam_new, first_new, second_new, mlp_new, momentum_new, loss_total, grad_norm)
 
 

time: 1010 us -> 942 us (0.933)
  local copies, waits for them, and re-layouts: 173 us -> 107 us
  Pallas kernels: 143 us -> 176 us
  starting transfers between devices: 165 us -> 146 us
    ppermute x34 -> x54, waiting for transfers between devices: 137 us -> 213 us  [swap(): return lax.ppermute(values, axis, [(0, 1), (1, 0)])]
    all_to_all x3, waiting for transfers between devices: 70.1 us -> 13 us  [to_items(): lax.all_to_all(packed, LAT_AXES, split_axis=0, concat_axis=0, tiled=True)]
    unnamed x456 -> x326, local copies, waits for them, and re-layouts: 83.3 us -> 38.5 us
    ppermute x12 -> x0, starting transfers between devices: 34.6 us -> none  [line_sum(): moving = lax.ppermute(value, Z_AXES, pairs)]
    pallas_call x31, Pallas kernels: 120 us -> 155 us  [launch(): pl.pallas_call(body, name=name, out_shape=out_shape, in_specs=in_specs, o...]
    ppermute x12 -> x0, waiting for transfers between devices: 24.1 us -> none  [line_sum(): moving = lax.ppermute(value, Z_AXES, pairs)]
    convert_element_type x18 -> x21, other arithmetic: 35.5 us -> 18.7 us  [add_low(): return sum((v.astype(jnp.float32) for v in values)).astype(NARROW)]
    another operation x19 -> x25, other arithmetic: 11.1 us -> 25 us  [the longest x9 13.5 us: gather_windows(): part = jnp.stack([part, swap(part, axis)])]
  transfers between devices with their start and end apart: 75 -> 82, of which waited for: 41 -> 43; matrix products, arithmetic and copies ran while one was open for 25% -> 23% of each run, Pallas kernels for 5% -> 4%
where the time goes in v3:
time: 942 us; the launch traced here: 929 us
  waiting for transfers between devices  327 us (35%)
  Pallas kernels  176 us (19%)
  starting transfers between devices  146 us (15%)
  local copies, waits for them, and re-layouts  107 us (11%)
  other arithmetic  91.6 us (10%)
  matrix products  57.3 us (6%)
  between operations  24.7 us (3%)
    ppermute x54, waiting for transfers between devices, swap(): return lax.ppermute(values, axis, [(0, 1), (1, 0)])  213 us
    pallas_call x31, Pallas kernels, launch(): pl.pallas_call(body, name=name, out_shape=out_shape, in_specs=in_specs, o...  155 us
    all_to_all x16, starting transfers between devices, exchange(): lax.all_to_all(values, ITEM_AXES, split_axis=0, concat_axis=0, tiled=True)  66.7 us
    all_to_all x16, waiting for transfers between devices, exchange(): lax.all_to_all(values, ITEM_AXES, split_axis=0, concat_axis=0, tiled=True)  59.2 us
    ppermute x54, starting transfers between devices, swap(): return lax.ppermute(values, axis, [(0, 1), (1, 0)])  47.8 us
    unnamed x326, local copies, waits for them, and re-layouts  38.5 us
    dot_general x14, matrix products, dot_tn(): lax.dot_general(left, right, (((0,), (0,)), ((), ())), preferred_element_...  36.7 us
    ppermute x3, waiting for transfers between devices, line_gather(): lax.ppermute(value, Z_AXES, [(i, i - 1) for i in range(1, 5 - step)])  23.8 us
  transfers between devices with their start and end apart: 82, of which 43 were waited for; matrix products, arithmetic and copies ran while one was open for 23% of the time, Pallas kernels for 4%

profile of v3, /device:TPU:0, one launch (start us, length us, event | category | flops | bytes accessed | tf_op | source)
XLA Modules:
  0.0 929.4 jit_solution(15303917058888413500)
XLA Ops:
  9.3 7.3 all-to-all-start
  25.3 6.3 narrow.2
  31.6 6.3 narrow.3
  37.9 11.1 %collective-permute-done = bf16[212,8,128]{2,1,0:T(8,128)(2,1)S(1)} collective-permute-done((bf16[212,8,128]{2,1,0:T(8,128)(2,1)S(1)}, bf16[212,8,128]{2,1,0:T(8,128)(2,1)S(1)}, u32[]{:S(2)}, u32[]{:S(2)}) %collective-permute-start) | collective-permute-done | bytes 434208 | tf_op jit(solution)/shard_map/ppermute | solution.py:1186
  62.4 8.7 collective-permute-done.10
  80.5 20.7 %collective-permute-done.11 = bf16[2,2,2,70,8,128]{5,4,3,2,1,0:T(8,128)(2,1)} collective-permute-done((bf16[2,2,2,70,8,128]{5,4,3,2,1,0:T(8,128)(2,1)}, bf16[2,2,2,70,8,128]{5,4,3,2,1,0:T(8,128)(2,1)}, u32[]{:S(2)}, u32[]{:S(2)}) %collective-permute-start.11) | collective-permute-done | bytes 1146912 | tf_op jit(solution)/shard_map/ppermute | solution.py:1186
  115.2 11.3 %collective-permute-done.14 = bf16[2,192,768]{2,1,0:T(8,128)(2,1)S(1)} collective-permute-done((bf16[2,192,768]{2,1,0:T(8,128)(2,1)S(1)}, bf16[2,192,768]{2,1,0:T(8,128)(2,1)S(1)}, u32[]{:S(2)}, u32[]{:S(2)}) %collective-permute-start.14) | collective-permute-done | bytes 589856 | tf_op jit(solution)/shard_map/ppermute | solution.py:1186
  130.6 5.3 all-to-all-start.6
  136.7 5.4 collective-permute-done.18
  142.1 13.6 %collective-permute-done.15 = bf16[2,2,192,768]{3,2,1,0:T(8,128)(2,1)} collective-permute-done((bf16[2,2,192,768]{3,2,1,0:T(8,128)(2,1)}, bf16[2,2,192,768]{3,2,1,0:T(8,128)(2,1)}, u32[]{:S(2)}, u32[]{:S(2)}) %collective-permute-start.15) | collective-permute-done | bytes 1179680 | tf_op jit(solution)/shard_map/ppermute | solution.py:1186
  180.5 7.9 all-to-all-done.1.refs_0_
  215.8 7.7 mlp.4
  223.5 13.0 %all-to-all-done.5 = bf16[8,36,1280]{2,1,0:T(8,128)(2,1)S(1)} async-done(((bf16[8,36,1280]{2,1,0:T(8,128)(2,1)}), bf16[8,36,1280]{2,1,0:T(8,128)(2,1)S(1)}, u32[]{:S(2)}, u32[]{:S(2)}) %all-to-all-start.5) | async-done | bytes 737312 | tf_op jit(solution)/shard_map/all_to_all | solution.py:1296
  242.8 5.6 all-to-all-done.3.refs_0_
  252.0 4.6 all-to-all-start.4
  272.9 8.5 mlp.5
  287.9 5.1 all-to-all-start.8
  311.4 5.2 all-to-all-done.9.refs_0_
  316.6 7.7 mlp.6
  347.4 5.0 all-to-all-done.11.refs_0_
  352.3 7.8 mlp.7
  369.0 9.2 mlp_back.4
  402.4 5.3 all-to-all-done.13.refs_0_
  410.4 9.2 mlp_back.5
  425.6 6.5 all-to-all-done.14.refs_0_
  437.4 4.7 all-to-all-start.15
  466.5 9.3 mlp_back.6
  513.1 5.5 all-to-all-start.17
  521.8 4.9 all-to-all-done.17.refs_0_
  529.4 9.3 mlp_back.7
  566.2 5.2 all-to-all-start.19
  588.6 6.5 pack.1
  604.1 31.3 %collective-permute-done.27 = bf16[2,2,1,2,128,768]{5,4,3,2,1,0:T(8,128)(2,1)} collective-permute-done((bf16[2,2,1,2,128,768]{5,4,3,2,1,0:T(8,128)(2,1)}, bf16[2,2,1,2,128,768]{5,4,3,2,1,0:T(8,128)(2,1)}, u32[]{:S(2)}, u32[]{:S(2)}) %collective-permute-start.27) | collective-permute-done | bytes 1572896 | tf_op jit(solution)/shard_map/ppermute | solution.py:1186
  651.3 9.8 %collective-permute-done.30 = bf16[2,2,1,1,128,768]{5,4,3,2,1,0:T(8,128)(2,1)S(1)} collective-permute-done((bf16[2,2,1,1,128,768]{5,4,3,2,1,0:T(8,128)(2,1)S(1)}, bf16[2,2,1,1,128,768]{5,4,3,2,1,0:T(8,128)(2,1)S(1)}, u32[]{:S(2)}, u32[]{:S(2)}) %collective-permute-start.30) | collective-permute-done | bytes 786464 | tf_op jit(solution)/shard_map/ppermute | solution.py:1186
  668.9 15.2 %collective-permute-done.40 = bf16[2,2,2,1,70,8,128]{6,5,4,3,2,1,0:T(8,128)(2,1)S(1)} collective-permute-done((bf16[2,2,2,1,70,8,128]{6,5,4,3,2,1,0:T(8,128)(2,1)S(1)}, bf16[2,2,2,1,70,8,128]{6,5,4,3,2,1,0:T(8,128)(2,1)S(1)}, u32[]{:S(2)}, u32[]{:S(2)}) %collective-permute-start.40) | collective-permute-done | bytes 1146912 | tf_op jit(solution)/shard_map/ppermute | solution.py:1186
  695.7 6.1 collective-permute-done.33
  704.4 7.1 collective-permute-done.41
  718.1 8.3 collective-permute-done.36
  740.4 26.4 %collective-permute-done.46 = bf16[212,8,128]{2,1,0:T(8,128)(2,1)} collective-permute-done((bf16[212,8,128]{2,1,0:T(8,128)(2,1)}, bf16[212,8,128]{2,1,0:T(8,128)(2,1)}, u32[]{:S(2)}, u32[]{:S(2)}) %collective-permute-start.46) | collective-permute-done | bytes 434208 | tf_op jit(solution)/shard_map/ppermute | solution.py:1186
  776.0 7.2 all-to-all-done.20
  784.6 4.8 fusion.14
  795.1 10.3 %collective-permute-done.48 = bf16[192,768]{1,0:T(8,128)(2,1)S(1)} collective-permute-done((bf16[192,768]{1,0:T(8,128)(2,1)S(1)}, bf16[192,768]{1,0:T(8,128)(2,1)S(1)}, u32[]{:S(2)}, u32[]{:S(2)}) %collective-permute-start.48) | collective-permute-done | bytes 294944 | tf_op jit(solution)/shard_map/ppermute | solution.py:1186
  807.6 6.7 collective-permute-done.49
  841.9 5.0 multiply_subtract_fusion
  848.2 7.1 collective-permute-done.53
  866.3 11.3 %multiply_add_fusion = f32[2,2,768,768]{3,2,1,0:T(8,128)} fusion(f32[2,2,768,768]{3,2,1,0:T(8,128)} %bitcast.365, f32[2,2,768,768]{3,2,1,0:T(8,128)} %param.23), kind=kLoop, calls=%fused_computation.1 | loop fusion | flops 4718592 | bytes 28311552 | tf_op jit(solution)/shard_map/add | solution.py:1582
  882.1 17.2 %collective-permute-done.58 = bf16[392,768]{1,0:T(8,128)(2,1)S(1)} collective-permute-done((bf16[392,768]{1,0:T(8,128)(2,1)S(1)}, bf16[392,768]{1,0:T(8,128)(2,1)S(1)}, u32[]{:S(2)}, u32[]{:S(2)}) %collective-permute-start.58) | collective-permute-done | bytes 602144 | tf_op jit(solution)/shard_map/ppermute | solution.py:1256
  911.7 8.4 muon.1
  (766 shorter events, 473.0 us)
Async XLA Ops:
  9.3 39.7 %all-to-all-start = ((bf16[8,18,1280]{2,1,0:T(8,128)(2,1)}), bf16[8,18,1280]{2,1,0:T(8,128)(2,1)}, u32[]{:S(2)}, u32[]{:S(2)}) async-start(bf16[8,18,1280]{2,1,0:T(8,128)(2,1)} %copy.142), calls=%async_computation | async-start | bytes 983040 | tf_op jit(solution)/shard_map/all_to_all | solution.py:1296
  21.9 27.1 %collective-permute-start = (bf16[212,8,128]{2,1,0:T(8,128)(2,1)S(1)}, bf16[212,8,128]{2,1,0:T(8,128)(2,1)S(1)}, u32[]{:S(2)}, u32[]{:S(2)}) collective-permute-start(bf16[212,8,128]{2,1,0:T(8,128)(2,1)S(1)} %fusion.35), channel_id=1, source_target_pairs={{0,16},{16,0},{1,17},{17,1},{2,18},{18,2},{3,19},{19,3},{4,20},{20... | collective-permute-start | bytes 1302536 | tf_op jit(solution)/shard_map/ppermute | solution.py:1186
  61.6 15.0 %collective-permute-start.6 = (bf16[2,2,70,8,128]{4,3,2,1,0:T(8,128)(2,1)S(1)}, bf16[2,2,70,8,128]{4,3,2,1,0:T(8,128)(2,1)S(1)}, u32[]{:S(2)}, u32[]{:S(2)}) collective-permute-start(bf16[2,2,70,8,128]{4,3,2,1,0:T(8,128)(2,1)S(1)} %get-tuple-element.283), channel_id=1, source_target_pairs={{0,8},{8,0},{1,9},{9,1},{2,10},{10,2},{3,11},{11,3},{4,12},{12,4},... | collective-permute-start | bytes 1720328 | tf_op jit(solution)/shard_map/ppermute | solution.py:1186
  72.8 28.5 %collective-permute-start.11 = (bf16[2,2,2,70,8,128]{5,4,3,2,1,0:T(8,128)(2,1)}, bf16[2,2,2,70,8,128]{5,4,3,2,1,0:T(8,128)(2,1)}, u32[]{:S(2)}, u32[]{:S(2)}) collective-permute-start(bf16[2,2,2,70,8,128]{5,4,3,2,1,0:T(8,128)(2,1)} %get-tuple-element.258), channel_id=1, source_target_pairs={{0,2},{2,0},{1,3},{3,1},{4,6},{6,4},{5,7},{7,5},{8,10},{10,8},{9,1... | collective-permute-start | bytes 3440648 | tf_op jit(solution)/shard_map/ppermute | solution.py:1186
  75.5 28.7 %collective-permute-start.3 = (bf16[2,2,2,72,8,128]{5,4,3,2,1,0:T(8,128)(2,1)}, bf16[2,2,2,72,8,128]{5,4,3,2,1,0:T(8,128)(2,1)}, u32[]{:S(2)}, u32[]{:S(2)}) collective-permute-start(bf16[2,2,2,72,8,128]{5,4,3,2,1,0:T(8,128)(2,1)} %get-tuple-element.256), channel_id=1, source_target_pairs={{0,8},{8,0},{1,9},{9,1},{2,10},{10,2},{3,11},{11,3},{4,12},{12,4},... | collective-permute-start | bytes 3538952 | tf_op jit(solution)/shard_map/ppermute | solution.py:1186
  78.2 29.5 %collective-permute-start.7 = (bf16[2,2,2,70,8,128]{5,4,3,2,1,0:T(8,128)(2,1)}, bf16[2,2,2,70,8,128]{5,4,3,2,1,0:T(8,128)(2,1)}, u32[]{:S(2)}, u32[]{:S(2)}) collective-permute-start(bf16[2,2,2,70,8,128]{5,4,3,2,1,0:T(8,128)(2,1)} %get-tuple-element.260), channel_id=1, source_target_pairs={{0,4},{4,0},{1,5},{5,1},{2,6},{6,2},{3,7},{7,3},{8,12},{12,8},{9,1... | collective-permute-start | bytes 3440648 | tf_op jit(solution)/shard_map/ppermute | solution.py:1186
  80.0 30.8 %collective-permute-start.13 = (bf16[2,192,768]{2,1,0:T(8,128)(2,1)S(1)}, bf16[2,192,768]{2,1,0:T(8,128)(2,1)S(1)}, u32[]{:S(2)}, u32[]{:S(2)}) collective-permute-start(bf16[2,192,768]{2,1,0:T(8,128)(2,1)S(1)} %dynamic-slice_bitcast_fusion), channel_id=1, source_target_pairs={{0,2},{2,0},{1,3},{3,1},{4,6},{6,4},{5,7},{7,5},{8,10},{10,8},{9,1... | collective-permute-start | bytes 1769480 | tf_op jit(solution)/shard_map/ppermute | solution.py:1186
  104.2 56.8 %collective-permute-start.12 = (bf16[2,2,2,2,70,8,128]{6,5,4,3,2,1,0:T(8,128)(2,1)}, bf16[2,2,2,2,70,8,128]{6,5,4,3,2,1,0:T(8,128)(2,1)}, u32[]{:S(2)}, u32[]{:S(2)}) collective-permute-start(bf16[2,2,2,2,70,8,128]{6,5,4,3,2,1,0:T(8,128)(2,1)} %pad_maximum_fusion.6.refs_5_), channel_id=1, source_target_pairs={{0,1},{1,0},{2,3},{3,2},{4,5},{5,4},{6,7},{7,6},{8,9},{9,8},{10,11... | collective-permute-start | bytes 6881288 | tf_op jit(solution)/shard_map/ppermute | solution.py:1186
  107.2 53.8 %collective-permute-start.4 = (bf16[2,2,2,2,72,8,128]{6,5,4,3,2,1,0:T(8,128)(2,1)}, bf16[2,2,2,2,72,8,128]{6,5,4,3,2,1,0:T(8,128)(2,1)}, u32[]{:S(2)}, u32[]{:S(2)}) collective-permute-start(bf16[2,2,2,2,72,8,128]{6,5,4,3,2,1,0:T(8,128)(2,1)} %pad_maximum_fusion.3.refs_1_), channel_id=1, source_target_pairs={{0,1},{1,0},{2,3},{3,2},{4,5},{5,4},{6,7},{7,6},{8,9},{9,8},{10,11... | collective-permute-start | bytes 7077896 | tf_op jit(solution)/shard_map/ppermute | solution.py:1186
  110.7 50.3 %collective-permute-start.8 = (bf16[2,2,2,2,70,8,128]{6,5,4,3,2,1,0:T(8,128)(2,1)}, bf16[2,2,2,2,70,8,128]{6,5,4,3,2,1,0:T(8,128)(2,1)}, u32[]{:S(2)}, u32[]{:S(2)}) collective-permute-start(bf16[2,2,2,2,70,8,128]{6,5,4,3,2,1,0:T(8,128)(2,1)} %pad_maximum_fusion.5.refs_3_), channel_id=1, source_target_pairs={{0,1},{1,0},{2,3},{3,2},{4,5},{5,4},{6,7},{7,6},{8,9},{9,8},{10,11... | collective-permute-start | bytes 6881288 | tf_op jit(solution)/shard_map/ppermute | solution.py:1186
  110.7 15.7 %collective-permute-start.14 = (bf16[2,192,768]{2,1,0:T(8,128)(2,1)S(1)}, bf16[2,192,768]{2,1,0:T(8,128)(2,1)S(1)}, u32[]{:S(2)}, u32[]{:S(2)}) collective-permute-start(bf16[2,192,768]{2,1,0:T(8,128)(2,1)S(1)} %collective-permute-done.13), channel_id=1, source_target_pairs={{0,4},{4,0},{1,5},{5,1},{2,6},{6,2},{3,7},{7,3},{8,12},{12,8},{9,1... | collective-permute-start | bytes 1769480 | tf_op jit(solution)/shard_map/ppermute | solution.py:1186
  113.6 28.5 %collective-permute-start.18 = (bf16[2,2,192,768]{3,2,1,0:T(8,128)(2,1)}, bf16[2,2,192,768]{3,2,1,0:T(8,128)(2,1)}, u32[]{:S(2)}, u32[]{:S(2)}) collective-permute-start(bf16[2,2,192,768]{3,2,1,0:T(8,128)(2,1)} %slice_bitcast_fusion), channel_id=1, source_target_pairs={{0,2},{2,0},{1,3},{3,1},{4,6},{6,4},{5,7},{7,5},{8,10},{10,8},{9,1... | collective-permute-start | bytes 3538952 | tf_op jit(solution)/shard_map/ppermute | solution.py:1186
  127.6 28.1 %collective-permute-start.15 = (bf16[2,2,192,768]{3,2,1,0:T(8,128)(2,1)}, bf16[2,2,192,768]{3,2,1,0:T(8,128)(2,1)}, u32[]{:S(2)}, u32[]{:S(2)}) collective-permute-start(bf16[2,2,192,768]{3,2,1,0:T(8,128)(2,1)} %get-tuple-element.254), channel_id=1, source_target_pairs={{0,8},{8,0},{1,9},{9,1},{2,10},{10,2},{3,11},{11,3},{4,12},{12,4},... | collective-permute-start | bytes 3538952 | tf_op jit(solution)/shard_map/ppermute | solution.py:1186
  130.6 46.0 %all-to-all-start.6 = ((f32[8,1,18]{2,1,0:T(1,128)}), f32[8,1,18]{2,1,0:T(1,128)S(1)}, u32[]{:S(2)}, u32[]{:S(2)}) async-start(f32[8,1,18]{2,1,0:T(1,128)} %copy.155), calls=%async_computation.6 | async-start | bytes 8192 | tf_op jit(solution)/shard_map/all_to_all | solution.py:1296
  142.1 73.7 %collective-permute-start.16 = (bf16[2,2,2,192,768]{4,3,2,1,0:T(8,128)(2,1)}, bf16[2,2,2,192,768]{4,3,2,1,0:T(8,128)(2,1)}, u32[]{:S(2)}, u32[]{:S(2)}) collective-permute-start(bf16[2,2,2,192,768]{4,3,2,1,0:T(8,128)(2,1)} %narrow.2), channel_id=1, source_target_pairs={{0,1},{1,0},{2,3},{3,2},{4,5},{5,4},{6,7},{7,6},{8,9},{9,8},{10,11... | collective-permute-start | bytes 7077896 | tf_op jit(solution)/shard_map/ppermute | solution.py:1186
  155.7 52.0 %collective-permute-start.19 = (bf16[2,2,192,768]{3,2,1,0:T(8,128)(2,1)}, bf16[2,2,192,768]{3,2,1,0:T(8,128)(2,1)}, u32[]{:S(2)}, u32[]{:S(2)}) collective-permute-start(bf16[2,2,192,768]{3,2,1,0:T(8,128)(2,1)} %collective-permute-done.18), channel_id=1, source_target_pairs={{0,4},{4,0},{1,5},{5,1},{2,6},{6,2},{3,7},{7,3},{8,12},{12,8},{9,1... | collective-permute-start | bytes 3538952 | tf_op jit(solution)/shard_map/ppermute | solution.py:1186
  161.0 54.8 %collective-permute-start.17 = (bf16[2,2,2,192,768]{4,3,2,1,0:T(8,128)(2,1)}, bf16[2,2,2,192,768]{4,3,2,1,0:T(8,128)(2,1)}, u32[]{:S(2)}, u32[]{:S(2)}) collective-permute-start(bf16[2,2,2,192,768]{4,3,2,1,0:T(8,128)(2,1)} %maximum_select_fusion), channel_id=1, source_target_pairs={{0,1},{1,0},{2,3},{3,2},{4,5},{5,4},{6,7},{7,6},{8,9},{9,8},{10,11... | collective-permute-start | bytes 7077896 | tf_op jit(solution)/shard_map/ppermute | solution.py:1186
  207.4 65.4 %collective-permute-start.20 = (bf16[2,2,2,192,768]{4,3,2,1,0:T(8,128)(2,1)}, bf16[2,2,2,192,768]{4,3,2,1,0:T(8,128)(2,1)}, u32[]{:S(2)}, u32[]{:S(2)}) collective-permute-start(bf16[2,2,2,192,768]{4,3,2,1,0:T(8,128)(2,1)} %narrow.3), channel_id=1, source_target_pairs={{0,1},{1,0},{2,3},{3,2},{4,5},{5,4},{6,7},{7,6},{8,9},{9,8},{10,11... | collective-permute-start | bytes 7077896 | tf_op jit(solution)/shard_map/ppermute | solution.py:1186
  211.0 58.4 %collective-permute-start.21 = (bf16[2,2,2,192,768]{4,3,2,0,1:T(8,128)(2,1)}, bf16[2,2,2,192,768]{4,3,2,0,1:T(8,128)(2,1)}, u32[]{:S(2)}, u32[]{:S(2)}) collective-permute-start(bf16[2,2,2,192,768]{4,3,2,0,1:T(8,128)(2,1)} %pad_maximum_fusion.4), channel_id=1, source_target_pairs={{0,1},{1,0},{2,3},{3,2},{4,5},{5,4},{6,7},{7,6},{8,9},{9,8},{10,11... | collective-permute-start | bytes 7077896 | tf_op jit(solution)/shard_map/ppermute | solution.py:1186
  211.3 25.2 %all-to-all-start.5 = ((bf16[8,36,1280]{2,1,0:T(8,128)(2,1)}), bf16[8,36,1280]{2,1,0:T(8,128)(2,1)S(1)}, u32[]{:S(2)}, u32[]{:S(2)}) async-start(bf16[8,36,1280]{2,1,0:T(8,128)(2,1)} %copy.150), calls=%async_computation.5 | async-start | bytes 1638400 | tf_op jit(solution)/shard_map/all_to_all | solution.py:1296
  252.0 20.8 %all-to-all-start.4 = ((bf16[16,72,128]{2,1,0:T(8,128)(2,1)}), bf16[16,72,128]{2,1,0:T(8,128)(2,1)}, u32[]{:S(2)}, u32[]{:S(2)}) async-start(bf16[16,72,128]{2,1,0:T(8,128)(2,1)} %get-tuple-element.129), calls=%async_computation.4 | async-start | bytes 589824 | tf_op jit(solution)/shard_map/all_to_all | solution.py:932
  479.9 19.8 %collective-permute-start.22 = (bf16[1536,768]{1,0:T(8,128)(2,1)}, bf16[1536,768]{1,0:T(8,128)(2,1)}, u32[]{:S(2)}, u32[]{:S(2)}) collective-permute-start(bf16[1536,768]{1,0:T(8,128)(2,1)} %convolution_convert_fusion.9), channel_id=1, source_target_pairs={{0,1},{1,0},{2,3},{3,2},{4,5},{5,4},{6,7},{7,6},{8,9},{9,8},{10,11... | collective-permute-start | bytes 7077896 | tf_op jit(solution)/shard_map/ppermute | solution.py:1186
  482.8 20.1 %collective-permute-start.23 = (bf16[1536,768]{1,0:T(8,128)(2,1)}, bf16[1536,768]{1,0:T(8,128)(2,1)}, u32[]{:S(2)}, u32[]{:S(2)}) collective-permute-start(bf16[1536,768]{1,0:T(8,128)(2,1)} %convolution_convert_fusion.8), channel_id=1, source_target_pairs={{0,1},{1,0},{2,3},{3,2},{4,5},{5,4},{6,7},{7,6},{8,9},{9,8},{10,11... | collective-permute-start | bytes 7077896 | tf_op jit(solution)/shard_map/ppermute | solution.py:1186
  483.3 25.3 %all-to-all-start.16 = ((bf16[16,72,128]{2,1,0:T(8,128)(2,1)}), bf16[16,72,128]{2,1,0:T(8,128)(2,1)S(1)}, u32[]{:S(2)}, u32[]{:S(2)}) async-start(bf16[16,72,128]{2,1,0:T(8,128)(2,1)} %get-tuple-element.169), calls=%async_computation.16 | async-start | bytes 589824 | tf_op jit(solution)/shard_map/all_to_all | solution.py:932
  571.4 267.1 %all-gather.2.cloned.1.call-start = ((), (), s32[]{:S(2)}) async-start(), calls=%async_computation.21 | async-start | bytes 5308416 | tf_op jit(solution)/shard_map/all_gather | solution.py:1552
  595.1 45.4 %collective-permute-start.29 = (bf16[2,2,2,2,212,8,128]{6,5,4,3,2,1,0:T(8,128)(2,1)}, bf16[2,2,2,2,212,8,128]{6,5,4,3,2,1,0:T(8,128)(2,1)}, u32[]{:S(2)}, u32[]{:S(2)}) collective-permute-start(bf16[2,2,2,2,212,8,128]{6,5,4,3,2,1,0:T(8,128)(2,1)} %get-tuple-element.222), channel_id=1, source_target_pairs={{0,1},{1,0},{2,3},{3,2},{4,5},{5,4},{6,7},{7,6},{8,9},{9,8},{10,11... | collective-permute-start | bytes 20840456 | tf_op jit(solution)/shard_map/ppermute | solution.py:1186
  596.7 43.3 %collective-permute-start.28 = (bf16[2,1,2,2,128,768]{5,4,3,2,1,0:T(8,128)(2,1)}, bf16[2,1,2,2,128,768]{5,4,3,2,1,0:T(8,128)(2,1)S(1)}, u32[]{:S(2)}, u32[]{:S(2)}) collective-permute-start(bf16[2,1,2,2,128,768]{5,4,3,2,1,0:T(8,128)(2,1)} %fusion.10), channel_id=1, source_target_pairs={{0,8},{8,0},{1,9},{9,1},{2,10},{10,2},{3,11},{11,3},{4,12},{12,4},... | collective-permute-start | bytes 4718600 | tf_op jit(solution)/shard_map/ppermute | solution.py:1186
  598.6 36.8 %collective-permute-start.27 = (bf16[2,2,1,2,128,768]{5,4,3,2,1,0:T(8,128)(2,1)}, bf16[2,2,1,2,128,768]{5,4,3,2,1,0:T(8,128)(2,1)}, u32[]{:S(2)}, u32[]{:S(2)}) collective-permute-start(bf16[2,2,1,2,128,768]{5,4,3,2,1,0:T(8,128)(2,1)} %pad_maximum_fusion.7), channel_id=1, source_target_pairs={{0,2},{2,0},{1,3},{3,1},{4,6},{6,4},{5,7},{7,5},{8,10},{10,8},{9,1... | collective-permute-start | bytes 4718600 | tf_op jit(solution)/shard_map/ppermute | solution.py:1186
  601.2 36.6 %collective-permute-start.26 = (bf16[2,2,2,1,128,768]{5,4,3,2,1,0:T(8,128)(2,1)}, bf16[2,2,2,1,128,768]{5,4,3,2,1,0:T(8,128)(2,1)}, u32[]{:S(2)}, u32[]{:S(2)}) collective-permute-start(bf16[2,2,2,1,128,768]{5,4,3,2,1,0:T(8,128)(2,1)} %pad_maximum_fusion.8), channel_id=1, source_target_pairs={{0,4},{4,0},{1,5},{5,1},{2,6},{6,2},{3,7},{7,3},{8,12},{12,8},{9,1... | collective-permute-start | bytes 4718600 | tf_op jit(solution)/shard_map/ppermute | solution.py:1186
  640.5 20.5 %collective-permute-start.30 = (bf16[2,2,1,1,128,768]{5,4,3,2,1,0:T(8,128)(2,1)S(1)}, bf16[2,2,1,1,128,768]{5,4,3,2,1,0:T(8,128)(2,1)S(1)}, u32[]{:S(2)}, u32[]{:S(2)}) collective-permute-start(bf16[2,2,1,1,128,768]{5,4,3,2,1,0:T(8,128)(2,1)S(1)} %slice.552), channel_id=1, source_target_pairs={{0,2},{2,0},{1,3},{3,1},{4,6},{6,4},{5,7},{7,5},{8,10},{10,8},{9,1... | collective-permute-start | bytes 2359304 | tf_op jit(solution)/shard_map/ppermute | solution.py:1186
  641.9 20.9 %collective-permute-start.32 = (bf16[2,1,1,2,128,768]{5,4,3,2,1,0:T(8,128)(2,1)S(1)}, bf16[2,1,1,2,128,768]{5,4,3,2,1,0:T(8,128)(2,1)S(1)}, u32[]{:S(2)}, u32[]{:S(2)}) collective-permute-start(bf16[2,1,1,2,128,768]{5,4,3,2,1,0:T(8,128)(2,1)S(1)} %constant_dynamic-slice_fusion.1), channel_id=1, source_target_pairs={{0,8},{8,0},{1,9},{9,1},{2,10},{10,2},{3,11},{11,3},{4,12},{12,4},... | collective-permute-start | bytes 2359304 | tf_op jit(solution)/shard_map/ppermute | solution.py:1186
  646.0 38.0 %collective-permute-start.40 = (bf16[2,2,2,1,70,8,128]{6,5,4,3,2,1,0:T(8,128)(2,1)S(1)}, bf16[2,2,2,1,70,8,128]{6,5,4,3,2,1,0:T(8,128)(2,1)S(1)}, u32[]{:S(2)}, u32[]{:S(2)}) collective-permute-start(bf16[2,2,2,1,70,8,128]{6,5,4,3,2,1,0:T(8,128)(2,1)S(1)} %add_convert_fusion.12), channel_id=1, source_target_pairs={{0,2},{2,0},{1,3},{3,1},{4,6},{6,4},{5,7},{7,5},{8,10},{10,8},{9,1... | collective-permute-start | bytes 3440648 | tf_op jit(solution)/shard_map/ppermute | solution.py:1186
  647.6 20.5 %collective-permute-start.34 = (bf16[2,1,2,1,128,768]{5,4,3,2,1,0:T(8,128)(2,1)S(1)}, bf16[2,1,2,1,128,768]{5,4,3,2,1,0:T(8,128)(2,1)S(1)}, u32[]{:S(2)}, u32[]{:S(2)}) collective-permute-start(bf16[2,1,2,1,128,768]{5,4,3,2,1,0:T(8,128)(2,1)S(1)} %slice.556), channel_id=1, source_target_pairs={{0,4},{4,0},{1,5},{5,1},{2,6},{6,2},{3,7},{7,3},{8,12},{12,8},{9,1... | collective-permute-start | bytes 2359304 | tf_op jit(solution)/shard_map/ppermute | solution.py:1186
  649.7 43.6 %collective-permute-start.37 = (bf16[2,2,1,2,72,8,128]{6,5,4,3,2,1,0:T(8,128)(2,1)S(1)}, bf16[2,2,1,2,72,8,128]{6,5,4,3,2,1,0:T(8,128)(2,1)S(1)}, u32[]{:S(2)}, u32[]{:S(2)}) collective-permute-start(bf16[2,2,1,2,72,8,128]{6,5,4,3,2,1,0:T(8,128)(2,1)S(1)} %add_convert_fusion.8), channel_id=1, source_target_pairs={{0,4},{4,0},{1,5},{5,1},{2,6},{6,2},{3,7},{7,3},{8,12},{12,8},{9,1... | collective-permute-start | bytes 3538952 | tf_op jit(solution)/shard_map/ppermute | solution.py:1186
  661.1 28.2 %collective-permute-start.43 = (bf16[2,1,2,2,70,8,128]{6,5,4,3,2,1,0:T(8,128)(2,1)S(1)}, bf16[2,1,2,2,70,8,128]{6,5,4,3,2,1,0:T(8,128)(2,1)S(1)}, u32[]{:S(2)}, u32[]{:S(2)}) collective-permute-start(bf16[2,1,2,2,70,8,128]{6,5,4,3,2,1,0:T(8,128)(2,1)S(1)} %add_convert_fusion.10), channel_id=1, source_target_pairs={{0,8},{8,0},{1,9},{9,1},{2,10},{10,2},{3,11},{11,3},{4,12},{12,4},... | collective-permute-start | bytes 3440648 | tf_op jit(solution)/shard_map/ppermute | solution.py:1186
  662.8 39.8 %collective-permute-start.31 = (bf16[2,1,1,1,128,768]{5,4,3,2,1,0:T(8,128)(2,1)S(1)}, bf16[2,1,1,1,128,768]{5,4,3,2,1,0:T(8,128)(2,1)S(1)}, u32[]{:S(2)}, u32[]{:S(2)}) collective-permute-start(bf16[2,1,1,1,128,768]{5,4,3,2,1,0:T(8,128)(2,1)S(1)} %constant_dynamic-slice_fusion.2), channel_id=1, source_target_pairs={{0,8},{8,0},{1,9},{9,1},{2,10},{10,2},{3,11},{11,3},{4,12},{12,4},... | collective-permute-start | bytes 1179656 | tf_op jit(solution)/shard_map/ppermute | solution.py:1186
  668.1 33.7 %collective-permute-start.33 = (bf16[2,1,1,1,128,768]{5,4,3,2,1,0:T(8,128)(2,1)S(1)}, bf16[2,1,1,1,128,768]{5,4,3,2,1,0:T(8,128)(2,1)S(1)}, u32[]{:S(2)}, u32[]{:S(2)}) collective-permute-start(bf16[2,1,1,1,128,768]{5,4,3,2,1,0:T(8,128)(2,1)S(1)} %slice.640), channel_id=1, source_target_pairs={{0,4},{4,0},{1,5},{5,1},{2,6},{6,2},{3,7},{7,3},{8,12},{12,8},{9,1... | collective-permute-start | bytes 1179656 | tf_op jit(solution)/shard_map/ppermute | solution.py:1186
  684.0 18.5 %collective-permute-start.35 = (bf16[2,1,1,1,128,768]{5,4,3,2,1,0:T(8,128)(2,1)S(1)}, bf16[2,1,1,1,128,768]{5,4,3,2,1,0:T(8,128)(2,1)S(1)}, u32[]{:S(2)}, u32[]{:S(2)}) collective-permute-start(bf16[2,1,1,1,128,768]{5,4,3,2,1,0:T(8,128)(2,1)S(1)} %slice.642), channel_id=1, source_target_pairs={{0,2},{2,0},{1,3},{3,1},{4,6},{6,4},{5,7},{7,5},{8,10},{10,8},{9,1... | collective-permute-start | bytes 1179656 | tf_op jit(solution)/shard_map/ppermute | solution.py:1186
  689.3 22.3 %collective-permute-start.41 = (bf16[2,1,2,1,70,8,128]{6,5,4,3,2,1,0:T(8,128)(2,1)S(1)}, bf16[2,1,2,1,70,8,128]{6,5,4,3,2,1,0:T(8,128)(2,1)S(1)}, u32[]{:S(2)}, u32[]{:S(2)}) collective-permute-start(bf16[2,1,2,1,70,8,128]{6,5,4,3,2,1,0:T(8,128)(2,1)S(1)} %slice.650), channel_id=1, source_target_pairs={{0,8},{8,0},{1,9},{9,1},{2,10},{10,2},{3,11},{11,3},{4,12},{12,4},... | collective-permute-start | bytes 1720328 | tf_op jit(solution)/shard_map/ppermute | solution.py:1186
  693.4 20.7 %collective-permute-start.44 = (bf16[2,1,1,2,70,8,128]{6,5,4,3,2,1,0:T(8,128)(2,1)S(1)}, bf16[2,1,1,2,70,8,128]{6,5,4,3,2,1,0:T(8,128)(2,1)S(1)}, u32[]{:S(2)}, u32[]{:S(2)}) collective-permute-start(bf16[2,1,1,2,70,8,128]{6,5,4,3,2,1,0:T(8,128)(2,1)S(1)} %slice.654), channel_id=1, source_target_pairs={{0,4},{4,0},{1,5},{5,1},{2,6},{6,2},{3,7},{7,3},{8,12},{12,8},{9,1... | collective-permute-start | bytes 1720328 | tf_op jit(solution)/shard_map/ppermute | solution.py:1186
  702.9 23.6 %collective-permute-start.36 = (bf16[384,768]{1,0:T(8,128)(2,1)S(1)}, bf16[384,768]{1,0:T(8,128)(2,1)S(1)}, u32[]{:S(2)}, u32[]{:S(2)}) collective-permute-start(bf16[384,768]{1,0:T(8,128)(2,1)S(1)} %select_bitcast_fusion), channel_id=1, source_target_pairs={{0,16},{16,0},{1,17},{17,1},{2,18},{18,2},{3,19},{19,3},{4,20},{20... | collective-permute-start | bytes 1769480 | tf_op jit(solution)/shard_map/ppermute | solution.py:1186
  712.4 15.1 %collective-permute-start.42 = (bf16[2,1,1,1,70,8,128]{6,5,4,3,2,1,0:T(8,128)(2,1)}, bf16[2,1,1,1,70,8,128]{6,5,4,3,2,1,0:T(8,128)(2,1)}, u32[]{:S(2)}, u32[]{:S(2)}) collective-permute-start(bf16[2,1,1,1,70,8,128]{6,5,4,3,2,1,0:T(8,128)(2,1)} %slice.652), channel_id=1, source_target_pairs={{0,4},{4,0},{1,5},{5,1},{2,6},{6,2},{3,7},{7,3},{8,12},{12,8},{9,1... | collective-permute-start | bytes 860168 | tf_op jit(solution)/shard_map/ppermute | solution.py:1186
  730.8 36.0 %collective-permute-start.46 = (bf16[212,8,128]{2,1,0:T(8,128)(2,1)}, bf16[212,8,128]{2,1,0:T(8,128)(2,1)}, u32[]{:S(2)}, u32[]{:S(2)}) collective-permute-start(bf16[212,8,128]{2,1,0:T(8,128)(2,1)} %slice_bitcast_fusion.1), channel_id=1, source_target_pairs={{0,16},{16,0},{1,17},{17,1},{2,18},{18,2},{3,19},{19,3},{4,20},{20... | collective-permute-start | bytes 1302536 | tf_op jit(solution)/shard_map/ppermute | solution.py:1186
  838.4 16.8 %collective-permute-start.53 = (bf16[392,768]{1,0:T(8,128)(2,1)}, bf16[392,768]{1,0:T(8,128)(2,1)S(1)}, u32[]{:S(2)}, u32[]{:S(2)}) collective-permute-start(bf16[392,768]{1,0:T(8,128)(2,1)} %pad_maximum_fusion.17), channel_id=1, source_target_pairs={{0,8},{8,16},{16,24},{1,9},{9,17},{17,25},{2,10},{10,18},{18,26},{... | collective-permute-start | bytes 1806344 | tf_op jit(solution)/shard_map/ppermute | solution.py:1252
  846.9 17.2 %collective-permute-start.56 = (bf16[392,768]{1,0:T(8,128)(2,1)S(1)}, bf16[392,768]{1,0:T(8,128)(2,1)S(1)}, u32[]{:S(2)}, u32[]{:S(2)}) collective-permute-start(bf16[392,768]{1,0:T(8,128)(2,1)S(1)} %copy-done.70), channel_id=1, source_target_pairs={{8,0},{16,8},{24,16},{9,1},{17,9},{25,17},{10,2},{18,10},{26,18},{... | collective-permute-start | bytes 1806344 | tf_op jit(solution)/shard_map/ppermute | solution.py:1256
  864.1 16.4 %collective-permute-start.57 = (bf16[392,768]{1,0:T(8,128)(2,1)S(1)}, bf16[392,768]{1,0:T(8,128)(2,1)S(1)}, u32[]{:S(2)}, u32[]{:S(2)}) collective-permute-start(bf16[392,768]{1,0:T(8,128)(2,1)S(1)} %collective-permute-done.56), channel_id=1, source_target_pairs={{8,0},{16,8},{9,1},{17,9},{10,2},{18,10},{11,3},{19,11},{12,4},{20... | collective-permute-start | bytes 1806344 | tf_op jit(solution)/shard_map/ppermute | solution.py:1256
  865.4 16.3 %collective-permute-start.55 = (bf16[392,768]{1,0:T(8,128)(2,1)S(1)}, bf16[392,768]{1,0:T(8,128)(2,1)S(1)}, u32[]{:S(2)}, u32[]{:S(2)}) collective-permute-start(bf16[392,768]{1,0:T(8,128)(2,1)S(1)} %collective-permute-done.54), channel_id=1, source_target_pairs={{16,24},{17,25},{18,26},{19,27},{20,28},{21,29},{22,30},{23,31}} | collective-permute-start | bytes 1806344 | tf_op jit(solution)/shard_map/ppermute | solution.py:1252
  880.5 18.8 %collective-permute-start.58 = (bf16[392,768]{1,0:T(8,128)(2,1)S(1)}, bf16[392,768]{1,0:T(8,128)(2,1)S(1)}, u32[]{:S(2)}, u32[]{:S(2)}) collective-permute-start(bf16[392,768]{1,0:T(8,128)(2,1)S(1)} %collective-permute-done.57), channel_id=1, source_target_pairs={{8,0},{9,1},{10,2},{11,3},{12,4},{13,5},{14,6},{15,7}} | collective-permute-start | bytes 1806344 | tf_op jit(solution)/shard_map/ppermute | solution.py:1256
  (186 other events, 2589.2 us)
Sparse Core Ops, SparseCore 0:
  727.7 91.1 all-gather.1

commit v4 on v3

--- a/solution.py
+++ b/solution.py
@@ -1304,20 +1304,24 @@
     quarters = [own_quarters(mlp_weights, depth, x[None]) for depth in range(L)]
     windows, source, *quarters = gather_windows(own, source, *quarters)
     own_mask = own_window(jnp.ones((width,), jnp.float32), device, width, total, devices)
-    mlp_low = []
-    for depth, own in enumerate(quarters):
-        if depth % 2 == 0:
-            first = swap(lax.dynamic_index_in_dim(own[:, 0], zl, 1, keepdims=False), "y")
-            both = jnp.stack([first, swap(first, "x")], axis=1)
-            others = swap(both, "zl")
-            across_y = jnp.where(
-                zl == 0, jnp.stack([both, others], axis=2), jnp.stack([others, both], axis=2)
-            )
-        else:
-            first = swap(own[:, 0], "y")
-            across_y = jnp.stack([first, swap(first, "x")], axis=1)
-        four = (own, across_y, swap(own, "c"), swap(across_y, "c"))
-        mlp_low.append([chunk.reshape(2, D, D) for chunk in four])
+    first = swap(lax.dynamic_index_in_dim(quarters[0][:, 0], zl, 1, keepdims=False), "y")
+    second = swap(first, "x")
+    others = swap(jnp.stack([first, second], axis=1), "zl")
+    third = swap(quarters[1][:, 0], "y")
+    coming = (first, second, others, third, swap(third, "x"))
+
+    def feed_forward(coming):
+        first, second, others, third, fourth = coming
+        both = jnp.stack([first, second], axis=1)
+        across = (
+            jnp.where(zl == 0, jnp.stack([both, others], axis=2), jnp.stack([others, both], axis=2)),
+            jnp.stack([third, fourth], axis=1),
+        )
+        return [
+            [chunk.reshape(2, D, D) for chunk in (own, far, swap(own, "c"), swap(far, "c"))]
+            for own, far in zip(quarters, across)
+        ]
+
     wanted = to_items(targets)
     row_weight = jnp.sin(math.pi * (lat_rows.astype(jnp.float32) + 0.5) / ROWS)
     weight_local = row_weight[None, :, None] * mask.astype(jnp.float32)
@@ -1369,6 +1373,8 @@
             embed_kernel, "embed", [state_f32, payload],
             [current, shifts, embed_b, norms[0], spread, row_fwd, embed_w], going=(0,),
         )
+        if roll_idx == 0:
+            sent, wanted = lax.optimization_barrier((sent, wanted))
         layers = []
         for depth in range(L):
             got = exchange(sent)
@@ -1377,6 +1383,9 @@
                 [got, col_fwd, col_back, pair_w[depth], pair_b[depth]], scratch=(wide, wide),
                 going=(1,),
             )
+            if roll_idx == 0 and depth == 0:
+                unused, coming = lax.optimization_barrier((out, coming))
+                mlp_low = feed_forward(coming)
             got = exchange(out)
             has_next = depth + 1 < L
             outs = [state_f32, ((TOK, D), NARROW), ((TOK, FF), f32), ((TOK, FF), NARROW), state_f32]

time: 942 us -> 926 us (0.983)
  local copies, waits for them, and re-layouts: 107 us -> 95.8 us
    all_to_all x16, waiting for transfers between devices: 59.2 us -> 76.7 us  [exchange(): lax.all_to_all(values, ITEM_AXES, split_axis=0, concat_axis=0, tiled=True)]
    unnamed x326 -> x330, local copies, waits for them, and re-layouts: 38.5 us -> 35.8 us
  transfers between devices with their start and end apart: 82 -> 82, of which waited for: 43 -> 46; matrix products, arithmetic and copies ran while one was open for 23% -> 22% of each run, Pallas kernels for 4% -> 5%
where the time goes in v4:
time: 926 us; the launch traced here: 917 us
  waiting for transfers between devices  326 us (35%)
  Pallas kernels  175 us (19%)
  starting transfers between devices  152 us (16%)
  local copies, waits for them, and re-layouts  95.8 us (10%)
  other arithmetic  86.2 us (9%)
  matrix products  57.3 us (6%)
  between operations  24.8 us (3%)
    ppermute x54, waiting for transfers between devices, swap(): return lax.ppermute(values, axis, [(0, 1), (1, 0)])  207 us
    pallas_call x31, Pallas kernels, launch(): pl.pallas_call(body, name=name, out_shape=out_shape, in_specs=in_specs, o...  154 us
    all_to_all x16, waiting for transfers between devices, exchange(): lax.all_to_all(values, ITEM_AXES, split_axis=0, concat_axis=0, tiled=True)  76.7 us
    all_to_all x16, starting transfers between devices, exchange(): lax.all_to_all(values, ITEM_AXES, split_axis=0, concat_axis=0, tiled=True)  67.5 us
    ppermute x54, starting transfers between devices, swap(): return lax.ppermute(values, axis, [(0, 1), (1, 0)])  45.9 us
    dot_general x14, matrix products, dot_tn(): lax.dot_general(left, right, (((0,), (0,)), ((), ())), preferred_element_...  36.7 us
    unnamed x330, local copies, waits for them, and re-layouts  35.8 us
    ppermute x3, waiting for transfers between devices, line_gather(): lax.ppermute(value, Z_AXES, [(i, i - 1) for i in range(1, 5 - step)])  23.6 us
  transfers between devices with their start and end apart: 82, of which 46 were waited for; matrix products, arithmetic and copies ran while one was open for 22% of the time, Pallas kernels for 5%

profile of v4, /device:TPU:0, one launch (start us, length us, event | category | flops | bytes accessed | tf_op | source)
XLA Modules:
  0.0 916.5 jit_solution(7640080359688118927)
XLA Ops:
  9.3 7.3 all-to-all-start
  25.3 6.3 narrow.2
  31.6 6.3 narrow.3
  37.9 11.1 %collective-permute-done = bf16[212,8,128]{2,1,0:T(8,128)(2,1)S(1)} collective-permute-done((bf16[212,8,128]{2,1,0:T(8,128)(2,1)S(1)}, bf16[212,8,128]{2,1,0:T(8,128)(2,1)S(1)}, u32[]{:S(2)}, u32[]{:S(2)}) %collective-permute-start) | collective-permute-done | bytes 434208 | tf_op jit(solution)/shard_map/ppermute | solution.py:1186
  62.4 8.7 collective-permute-done.10
  76.3 21.4 %collective-permute-done.11 = bf16[2,2,2,70,8,128]{5,4,3,2,1,0:T(8,128)(2,1)S(1)} collective-permute-done((bf16[2,2,2,70,8,128]{5,4,3,2,1,0:T(8,128)(2,1)S(1)}, bf16[2,2,2,70,8,128]{5,4,3,2,1,0:T(8,128)(2,1)S(1)}, u32[]{:S(2)}, u32[]{:S(2)}) %collective-permute-start.11) | collective-permute-done | bytes 1146912 | tf_op jit(solution)/shard_map/ppermute | solution.py:1186
  104.6 5.8 all-to-all-start.1
  114.3 12.6 %collective-permute-done.13 = bf16[2,192,768]{2,1,0:T(8,128)(2,1)S(1)} collective-permute-done((bf16[2,192,768]{2,1,0:T(8,128)(2,1)S(1)}, bf16[2,192,768]{2,1,0:T(8,128)(2,1)S(1)}, u32[]{:S(2)}, u32[]{:S(2)}) %collective-permute-start.13) | collective-permute-done | bytes 589856 | tf_op jit(solution)/shard_map/ppermute | solution.py:1186
  133.0 7.2 collective-permute-done.14
  142.4 8.6 collective-permute-done.16
  171.1 12.3 %all-to-all-done.2.refs_0_ = bf16[16,72,128]{2,1,0:T(8,128)(2,1)S(1)} async-done(((bf16[16,72,128]{2,1,0:T(8,128)(2,1)}), bf16[16,72,128]{2,1,0:T(8,128)(2,1)S(1)}, u32[]{:S(2)}, u32[]{:S(2)}) %all-to-all-start.2) | async-done | bytes 294944 | tf_op jit(solution)/shard_map/all_to_all | solution.py:932
  208.6 7.8 all-to-all-done.3.refs_0_
  220.0 7.7 mlp.4
  227.7 5.2 all-to-all-start.4
  234.5 6.5 all-to-all-done.4.refs_0_
  263.7 8.5 mlp.5
  278.8 5.3 all-to-all-start.8
  286.3 5.9 all-to-all-done.8.refs_0_
  301.3 6.3 all-to-all-done.9.refs_0_
  307.6 7.7 mlp.6
  321.8 5.3 all-to-all-done.10.refs_0_
  336.9 5.6 all-to-all-done.11.refs_0_
  342.6 6.9 mlp.7
  358.4 9.2 %mlp_back.4 = (bf16[144,768]{1,0:T(8,128)(2,1)}, bf16[144,3072]{1,0:T(8,128)(2,1)}, f32[144,768]{1,0:T(8,128)}, f32[1,3072]{1,0:T(1,128)S(1)}, f32[3,768]{1,0:T(4,128)S(1)}, /*index=5*/bf16[16,72,128]{2,1,0:T(8,128)(2,1)}) custom-call(f32[144,768]{1,0:T(8,128)S(1)} %get-tuple-element.156.refs_0_, f32[144,3072]{1,0:T(8,128)} %get-tuple-element.157.refs_1_, ...), custom_call_target="tpu_custom_call" | custom-call | tf_op jit(solution)/shard_map/mlp_back/pallas_call | solution.py:920
  391.7 5.3 all-to-all-done.13.refs_0_
  399.7 9.2 %mlp_back.5 = (bf16[144,768]{1,0:T(8,128)(2,1)}, bf16[144,3072]{1,0:T(8,128)(2,1)}, f32[144,768]{1,0:T(8,128)}, f32[1,3072]{1,0:T(1,128)S(1)}, f32[3,768]{1,0:T(4,128)S(1)}, /*index=5*/bf16[16,72,128]{2,1,0:T(8,128)(2,1)}) custom-call(f32[144,768]{1,0:T(8,128)S(1)} %get-tuple-element.164.refs_0_, f32[144,3072]{1,0:T(8,128)} %get-tuple-element.165.refs_1_, ...), custom_call_target="tpu_custom_call" | custom-call | tf_op jit(solution)/shard_map/mlp_back/pallas_call | solution.py:920
  414.9 6.5 all-to-all-done.14.refs_0_
  455.8 9.3 %mlp_back.6 = (bf16[144,768]{1,0:T(8,128)(2,1)}, bf16[144,3072]{1,0:T(8,128)(2,1)}, f32[144,768]{1,0:T(8,128)}, f32[1,3072]{1,0:T(1,128)S(1)}, f32[3,768]{1,0:T(4,128)S(1)}, /*index=5*/bf16[16,72,128]{2,1,0:T(8,128)(2,1)}) custom-call(f32[144,768]{1,0:T(8,128)S(1)} %get-tuple-element.173.refs_0_, f32[144,3072]{1,0:T(8,128)} %get-tuple-element.174.refs_1_, ...), custom_call_target="tpu_custom_call" | custom-call | tf_op jit(solution)/shard_map/mlp_back/pallas_call | solution.py:920
  502.6 5.5 all-to-all-start.17
  518.9 9.3 %mlp_back.7 = (bf16[144,768]{1,0:T(8,128)(2,1)}, bf16[144,3072]{1,0:T(8,128)(2,1)}, f32[144,768]{1,0:T(8,128)}, f32[1,3072]{1,0:T(1,128)S(1)}, f32[3,768]{1,0:T(4,128)S(1)}, /*index=5*/bf16[16,72,128]{2,1,0:T(8,128)(2,1)}) custom-call(f32[144,768]{1,0:T(8,128)S(1)} %get-tuple-element.190.refs_0_, f32[144,3072]{1,0:T(8,128)} %get-tuple-element.191.refs_1_, ...), custom_call_target="tpu_custom_call" | custom-call | tf_op jit(solution)/shard_map/mlp_back/pallas_call | solution.py:920
  555.8 5.2 all-to-all-start.19
  578.2 6.5 pack.1
  593.6 31.3 %collective-permute-done.27 = bf16[2,2,1,2,128,768]{5,4,3,2,1,0:T(8,128)(2,1)} collective-permute-done((bf16[2,2,1,2,128,768]{5,4,3,2,1,0:T(8,128)(2,1)}, bf16[2,2,1,2,128,768]{5,4,3,2,1,0:T(8,128)(2,1)}, u32[]{:S(2)}, u32[]{:S(2)}) %collective-permute-start.27) | collective-permute-done | bytes 1572896 | tf_op jit(solution)/shard_map/ppermute | solution.py:1186
  640.8 9.8 %collective-permute-done.30 = bf16[2,2,1,1,128,768]{5,4,3,2,1,0:T(8,128)(2,1)S(1)} collective-permute-done((bf16[2,2,1,1,128,768]{5,4,3,2,1,0:T(8,128)(2,1)S(1)}, bf16[2,2,1,1,128,768]{5,4,3,2,1,0:T(8,128)(2,1)S(1)}, u32[]{:S(2)}, u32[]{:S(2)}) %collective-permute-start.30) | collective-permute-done | bytes 786464 | tf_op jit(solution)/shard_map/ppermute | solution.py:1186
  658.4 15.2 %collective-permute-done.40 = bf16[2,2,2,1,70,8,128]{6,5,4,3,2,1,0:T(8,128)(2,1)S(1)} collective-permute-done((bf16[2,2,2,1,70,8,128]{6,5,4,3,2,1,0:T(8,128)(2,1)S(1)}, bf16[2,2,2,1,70,8,128]{6,5,4,3,2,1,0:T(8,128)(2,1)S(1)}, u32[]{:S(2)}, u32[]{:S(2)}) %collective-permute-start.40) | collective-permute-done | bytes 1146912 | tf_op jit(solution)/shard_map/ppermute | solution.py:1186
  685.3 6.1 collective-permute-done.33
  694.9 7.1 collective-permute-done.41
  707.6 8.3 collective-permute-done.36
  732.4 13.3 %collective-permute-done.46 = bf16[212,8,128]{2,1,0:T(8,128)(2,1)} collective-permute-done((bf16[212,8,128]{2,1,0:T(8,128)(2,1)}, bf16[212,8,128]{2,1,0:T(8,128)(2,1)}, u32[]{:S(2)}, u32[]{:S(2)}) %collective-permute-start.46) | collective-permute-done | bytes 434208 | tf_op jit(solution)/shard_map/ppermute | solution.py:1186
  751.4 9.8 %all-to-all-start.20 = ((f32[32,1,128]{2,1,0:T(1,128)}), f32[32,1,128]{2,1,0:T(1,128)S(1)}, u32[]{:S(2)}, u32[]{:S(2)}) async-start(f32[32,1,128]{2,1,0:T(1,128)} %broadcast_in_dim.104), calls=%async_computation.20 | async-start | bytes 32768 | tf_op jit(solution)/shard_map/all_to_all | solution.py:938
  761.3 7.1 all-to-all-done.20
  780.0 14.8 %collective-permute-done.48 = bf16[192,768]{1,0:T(8,128)(2,1)S(1)} collective-permute-done((bf16[192,768]{1,0:T(8,128)(2,1)S(1)}, bf16[192,768]{1,0:T(8,128)(2,1)S(1)}, u32[]{:S(2)}, u32[]{:S(2)}) %collective-permute-start.48) | collective-permute-done | bytes 294944 | tf_op jit(solution)/shard_map/ppermute | solution.py:1186
  796.1 7.3 collective-permute-done.49
  829.2 5.0 multiply_subtract_fusion
  835.5 7.1 collective-permute-done.53
  853.6 11.3 %multiply_add_fusion = f32[2,2,768,768]{3,2,1,0:T(8,128)} fusion(f32[2,2,768,768]{3,2,1,0:T(8,128)} %bitcast.372, f32[2,2,768,768]{3,2,1,0:T(8,128)} %param.23), kind=kLoop, calls=%fused_computation.1 | loop fusion | flops 4718592 | bytes 28311552 | tf_op jit(solution)/shard_map/add | solution.py:1591
  869.4 17.0 %collective-permute-done.58 = bf16[392,768]{1,0:T(8,128)(2,1)S(1)} collective-permute-done((bf16[392,768]{1,0:T(8,128)(2,1)S(1)}, bf16[392,768]{1,0:T(8,128)(2,1)S(1)}, u32[]{:S(2)}, u32[]{:S(2)}) %collective-permute-start.58) | collective-permute-done | bytes 602144 | tf_op jit(solution)/shard_map/ppermute | solution.py:1256
  898.8 8.4 muon.1
  (769 shorter events, 460.9 us)
Async XLA Ops:
  9.3 39.7 %all-to-all-start = ((bf16[8,18,1280]{2,1,0:T(8,128)(2,1)}), bf16[8,18,1280]{2,1,0:T(8,128)(2,1)}, u32[]{:S(2)}, u32[]{:S(2)}) async-start(bf16[8,18,1280]{2,1,0:T(8,128)(2,1)} %copy.149), calls=%async_computation | async-start | bytes 983040 | tf_op jit(solution)/shard_map/all_to_all | solution.py:1296
  21.9 27.1 %collective-permute-start = (bf16[212,8,128]{2,1,0:T(8,128)(2,1)S(1)}, bf16[212,8,128]{2,1,0:T(8,128)(2,1)S(1)}, u32[]{:S(2)}, u32[]{:S(2)}) collective-permute-start(bf16[212,8,128]{2,1,0:T(8,128)(2,1)S(1)} %fusion.35), channel_id=1, source_target_pairs={{0,16},{16,0},{1,17},{17,1},{2,18},{18,2},{3,19},{19,3},{4,20},{20... | collective-permute-start | bytes 1302536 | tf_op jit(solution)/shard_map/ppermute | solution.py:1186
  71.3 26.4 %collective-permute-start.11 = (bf16[2,2,2,70,8,128]{5,4,3,2,1,0:T(8,128)(2,1)S(1)}, bf16[2,2,2,70,8,128]{5,4,3,2,1,0:T(8,128)(2,1)S(1)}, u32[]{:S(2)}, u32[]{:S(2)}) collective-permute-start(bf16[2,2,2,70,8,128]{5,4,3,2,1,0:T(8,128)(2,1)S(1)} %get-tuple-element.270), channel_id=1, source_target_pairs={{0,2},{2,0},{1,3},{3,1},{4,6},{6,4},{5,7},{7,5},{8,10},{10,8},{9,1... | collective-permute-start | bytes 3440648 | tf_op jit(solution)/shard_map/ppermute | solution.py:1186
  75.0 24.4 %collective-permute-start.3 = (bf16[2,2,2,72,8,128]{5,4,3,2,1,0:T(8,128)(2,1)S(1)}, bf16[2,2,2,72,8,128]{5,4,3,2,1,0:T(8,128)(2,1)S(1)}, u32[]{:S(2)}, u32[]{:S(2)}) collective-permute-start(bf16[2,2,2,72,8,128]{5,4,3,2,1,0:T(8,128)(2,1)S(1)} %get-tuple-element.268), channel_id=1, source_target_pairs={{0,8},{8,0},{1,9},{9,1},{2,10},{10,2},{3,11},{11,3},{4,12},{12,4},... | collective-permute-start | bytes 3538952 | tf_op jit(solution)/shard_map/ppermute | solution.py:1186
  75.2 26.2 %collective-permute-start.7 = (bf16[2,2,2,70,8,128]{5,4,3,2,1,0:T(8,128)(2,1)S(1)}, bf16[2,2,2,70,8,128]{5,4,3,2,1,0:T(8,128)(2,1)S(1)}, u32[]{:S(2)}, u32[]{:S(2)}) collective-permute-start(bf16[2,2,2,70,8,128]{5,4,3,2,1,0:T(8,128)(2,1)S(1)} %get-tuple-element.272), channel_id=1, source_target_pairs={{0,4},{4,0},{1,5},{5,1},{2,6},{6,2},{3,7},{7,3},{8,12},{12,8},{9,1... | collective-permute-start | bytes 3440648 | tf_op jit(solution)/shard_map/ppermute | solution.py:1186
  99.3 53.4 %collective-permute-start.12 = (bf16[2,2,2,2,70,8,128]{6,5,4,3,2,1,0:T(8,128)(2,1)}, bf16[2,2,2,2,70,8,128]{6,5,4,3,2,1,0:T(8,128)(2,1)}, u32[]{:S(2)}, u32[]{:S(2)}) collective-permute-start(bf16[2,2,2,2,70,8,128]{6,5,4,3,2,1,0:T(8,128)(2,1)} %pad_maximum_fusion.6.refs_5_), channel_id=1, source_target_pairs={{0,1},{1,0},{2,3},{3,2},{4,5},{5,4},{6,7},{7,6},{8,9},{9,8},{10,11... | collective-permute-start | bytes 6881288 | tf_op jit(solution)/shard_map/ppermute | solution.py:1186
  101.0 53.2 %collective-permute-start.4 = (bf16[2,2,2,2,72,8,128]{6,5,4,3,2,1,0:T(8,128)(2,1)}, bf16[2,2,2,2,72,8,128]{6,5,4,3,2,1,0:T(8,128)(2,1)}, u32[]{:S(2)}, u32[]{:S(2)}) collective-permute-start(bf16[2,2,2,2,72,8,128]{6,5,4,3,2,1,0:T(8,128)(2,1)} %pad_maximum_fusion.3.refs_1_), channel_id=1, source_target_pairs={{0,1},{1,0},{2,3},{3,2},{4,5},{5,4},{6,7},{7,6},{8,9},{9,8},{10,11... | collective-permute-start | bytes 7077896 | tf_op jit(solution)/shard_map/ppermute | solution.py:1186
  103.1 51.1 %collective-permute-start.8 = (bf16[2,2,2,2,70,8,128]{6,5,4,3,2,1,0:T(8,128)(2,1)}, bf16[2,2,2,2,70,8,128]{6,5,4,3,2,1,0:T(8,128)(2,1)}, u32[]{:S(2)}, u32[]{:S(2)}) collective-permute-start(bf16[2,2,2,2,70,8,128]{6,5,4,3,2,1,0:T(8,128)(2,1)} %pad_maximum_fusion.5.refs_3_), channel_id=1, source_target_pairs={{0,1},{1,0},{2,3},{3,2},{4,5},{5,4},{6,7},{7,6},{8,9},{9,8},{10,11... | collective-permute-start | bytes 6881288 | tf_op jit(solution)/shard_map/ppermute | solution.py:1186
  104.6 26.8 %all-to-all-start.1 = ((bf16[8,36,1280]{2,1,0:T(8,128)(2,1)}), bf16[8,36,1280]{2,1,0:T(8,128)(2,1)S(1)}, u32[]{:S(2)}, u32[]{:S(2)}) async-start(bf16[8,36,1280]{2,1,0:T(8,128)(2,1)} %copy.151), calls=%async_computation.1 | async-start | bytes 1638400 | tf_op jit(solution)/shard_map/all_to_all | solution.py:1296
  110.6 16.3 %collective-permute-start.13 = (bf16[2,192,768]{2,1,0:T(8,128)(2,1)S(1)}, bf16[2,192,768]{2,1,0:T(8,128)(2,1)S(1)}, u32[]{:S(2)}, u32[]{:S(2)}) collective-permute-start(bf16[2,192,768]{2,1,0:T(8,128)(2,1)S(1)} %dynamic-slice_bitcast_fusion), channel_id=1, source_target_pairs={{0,2},{2,0},{1,3},{3,1},{4,6},{6,4},{5,7},{7,5},{8,10},{10,8},{9,1... | collective-permute-start | bytes 1769480 | tf_op jit(solution)/shard_map/ppermute | solution.py:1186
  113.3 37.7 %collective-permute-start.16 = (bf16[2,2,192,768]{3,2,1,0:T(8,128)(2,1)}, bf16[2,2,192,768]{3,2,1,0:T(8,128)(2,1)}, u32[]{:S(2)}, u32[]{:S(2)}) collective-permute-start(bf16[2,2,192,768]{3,2,1,0:T(8,128)(2,1)} %slice_bitcast_fusion), channel_id=1, source_target_pairs={{0,2},{2,0},{1,3},{3,1},{4,6},{6,4},{5,7},{7,5},{8,10},{10,8},{9,1... | collective-permute-start | bytes 3538952 | tf_op jit(solution)/shard_map/ppermute | solution.py:1186
  140.2 79.7 %collective-permute-start.18 = (bf16[2,2,2,192,768]{4,3,2,1,0:T(8,128)(2,1)}, bf16[2,2,2,192,768]{4,3,2,1,0:T(8,128)(2,1)}, u32[]{:S(2)}, u32[]{:S(2)}) collective-permute-start(bf16[2,2,2,192,768]{4,3,2,1,0:T(8,128)(2,1)} %narrow.2), channel_id=1, source_target_pairs={{0,1},{1,0},{2,3},{3,2},{4,5},{5,4},{6,7},{7,6},{8,9},{9,8},{10,11... | collective-permute-start | bytes 7077896 | tf_op jit(solution)/shard_map/ppermute | solution.py:1186
  151.0 36.1 %collective-permute-start.15 = (bf16[2,2,192,768]{3,2,1,0:T(8,128)(2,1)}, bf16[2,2,192,768]{3,2,1,0:T(8,128)(2,1)}, u32[]{:S(2)}, u32[]{:S(2)}) collective-permute-start(bf16[2,2,192,768]{3,2,1,0:T(8,128)(2,1)} %pad_maximum_fusion.10), channel_id=1, source_target_pairs={{0,8},{8,0},{1,9},{9,1},{2,10},{10,2},{3,11},{11,3},{4,12},{12,4},... | collective-permute-start | bytes 3538952 | tf_op jit(solution)/shard_map/ppermute | solution.py:1186
  152.7 34.4 %collective-permute-start.17 = (bf16[2,2,192,768]{3,2,1,0:T(8,128)(2,1)}, bf16[2,2,192,768]{3,2,1,0:T(8,128)(2,1)}, u32[]{:S(2)}, u32[]{:S(2)}) collective-permute-start(bf16[2,2,192,768]{3,2,1,0:T(8,128)(2,1)} %collective-permute-done.16), channel_id=1, source_target_pairs={{0,4},{4,0},{1,5},{5,1},{2,6},{6,2},{3,7},{7,3},{8,12},{12,8},{9,1... | collective-permute-start | bytes 3538952 | tf_op jit(solution)/shard_map/ppermute | solution.py:1186
  166.1 17.3 %all-to-all-start.2 = ((bf16[16,72,128]{2,1,0:T(8,128)(2,1)}), bf16[16,72,128]{2,1,0:T(8,128)(2,1)S(1)}, u32[]{:S(2)}, u32[]{:S(2)}) async-start(bf16[16,72,128]{2,1,0:T(8,128)(2,1)} %get-tuple-element.132), calls=%async_computation.2 | async-start | bytes 589824 | tf_op jit(solution)/shard_map/all_to_all | solution.py:932
  191.8 28.1 %collective-permute-start.19 = (bf16[2,2,2,192,768]{4,3,2,1,0:T(8,128)(2,1)}, bf16[2,2,2,192,768]{4,3,2,1,0:T(8,128)(2,1)}, u32[]{:S(2)}, u32[]{:S(2)}) collective-permute-start(bf16[2,2,2,192,768]{4,3,2,1,0:T(8,128)(2,1)} %maximum_select_fusion), channel_id=1, source_target_pairs={{0,1},{1,0},{2,3},{3,2},{4,5},{5,4},{6,7},{7,6},{8,9},{9,8},{10,11... | collective-permute-start | bytes 7077896 | tf_op jit(solution)/shard_map/ppermute | solution.py:1186
  199.1 64.5 %collective-permute-start.20 = (bf16[2,2,2,192,768]{4,3,2,1,0:T(8,128)(2,1)}, bf16[2,2,2,192,768]{4,3,2,1,0:T(8,128)(2,1)}, u32[]{:S(2)}, u32[]{:S(2)}) collective-permute-start(bf16[2,2,2,192,768]{4,3,2,1,0:T(8,128)(2,1)} %narrow.3), channel_id=1, source_target_pairs={{0,1},{1,0},{2,3},{3,2},{4,5},{5,4},{6,7},{7,6},{8,9},{9,8},{10,11... | collective-permute-start | bytes 7077896 | tf_op jit(solution)/shard_map/ppermute | solution.py:1186
  202.8 57.5 %collective-permute-start.21 = (bf16[2,2,2,192,768]{4,3,2,0,1:T(8,128)(2,1)}, bf16[2,2,2,192,768]{4,3,2,0,1:T(8,128)(2,1)}, u32[]{:S(2)}, u32[]{:S(2)}) collective-permute-start(bf16[2,2,2,192,768]{4,3,2,0,1:T(8,128)(2,1)} %pad_maximum_fusion.4), channel_id=1, source_target_pairs={{0,1},{1,0},{2,3},{3,2},{4,5},{5,4},{6,7},{7,6},{8,9},{9,8},{10,11... | collective-permute-start | bytes 7077896 | tf_op jit(solution)/shard_map/ppermute | solution.py:1186
  244.7 19.0 %all-to-all-start.5 = ((bf16[16,72,128]{2,1,0:T(8,128)(2,1)}), bf16[16,72,128]{2,1,0:T(8,128)(2,1)}, u32[]{:S(2)}, u32[]{:S(2)}) async-start(bf16[16,72,128]{2,1,0:T(8,128)(2,1)} %get-tuple-element.141), calls=%async_computation.5 | async-start | bytes 589824 | tf_op jit(solution)/shard_map/all_to_all | solution.py:932
  469.2 19.8 %collective-permute-start.22 = (bf16[1536,768]{1,0:T(8,128)(2,1)}, bf16[1536,768]{1,0:T(8,128)(2,1)}, u32[]{:S(2)}, u32[]{:S(2)}) collective-permute-start(bf16[1536,768]{1,0:T(8,128)(2,1)} %convolution_convert_fusion.9), channel_id=1, source_target_pairs={{0,1},{1,0},{2,3},{3,2},{4,5},{5,4},{6,7},{7,6},{8,9},{9,8},{10,11... | collective-permute-start | bytes 7077896 | tf_op jit(solution)/shard_map/ppermute | solution.py:1186
  472.2 20.1 %collective-permute-start.23 = (bf16[1536,768]{1,0:T(8,128)(2,1)}, bf16[1536,768]{1,0:T(8,128)(2,1)}, u32[]{:S(2)}, u32[]{:S(2)}) collective-permute-start(bf16[1536,768]{1,0:T(8,128)(2,1)} %convolution_convert_fusion.8), channel_id=1, source_target_pairs={{0,1},{1,0},{2,3},{3,2},{4,5},{5,4},{6,7},{7,6},{8,9},{9,8},{10,11... | collective-permute-start | bytes 7077896 | tf_op jit(solution)/shard_map/ppermute | solution.py:1186
  472.7 25.4 %all-to-all-start.16 = ((bf16[16,72,128]{2,1,0:T(8,128)(2,1)}), bf16[16,72,128]{2,1,0:T(8,128)(2,1)S(1)}, u32[]{:S(2)}, u32[]{:S(2)}) async-start(bf16[16,72,128]{2,1,0:T(8,128)(2,1)} %get-tuple-element.183), calls=%async_computation.16 | async-start | bytes 589824 | tf_op jit(solution)/shard_map/all_to_all | solution.py:932
  561.0 265.6 %all-gather.2.cloned.1.call-start = ((), (), s32[]{:S(2)}) async-start(), calls=%async_computation.21 | async-start | bytes 5308416 | tf_op jit(solution)/shard_map/all_gather | solution.py:1561
  584.7 45.3 %collective-permute-start.29 = (bf16[2,2,2,2,212,8,128]{6,5,4,3,2,1,0:T(8,128)(2,1)}, bf16[2,2,2,2,212,8,128]{6,5,4,3,2,1,0:T(8,128)(2,1)}, u32[]{:S(2)}, u32[]{:S(2)}) collective-permute-start(bf16[2,2,2,2,212,8,128]{6,5,4,3,2,1,0:T(8,128)(2,1)} %get-tuple-element.236), channel_id=1, source_target_pairs={{0,1},{1,0},{2,3},{3,2},{4,5},{5,4},{6,7},{7,6},{8,9},{9,8},{10,11... | collective-permute-start | bytes 20840456 | tf_op jit(solution)/shard_map/ppermute | solution.py:1186
  586.3 43.3 %collective-permute-start.28 = (bf16[2,1,2,2,128,768]{5,4,3,2,1,0:T(8,128)(2,1)}, bf16[2,1,2,2,128,768]{5,4,3,2,1,0:T(8,128)(2,1)S(1)}, u32[]{:S(2)}, u32[]{:S(2)}) collective-permute-start(bf16[2,1,2,2,128,768]{5,4,3,2,1,0:T(8,128)(2,1)} %fusion.10), channel_id=1, source_target_pairs={{0,8},{8,0},{1,9},{9,1},{2,10},{10,2},{3,11},{11,3},{4,12},{12,4},... | collective-permute-start | bytes 4718600 | tf_op jit(solution)/shard_map/ppermute | solution.py:1186
  588.1 36.8 %collective-permute-start.27 = (bf16[2,2,1,2,128,768]{5,4,3,2,1,0:T(8,128)(2,1)}, bf16[2,2,1,2,128,768]{5,4,3,2,1,0:T(8,128)(2,1)}, u32[]{:S(2)}, u32[]{:S(2)}) collective-permute-start(bf16[2,2,1,2,128,768]{5,4,3,2,1,0:T(8,128)(2,1)} %pad_maximum_fusion.7), channel_id=1, source_target_pairs={{0,2},{2,0},{1,3},{3,1},{4,6},{6,4},{5,7},{7,5},{8,10},{10,8},{9,1... | collective-permute-start | bytes 4718600 | tf_op jit(solution)/shard_map/ppermute | solution.py:1186
  590.8 36.6 %collective-permute-start.26 = (bf16[2,2,2,1,128,768]{5,4,3,2,1,0:T(8,128)(2,1)}, bf16[2,2,2,1,128,768]{5,4,3,2,1,0:T(8,128)(2,1)}, u32[]{:S(2)}, u32[]{:S(2)}) collective-permute-start(bf16[2,2,2,1,128,768]{5,4,3,2,1,0:T(8,128)(2,1)} %pad_maximum_fusion.8), channel_id=1, source_target_pairs={{0,4},{4,0},{1,5},{5,1},{2,6},{6,2},{3,7},{7,3},{8,12},{12,8},{9,1... | collective-permute-start | bytes 4718600 | tf_op jit(solution)/shard_map/ppermute | solution.py:1186
  630.0 20.5 %collective-permute-start.30 = (bf16[2,2,1,1,128,768]{5,4,3,2,1,0:T(8,128)(2,1)S(1)}, bf16[2,2,1,1,128,768]{5,4,3,2,1,0:T(8,128)(2,1)S(1)}, u32[]{:S(2)}, u32[]{:S(2)}) collective-permute-start(bf16[2,2,1,1,128,768]{5,4,3,2,1,0:T(8,128)(2,1)S(1)} %slice.550), channel_id=1, source_target_pairs={{0,2},{2,0},{1,3},{3,1},{4,6},{6,4},{5,7},{7,5},{8,10},{10,8},{9,1... | collective-permute-start | bytes 2359304 | tf_op jit(solution)/shard_map/ppermute | solution.py:1186
  631.4 20.9 %collective-permute-start.32 = (bf16[2,1,1,2,128,768]{5,4,3,2,1,0:T(8,128)(2,1)S(1)}, bf16[2,1,1,2,128,768]{5,4,3,2,1,0:T(8,128)(2,1)S(1)}, u32[]{:S(2)}, u32[]{:S(2)}) collective-permute-start(bf16[2,1,1,2,128,768]{5,4,3,2,1,0:T(8,128)(2,1)S(1)} %constant_dynamic-slice_fusion.1), channel_id=1, source_target_pairs={{0,8},{8,0},{1,9},{9,1},{2,10},{10,2},{3,11},{11,3},{4,12},{12,4},... | collective-permute-start | bytes 2359304 | tf_op jit(solution)/shard_map/ppermute | solution.py:1186
  635.5 38.0 %collective-permute-start.40 = (bf16[2,2,2,1,70,8,128]{6,5,4,3,2,1,0:T(8,128)(2,1)S(1)}, bf16[2,2,2,1,70,8,128]{6,5,4,3,2,1,0:T(8,128)(2,1)S(1)}, u32[]{:S(2)}, u32[]{:S(2)}) collective-permute-start(bf16[2,2,2,1,70,8,128]{6,5,4,3,2,1,0:T(8,128)(2,1)S(1)} %add_convert_fusion.12), channel_id=1, source_target_pairs={{0,2},{2,0},{1,3},{3,1},{4,6},{6,4},{5,7},{7,5},{8,10},{10,8},{9,1... | collective-permute-start | bytes 3440648 | tf_op jit(solution)/shard_map/ppermute | solution.py:1186
  637.1 20.5 %collective-permute-start.34 = (bf16[2,1,2,1,128,768]{5,4,3,2,1,0:T(8,128)(2,1)S(1)}, bf16[2,1,2,1,128,768]{5,4,3,2,1,0:T(8,128)(2,1)S(1)}, u32[]{:S(2)}, u32[]{:S(2)}) collective-permute-start(bf16[2,1,2,1,128,768]{5,4,3,2,1,0:T(8,128)(2,1)S(1)} %slice.554), channel_id=1, source_target_pairs={{0,4},{4,0},{1,5},{5,1},{2,6},{6,2},{3,7},{7,3},{8,12},{12,8},{9,1... | collective-permute-start | bytes 2359304 | tf_op jit(solution)/shard_map/ppermute | solution.py:1186
  639.3 43.6 %collective-permute-start.37 = (bf16[2,2,1,2,72,8,128]{6,5,4,3,2,1,0:T(8,128)(2,1)S(1)}, bf16[2,2,1,2,72,8,128]{6,5,4,3,2,1,0:T(8,128)(2,1)S(1)}, u32[]{:S(2)}, u32[]{:S(2)}) collective-permute-start(bf16[2,2,1,2,72,8,128]{6,5,4,3,2,1,0:T(8,128)(2,1)S(1)} %add_convert_fusion.8), channel_id=1, source_target_pairs={{0,4},{4,0},{1,5},{5,1},{2,6},{6,2},{3,7},{7,3},{8,12},{12,8},{9,1... | collective-permute-start | bytes 3538952 | tf_op jit(solution)/shard_map/ppermute | solution.py:1186
  650.6 28.2 %collective-permute-start.43 = (bf16[2,1,2,2,70,8,128]{6,5,4,3,2,1,0:T(8,128)(2,1)S(1)}, bf16[2,1,2,2,70,8,128]{6,5,4,3,2,1,0:T(8,128)(2,1)S(1)}, u32[]{:S(2)}, u32[]{:S(2)}) collective-permute-start(bf16[2,1,2,2,70,8,128]{6,5,4,3,2,1,0:T(8,128)(2,1)S(1)} %add_convert_fusion.10), channel_id=1, source_target_pairs={{0,8},{8,0},{1,9},{9,1},{2,10},{10,2},{3,11},{11,3},{4,12},{12,4},... | collective-permute-start | bytes 3440648 | tf_op jit(solution)/shard_map/ppermute | solution.py:1186
  652.3 39.8 %collective-permute-start.31 = (bf16[2,1,1,1,128,768]{5,4,3,2,1,0:T(8,128)(2,1)S(1)}, bf16[2,1,1,1,128,768]{5,4,3,2,1,0:T(8,128)(2,1)S(1)}, u32[]{:S(2)}, u32[]{:S(2)}) collective-permute-start(bf16[2,1,1,1,128,768]{5,4,3,2,1,0:T(8,128)(2,1)S(1)} %constant_dynamic-slice_fusion.2), channel_id=1, source_target_pairs={{0,8},{8,0},{1,9},{9,1},{2,10},{10,2},{3,11},{11,3},{4,12},{12,4},... | collective-permute-start | bytes 1179656 | tf_op jit(solution)/shard_map/ppermute | solution.py:1186
  657.6 33.7 %collective-permute-start.33 = (bf16[2,1,1,1,128,768]{5,4,3,2,1,0:T(8,128)(2,1)S(1)}, bf16[2,1,1,1,128,768]{5,4,3,2,1,0:T(8,128)(2,1)S(1)}, u32[]{:S(2)}, u32[]{:S(2)}) collective-permute-start(bf16[2,1,1,1,128,768]{5,4,3,2,1,0:T(8,128)(2,1)S(1)} %slice.638), channel_id=1, source_target_pairs={{0,4},{4,0},{1,5},{5,1},{2,6},{6,2},{3,7},{7,3},{8,12},{12,8},{9,1... | collective-permute-start | bytes 1179656 | tf_op jit(solution)/shard_map/ppermute | solution.py:1186
  673.5 18.5 %collective-permute-start.35 = (bf16[2,1,1,1,128,768]{5,4,3,2,1,0:T(8,128)(2,1)S(1)}, bf16[2,1,1,1,128,768]{5,4,3,2,1,0:T(8,128)(2,1)S(1)}, u32[]{:S(2)}, u32[]{:S(2)}) collective-permute-start(bf16[2,1,1,1,128,768]{5,4,3,2,1,0:T(8,128)(2,1)S(1)} %slice.640), channel_id=1, source_target_pairs={{0,2},{2,0},{1,3},{3,1},{4,6},{6,4},{5,7},{7,5},{8,10},{10,8},{9,1... | collective-permute-start | bytes 1179656 | tf_op jit(solution)/shard_map/ppermute | solution.py:1186
  678.8 23.3 %collective-permute-start.41 = (bf16[2,1,2,1,70,8,128]{6,5,4,3,2,1,0:T(8,128)(2,1)S(1)}, bf16[2,1,2,1,70,8,128]{6,5,4,3,2,1,0:T(8,128)(2,1)S(1)}, u32[]{:S(2)}, u32[]{:S(2)}) collective-permute-start(bf16[2,1,2,1,70,8,128]{6,5,4,3,2,1,0:T(8,128)(2,1)S(1)} %slice.648), channel_id=1, source_target_pairs={{0,8},{8,0},{1,9},{9,1},{2,10},{10,2},{3,11},{11,3},{4,12},{12,4},... | collective-permute-start | bytes 1720328 | tf_op jit(solution)/shard_map/ppermute | solution.py:1186
  682.9 21.4 %collective-permute-start.44 = (bf16[2,1,1,2,70,8,128]{6,5,4,3,2,1,0:T(8,128)(2,1)S(1)}, bf16[2,1,1,2,70,8,128]{6,5,4,3,2,1,0:T(8,128)(2,1)S(1)}, u32[]{:S(2)}, u32[]{:S(2)}) collective-permute-start(bf16[2,1,1,2,70,8,128]{6,5,4,3,2,1,0:T(8,128)(2,1)S(1)} %slice.652), channel_id=1, source_target_pairs={{0,4},{4,0},{1,5},{5,1},{2,6},{6,2},{3,7},{7,3},{8,12},{12,8},{9,1... | collective-permute-start | bytes 1720328 | tf_op jit(solution)/shard_map/ppermute | solution.py:1186
  692.4 23.5 %collective-permute-start.36 = (bf16[384,768]{1,0:T(8,128)(2,1)S(1)}, bf16[384,768]{1,0:T(8,128)(2,1)S(1)}, u32[]{:S(2)}, u32[]{:S(2)}) collective-permute-start(bf16[384,768]{1,0:T(8,128)(2,1)S(1)} %select_bitcast_fusion), channel_id=1, source_target_pairs={{0,16},{16,0},{1,17},{17,1},{2,18},{18,2},{3,19},{19,3},{4,20},{20... | collective-permute-start | bytes 1769480 | tf_op jit(solution)/shard_map/ppermute | solution.py:1186
  722.7 23.0 %collective-permute-start.46 = (bf16[212,8,128]{2,1,0:T(8,128)(2,1)}, bf16[212,8,128]{2,1,0:T(8,128)(2,1)}, u32[]{:S(2)}, u32[]{:S(2)}) collective-permute-start(bf16[212,8,128]{2,1,0:T(8,128)(2,1)} %slice_bitcast_fusion.1), channel_id=1, source_target_pairs={{0,16},{16,0},{1,17},{17,1},{2,18},{18,2},{3,19},{19,3},{4,20},{20... | collective-permute-start | bytes 1302536 | tf_op jit(solution)/shard_map/ppermute | solution.py:1186
  751.4 16.9 %all-to-all-start.20 = ((f32[32,1,128]{2,1,0:T(1,128)}), f32[32,1,128]{2,1,0:T(1,128)S(1)}, u32[]{:S(2)}, u32[]{:S(2)}) async-start(f32[32,1,128]{2,1,0:T(1,128)} %broadcast_in_dim.104), calls=%async_computation.20 | async-start | bytes 32768 | tf_op jit(solution)/shard_map/all_to_all | solution.py:938
  778.9 16.0 %collective-permute-start.48 = (bf16[192,768]{1,0:T(8,128)(2,1)S(1)}, bf16[192,768]{1,0:T(8,128)(2,1)S(1)}, u32[]{:S(2)}, u32[]{:S(2)}) collective-permute-start(bf16[192,768]{1,0:T(8,128)(2,1)S(1)} %get-tuple-element.288), channel_id=1, source_target_pairs={{0,4},{4,0},{1,5},{5,1},{2,6},{6,2},{3,7},{7,3},{8,12},{12,8},{9,1... | collective-permute-start | bytes 884744 | tf_op jit(solution)/shard_map/ppermute | solution.py:1186
  779.4 15.4 %collective-permute-start.50 = (bf16[192,768]{1,0:T(8,128)(2,1)S(1)}, bf16[192,768]{1,0:T(8,128)(2,1)S(1)}, u32[]{:S(2)}, u32[]{:S(2)}) collective-permute-start(bf16[192,768]{1,0:T(8,128)(2,1)S(1)} %get-tuple-element.289), channel_id=1, source_target_pairs={{0,2},{2,0},{1,3},{3,1},{4,6},{6,4},{5,7},{7,5},{8,10},{10,8},{9,1... | collective-permute-start | bytes 884744 | tf_op jit(solution)/shard_map/ppermute | solution.py:1186
  826.6 16.0 %collective-permute-start.53 = (bf16[392,768]{1,0:T(8,128)(2,1)}, bf16[392,768]{1,0:T(8,128)(2,1)S(1)}, u32[]{:S(2)}, u32[]{:S(2)}) collective-permute-start(bf16[392,768]{1,0:T(8,128)(2,1)} %pad_maximum_fusion.18), channel_id=1, source_target_pairs={{0,8},{8,16},{16,24},{1,9},{9,17},{17,25},{2,10},{10,18},{18,26},{... | collective-permute-start | bytes 1806344 | tf_op jit(solution)/shard_map/ppermute | solution.py:1252
  834.2 17.2 %collective-permute-start.56 = (bf16[392,768]{1,0:T(8,128)(2,1)S(1)}, bf16[392,768]{1,0:T(8,128)(2,1)S(1)}, u32[]{:S(2)}, u32[]{:S(2)}) collective-permute-start(bf16[392,768]{1,0:T(8,128)(2,1)S(1)} %copy-done.68), channel_id=1, source_target_pairs={{8,0},{16,8},{24,16},{9,1},{17,9},{25,17},{10,2},{18,10},{26,18},{... | collective-permute-start | bytes 1806344 | tf_op jit(solution)/shard_map/ppermute | solution.py:1256
  851.4 16.4 %collective-permute-start.57 = (bf16[392,768]{1,0:T(8,128)(2,1)S(1)}, bf16[392,768]{1,0:T(8,128)(2,1)S(1)}, u32[]{:S(2)}, u32[]{:S(2)}) collective-permute-start(bf16[392,768]{1,0:T(8,128)(2,1)S(1)} %collective-permute-done.56), channel_id=1, source_target_pairs={{8,0},{16,8},{9,1},{17,9},{10,2},{18,10},{11,3},{19,11},{12,4},{20... | collective-permute-start | bytes 1806344 | tf_op jit(solution)/shard_map/ppermute | solution.py:1256
  852.7 16.4 %collective-permute-start.55 = (bf16[392,768]{1,0:T(8,128)(2,1)S(1)}, bf16[392,768]{1,0:T(8,128)(2,1)S(1)}, u32[]{:S(2)}, u32[]{:S(2)}) collective-permute-start(bf16[392,768]{1,0:T(8,128)(2,1)S(1)} %collective-permute-done.54), channel_id=1, source_target_pairs={{16,24},{17,25},{18,26},{19,27},{20,28},{21,29},{22,30},{23,31}} | collective-permute-start | bytes 1806344 | tf_op jit(solution)/shard_map/ppermute | solution.py:1252
  867.8 18.6 %collective-permute-start.58 = (bf16[392,768]{1,0:T(8,128)(2,1)S(1)}, bf16[392,768]{1,0:T(8,128)(2,1)S(1)}, u32[]{:S(2)}, u32[]{:S(2)}) collective-permute-start(bf16[392,768]{1,0:T(8,128)(2,1)S(1)} %collective-permute-done.57), channel_id=1, source_target_pairs={{8,0},{9,1},{10,2},{11,3},{12,4},{13,5},{14,6},{15,7}} | collective-permute-start | bytes 1806344 | tf_op jit(solution)/shard_map/ppermute | solution.py:1256
  (188 other events, 2610.6 us)
Sparse Core Ops, SparseCore 0:
  717.2 95.9 all-gather.1

commit v5 on v4

--- a/solution.py
+++ b/solution.py
@@ -1374,7 +1374,7 @@
             [current, shifts, embed_b, norms[0], spread, row_fwd, embed_w], going=(0,),
         )
         if roll_idx == 0:
-            sent, wanted = lax.optimization_barrier((sent, wanted))
+            sent, wanted, weight_pair = lax.optimization_barrier((sent, wanted, weight_pair))
         layers = []
         for depth in range(L):
             got = exchange(sent)

time: 926 us -> 924 us (level)
  waiting for transfers between devices: 326 us -> 314 us
    ppermute x54, waiting for transfers between devices: 207 us -> 177 us  [swap(): return lax.ppermute(values, axis, [(0, 1), (1, 0)])]
    all_to_all x3, waiting for transfers between devices: 4.06 us -> 18.8 us  [to_items(): lax.all_to_all(packed, LAT_AXES, split_axis=0, concat_axis=0, tiled=True)]
    unnamed x330 -> x326, local copies, waits for them, and re-layouts: 35.8 us -> 35.8 us
  transfers between devices with their start and end apart: 82 -> 82, of which waited for: 46 -> 45; matrix products, arithmetic and copies ran while one was open for 22% -> 23% of each run, Pallas kernels for 5% -> 5%
where the time goes in v5:
time: 924 us; the launch traced here: 913 us
  waiting for transfers between devices  314 us (34%)
  Pallas kernels  175 us (19%)
  starting transfers between devices  154 us (17%)
  local copies, waits for them, and re-layouts  99.9 us (11%)
  other arithmetic  88.7 us (10%)
  matrix products  57.3 us (6%)
  between operations  24.6 us (3%)
    ppermute x54, waiting for transfers between devices, swap(): return lax.ppermute(values, axis, [(0, 1), (1, 0)])  177 us
    pallas_call x31, Pallas kernels, launch(): pl.pallas_call(body, name=name, out_shape=out_shape, in_specs=in_specs, o...  154 us
    all_to_all x16, waiting for transfers between devices, exchange(): lax.all_to_all(values, ITEM_AXES, split_axis=0, concat_axis=0, tiled=True)  77.1 us
    all_to_all x16, starting transfers between devices, exchange(): lax.all_to_all(values, ITEM_AXES, split_axis=0, concat_axis=0, tiled=True)  65.8 us
    ppermute x54, starting transfers between devices, swap(): return lax.ppermute(values, axis, [(0, 1), (1, 0)])  45.6 us
    dot_general x14, matrix products, dot_tn(): lax.dot_general(left, right, (((0,), (0,)), ((), ())), preferred_element_...  36.6 us
    unnamed x326, local copies, waits for them, and re-layouts  35.8 us
    ppermute x3, waiting for transfers between devices, line_gather(): lax.ppermute(value, Z_AXES, [(i, i - 1) for i in range(1, 5 - step)])  23.6 us
  transfers between devices with their start and end apart: 82, of which 45 were waited for; matrix products, arithmetic and copies ran while one was open for 23% of the time, Pallas kernels for 5%

profile of v5, /device:TPU:0, one launch (start us, length us, event | category | flops | bytes accessed | tf_op | source)
XLA Modules:
  0.0 913.3 jit_solution(7729694789495906739)
XLA Ops:
  9.3 7.3 all-to-all-start
  25.3 6.3 narrow.2
  31.6 6.3 narrow.3
  37.9 11.1 %collective-permute-done = bf16[212,8,128]{2,1,0:T(8,128)(2,1)S(1)} collective-permute-done((bf16[212,8,128]{2,1,0:T(8,128)(2,1)S(1)}, bf16[212,8,128]{2,1,0:T(8,128)(2,1)S(1)}, u32[]{:S(2)}, u32[]{:S(2)}) %collective-permute-start) | collective-permute-done | bytes 434208 | tf_op jit(solution)/shard_map/ppermute | solution.py:1186
  62.4 8.7 collective-permute-done.10
  76.3 21.4 %collective-permute-done.11 = bf16[2,2,2,70,8,128]{5,4,3,2,1,0:T(8,128)(2,1)S(1)} collective-permute-done((bf16[2,2,2,70,8,128]{5,4,3,2,1,0:T(8,128)(2,1)S(1)}, bf16[2,2,2,70,8,128]{5,4,3,2,1,0:T(8,128)(2,1)S(1)}, u32[]{:S(2)}, u32[]{:S(2)}) %collective-permute-start.11) | collective-permute-done | bytes 1146912 | tf_op jit(solution)/shard_map/ppermute | solution.py:1186
  107.1 5.0 all-to-all-start.2
  112.8 5.7 all-to-all-done.2
  141.1 13.1 %all-to-all-done.1 = bf16[8,36,1280]{2,1,0:T(8,128)(2,1)S(1)} async-done(((bf16[8,36,1280]{2,1,0:T(8,128)(2,1)}), bf16[8,36,1280]{2,1,0:T(8,128)(2,1)S(1)}, u32[]{:S(2)}, u32[]{:S(2)}) %all-to-all-start.1) | async-done | bytes 737312 | tf_op jit(solution)/shard_map/all_to_all | solution.py:1296
  182.4 11.0 %all-to-all-done.4.refs_0_ = bf16[16,72,128]{2,1,0:T(8,128)(2,1)S(1)} async-done(((bf16[16,72,128]{2,1,0:T(8,128)(2,1)}), bf16[16,72,128]{2,1,0:T(8,128)(2,1)S(1)}, u32[]{:S(2)}, u32[]{:S(2)}) %all-to-all-start.4) | async-done | bytes 294944 | tf_op jit(solution)/shard_map/all_to_all | solution.py:932
  210.0 8.0 all-to-all-done.5.refs_0_
  217.9 7.7 mlp.4
  229.8 8.0 all-to-all-done.6.refs_0_
  261.1 8.5 mlp.5
  276.2 5.1 all-to-all-start.8
  283.6 5.9 all-to-all-done.8.refs_0_
  298.6 6.3 all-to-all-done.9.refs_0_
  304.9 7.7 mlp.6
  319.1 5.3 all-to-all-done.10.refs_0_
  334.0 5.7 all-to-all-done.11.refs_0_
  339.7 6.9 mlp.7
  355.5 9.2 %mlp_back.4 = (bf16[144,768]{1,0:T(8,128)(2,1)}, bf16[144,3072]{1,0:T(8,128)(2,1)}, f32[144,768]{1,0:T(8,128)}, f32[1,3072]{1,0:T(1,128)S(1)}, f32[3,768]{1,0:T(4,128)S(1)}, /*index=5*/bf16[16,72,128]{2,1,0:T(8,128)(2,1)}) custom-call(f32[144,768]{1,0:T(8,128)S(1)} %get-tuple-element.158.refs_0_, f32[144,3072]{1,0:T(8,128)} %get-tuple-element.159.refs_1_, ...), custom_call_target="tpu_custom_call" | custom-call | tf_op jit(solution)/shard_map/mlp_back/pallas_call | solution.py:920
  388.7 5.3 all-to-all-done.13.refs_0_
  396.8 9.2 %mlp_back.5 = (bf16[144,768]{1,0:T(8,128)(2,1)}, bf16[144,3072]{1,0:T(8,128)(2,1)}, f32[144,768]{1,0:T(8,128)}, f32[1,3072]{1,0:T(1,128)S(1)}, f32[3,768]{1,0:T(4,128)S(1)}, /*index=5*/bf16[16,72,128]{2,1,0:T(8,128)(2,1)}) custom-call(f32[144,768]{1,0:T(8,128)S(1)} %get-tuple-element.166.refs_0_, f32[144,3072]{1,0:T(8,128)} %get-tuple-element.167.refs_1_, ...), custom_call_target="tpu_custom_call" | custom-call | tf_op jit(solution)/shard_map/mlp_back/pallas_call | solution.py:920
  411.9 6.5 all-to-all-done.14.refs_0_
  452.7 9.3 %mlp_back.6 = (bf16[144,768]{1,0:T(8,128)(2,1)}, bf16[144,3072]{1,0:T(8,128)(2,1)}, f32[144,768]{1,0:T(8,128)}, f32[1,3072]{1,0:T(1,128)S(1)}, f32[3,768]{1,0:T(4,128)S(1)}, /*index=5*/bf16[16,72,128]{2,1,0:T(8,128)(2,1)}) custom-call(f32[144,768]{1,0:T(8,128)S(1)} %get-tuple-element.175.refs_0_, f32[144,3072]{1,0:T(8,128)} %get-tuple-element.176.refs_1_, ...), custom_call_target="tpu_custom_call" | custom-call | tf_op jit(solution)/shard_map/mlp_back/pallas_call | solution.py:920
  499.4 5.5 all-to-all-start.17
  508.1 4.9 all-to-all-done.17.refs_0_
  515.7 9.3 %mlp_back.7 = (bf16[144,768]{1,0:T(8,128)(2,1)}, bf16[144,3072]{1,0:T(8,128)(2,1)}, f32[144,768]{1,0:T(8,128)}, f32[1,3072]{1,0:T(1,128)S(1)}, f32[3,768]{1,0:T(4,128)S(1)}, /*index=5*/bf16[16,72,128]{2,1,0:T(8,128)(2,1)}) custom-call(f32[144,768]{1,0:T(8,128)S(1)} %get-tuple-element.192.refs_0_, f32[144,3072]{1,0:T(8,128)} %get-tuple-element.193.refs_1_, ...), custom_call_target="tpu_custom_call" | custom-call | tf_op jit(solution)/shard_map/mlp_back/pallas_call | solution.py:920
  552.6 5.2 all-to-all-start.19
  575.0 6.5 pack.1
  590.5 31.3 %collective-permute-done.27 = bf16[2,2,1,2,128,768]{5,4,3,2,1,0:T(8,128)(2,1)} collective-permute-done((bf16[2,2,1,2,128,768]{5,4,3,2,1,0:T(8,128)(2,1)}, bf16[2,2,1,2,128,768]{5,4,3,2,1,0:T(8,128)(2,1)}, u32[]{:S(2)}, u32[]{:S(2)}) %collective-permute-start.27) | collective-permute-done | bytes 1572896 | tf_op jit(solution)/shard_map/ppermute | solution.py:1186
  637.7 9.8 %collective-permute-done.30 = bf16[2,2,1,1,128,768]{5,4,3,2,1,0:T(8,128)(2,1)S(1)} collective-permute-done((bf16[2,2,1,1,128,768]{5,4,3,2,1,0:T(8,128)(2,1)S(1)}, bf16[2,2,1,1,128,768]{5,4,3,2,1,0:T(8,128)(2,1)S(1)}, u32[]{:S(2)}, u32[]{:S(2)}) %collective-permute-start.30) | collective-permute-done | bytes 786464 | tf_op jit(solution)/shard_map/ppermute | solution.py:1186
  655.2 15.2 %collective-permute-done.40 = bf16[2,2,2,1,70,8,128]{6,5,4,3,2,1,0:T(8,128)(2,1)S(1)} collective-permute-done((bf16[2,2,2,1,70,8,128]{6,5,4,3,2,1,0:T(8,128)(2,1)S(1)}, bf16[2,2,2,1,70,8,128]{6,5,4,3,2,1,0:T(8,128)(2,1)S(1)}, u32[]{:S(2)}, u32[]{:S(2)}) %collective-permute-start.40) | collective-permute-done | bytes 1146912 | tf_op jit(solution)/shard_map/ppermute | solution.py:1186
  682.1 6.1 collective-permute-done.33
  691.7 7.1 collective-permute-done.41
  704.5 8.4 collective-permute-done.36
  726.7 9.9 %collective-permute-done.46 = bf16[212,8,128]{2,1,0:T(8,128)(2,1)} collective-permute-done((bf16[212,8,128]{2,1,0:T(8,128)(2,1)}, bf16[212,8,128]{2,1,0:T(8,128)(2,1)}, u32[]{:S(2)}, u32[]{:S(2)}) %collective-permute-start.46) | collective-permute-done | bytes 434208 | tf_op jit(solution)/shard_map/ppermute | solution.py:1186
  742.2 15.9 %all-to-all-start.20 = ((f32[32,1,128]{2,1,0:T(1,128)}), f32[32,1,128]{2,1,0:T(1,128)S(1)}, u32[]{:S(2)}, u32[]{:S(2)}) async-start(f32[32,1,128]{2,1,0:T(1,128)} %broadcast_in_dim.104), calls=%async_computation.20 | async-start | bytes 32768 | tf_op jit(solution)/shard_map/all_to_all | solution.py:938
  758.1 7.1 all-to-all-done.20
  766.5 4.8 fusion.14
  776.8 14.9 %collective-permute-done.48 = bf16[192,768]{1,0:T(8,128)(2,1)S(1)} collective-permute-done((bf16[192,768]{1,0:T(8,128)(2,1)S(1)}, bf16[192,768]{1,0:T(8,128)(2,1)S(1)}, u32[]{:S(2)}, u32[]{:S(2)}) %collective-permute-start.48) | collective-permute-done | bytes 294944 | tf_op jit(solution)/shard_map/ppermute | solution.py:1186
  792.9 7.3 collective-permute-done.49
  826.0 5.0 multiply_subtract_fusion
  832.3 7.1 collective-permute-done.53
  850.4 11.3 %multiply_add_fusion = f32[2,2,768,768]{3,2,1,0:T(8,128)} fusion(f32[2,2,768,768]{3,2,1,0:T(8,128)} %bitcast.372, f32[2,2,768,768]{3,2,1,0:T(8,128)} %param.23), kind=kLoop, calls=%fused_computation.1 | loop fusion | flops 4718592 | bytes 28311552 | tf_op jit(solution)/shard_map/add | solution.py:1591
  866.2 17.0 %collective-permute-done.58 = bf16[392,768]{1,0:T(8,128)(2,1)S(1)} collective-permute-done((bf16[392,768]{1,0:T(8,128)(2,1)S(1)}, bf16[392,768]{1,0:T(8,128)(2,1)S(1)}, u32[]{:S(2)}, u32[]{:S(2)}) %collective-permute-start.58) | collective-permute-done | bytes 602144 | tf_op jit(solution)/shard_map/ppermute | solution.py:1256
  895.6 8.4 muon.1
  (765 shorter events, 460.7 us)
Async XLA Ops:
  9.3 39.7 %all-to-all-start = ((bf16[8,18,1280]{2,1,0:T(8,128)(2,1)}), bf16[8,18,1280]{2,1,0:T(8,128)(2,1)}, u32[]{:S(2)}, u32[]{:S(2)}) async-start(bf16[8,18,1280]{2,1,0:T(8,128)(2,1)} %copy.149), calls=%async_computation | async-start | bytes 983040 | tf_op jit(solution)/shard_map/all_to_all | solution.py:1296
  21.9 27.1 %collective-permute-start = (bf16[212,8,128]{2,1,0:T(8,128)(2,1)S(1)}, bf16[212,8,128]{2,1,0:T(8,128)(2,1)S(1)}, u32[]{:S(2)}, u32[]{:S(2)}) collective-permute-start(bf16[212,8,128]{2,1,0:T(8,128)(2,1)S(1)} %fusion.35), channel_id=1, source_target_pairs={{0,16},{16,0},{1,17},{17,1},{2,18},{18,2},{3,19},{19,3},{4,20},{20... | collective-permute-start | bytes 1302536 | tf_op jit(solution)/shard_map/ppermute | solution.py:1186
  71.3 26.4 %collective-permute-start.11 = (bf16[2,2,2,70,8,128]{5,4,3,2,1,0:T(8,128)(2,1)S(1)}, bf16[2,2,2,70,8,128]{5,4,3,2,1,0:T(8,128)(2,1)S(1)}, u32[]{:S(2)}, u32[]{:S(2)}) collective-permute-start(bf16[2,2,2,70,8,128]{5,4,3,2,1,0:T(8,128)(2,1)S(1)} %get-tuple-element.272), channel_id=1, source_target_pairs={{0,2},{2,0},{1,3},{3,1},{4,6},{6,4},{5,7},{7,5},{8,10},{10,8},{9,1... | collective-permute-start | bytes 3440648 | tf_op jit(solution)/shard_map/ppermute | solution.py:1186
  75.0 24.4 %collective-permute-start.3 = (bf16[2,2,2,72,8,128]{5,4,3,2,1,0:T(8,128)(2,1)S(1)}, bf16[2,2,2,72,8,128]{5,4,3,2,1,0:T(8,128)(2,1)S(1)}, u32[]{:S(2)}, u32[]{:S(2)}) collective-permute-start(bf16[2,2,2,72,8,128]{5,4,3,2,1,0:T(8,128)(2,1)S(1)} %get-tuple-element.270), channel_id=1, source_target_pairs={{0,8},{8,0},{1,9},{9,1},{2,10},{10,2},{3,11},{11,3},{4,12},{12,4},... | collective-permute-start | bytes 3538952 | tf_op jit(solution)/shard_map/ppermute | solution.py:1186
  75.2 26.2 %collective-permute-start.7 = (bf16[2,2,2,70,8,128]{5,4,3,2,1,0:T(8,128)(2,1)S(1)}, bf16[2,2,2,70,8,128]{5,4,3,2,1,0:T(8,128)(2,1)S(1)}, u32[]{:S(2)}, u32[]{:S(2)}) collective-permute-start(bf16[2,2,2,70,8,128]{5,4,3,2,1,0:T(8,128)(2,1)S(1)} %get-tuple-element.274), channel_id=1, source_target_pairs={{0,4},{4,0},{1,5},{5,1},{2,6},{6,2},{3,7},{7,3},{8,12},{12,8},{9,1... | collective-permute-start | bytes 3440648 | tf_op jit(solution)/shard_map/ppermute | solution.py:1186
  99.3 64.7 %collective-permute-start.12 = (bf16[2,2,2,2,70,8,128]{6,5,4,3,2,1,0:T(8,128)(2,1)}, bf16[2,2,2,2,70,8,128]{6,5,4,3,2,1,0:T(8,128)(2,1)}, u32[]{:S(2)}, u32[]{:S(2)}) collective-permute-start(bf16[2,2,2,2,70,8,128]{6,5,4,3,2,1,0:T(8,128)(2,1)} %pad_maximum_fusion.6.refs_5_), channel_id=1, source_target_pairs={{0,1},{1,0},{2,3},{3,2},{4,5},{5,4},{6,7},{7,6},{8,9},{9,8},{10,11... | collective-permute-start | bytes 6881288 | tf_op jit(solution)/shard_map/ppermute | solution.py:1186
  101.0 64.4 %collective-permute-start.4 = (bf16[2,2,2,2,72,8,128]{6,5,4,3,2,1,0:T(8,128)(2,1)}, bf16[2,2,2,2,72,8,128]{6,5,4,3,2,1,0:T(8,128)(2,1)}, u32[]{:S(2)}, u32[]{:S(2)}) collective-permute-start(bf16[2,2,2,2,72,8,128]{6,5,4,3,2,1,0:T(8,128)(2,1)} %pad_maximum_fusion.3.refs_1_), channel_id=1, source_target_pairs={{0,1},{1,0},{2,3},{3,2},{4,5},{5,4},{6,7},{7,6},{8,9},{9,8},{10,11... | collective-permute-start | bytes 7077896 | tf_op jit(solution)/shard_map/ppermute | solution.py:1186
  103.0 62.4 %collective-permute-start.8 = (bf16[2,2,2,2,70,8,128]{6,5,4,3,2,1,0:T(8,128)(2,1)}, bf16[2,2,2,2,70,8,128]{6,5,4,3,2,1,0:T(8,128)(2,1)}, u32[]{:S(2)}, u32[]{:S(2)}) collective-permute-start(bf16[2,2,2,2,70,8,128]{6,5,4,3,2,1,0:T(8,128)(2,1)} %pad_maximum_fusion.5.refs_3_), channel_id=1, source_target_pairs={{0,1},{1,0},{2,3},{3,2},{4,5},{5,4},{6,7},{7,6},{8,9},{9,8},{10,11... | collective-permute-start | bytes 6881288 | tf_op jit(solution)/shard_map/ppermute | solution.py:1186
  104.0 30.8 %collective-permute-start.13 = (bf16[2,192,768]{2,1,0:T(8,128)(2,1)}, bf16[2,192,768]{2,1,0:T(8,128)(2,1)}, u32[]{:S(2)}, u32[]{:S(2)}) collective-permute-start(bf16[2,192,768]{2,1,0:T(8,128)(2,1)} %dynamic-slice_bitcast_fusion), channel_id=1, source_target_pairs={{0,2},{2,0},{1,3},{3,1},{4,6},{6,4},{5,7},{7,5},{8,10},{10,8},{9,1... | collective-permute-start | bytes 1769480 | tf_op jit(solution)/shard_map/ppermute | solution.py:1186
  129.4 24.8 %all-to-all-start.1 = ((bf16[8,36,1280]{2,1,0:T(8,128)(2,1)}), bf16[8,36,1280]{2,1,0:T(8,128)(2,1)S(1)}, u32[]{:S(2)}, u32[]{:S(2)}) async-start(bf16[8,36,1280]{2,1,0:T(8,128)(2,1)} %copy.151), calls=%async_computation.1 | async-start | bytes 1638400 | tf_op jit(solution)/shard_map/all_to_all | solution.py:1296
  134.2 28.1 %collective-permute-start.16 = (bf16[2,2,192,768]{3,2,1,0:T(8,128)(2,1)}, bf16[2,2,192,768]{3,2,1,0:T(8,128)(2,1)}, u32[]{:S(2)}, u32[]{:S(2)}) collective-permute-start(bf16[2,2,192,768]{3,2,1,0:T(8,128)(2,1)} %slice_bitcast_fusion), channel_id=1, source_target_pairs={{0,2},{2,0},{1,3},{3,1},{4,6},{6,4},{5,7},{7,5},{8,10},{10,8},{9,1... | collective-permute-start | bytes 3538952 | tf_op jit(solution)/shard_map/ppermute | solution.py:1186
  134.8 22.3 %collective-permute-start.14 = (bf16[2,192,768]{2,1,0:T(8,128)(2,1)}, bf16[2,192,768]{2,1,0:T(8,128)(2,1)S(1)}, u32[]{:S(2)}, u32[]{:S(2)}) collective-permute-start(bf16[2,192,768]{2,1,0:T(8,128)(2,1)} %collective-permute-done.13), channel_id=1, source_target_pairs={{0,4},{4,0},{1,5},{5,1},{2,6},{6,2},{3,7},{7,3},{8,12},{12,8},{9,1... | collective-permute-start | bytes 1769480 | tf_op jit(solution)/shard_map/ppermute | solution.py:1186
  157.1 52.9 %collective-permute-start.18 = (bf16[2,2,2,192,768]{4,3,2,1,0:T(8,128)(2,1)}, bf16[2,2,2,192,768]{4,3,2,1,0:T(8,128)(2,1)}, u32[]{:S(2)}, u32[]{:S(2)}) collective-permute-start(bf16[2,2,2,192,768]{4,3,2,1,0:T(8,128)(2,1)} %narrow.2), channel_id=1, source_target_pairs={{0,1},{1,0},{2,3},{3,2},{4,5},{5,4},{6,7},{7,6},{8,9},{9,8},{10,11... | collective-permute-start | bytes 7077896 | tf_op jit(solution)/shard_map/ppermute | solution.py:1186
  162.3 34.8 %collective-permute-start.15 = (bf16[2,2,192,768]{3,2,1,0:T(8,128)(2,1)}, bf16[2,2,192,768]{3,2,1,0:T(8,128)(2,1)}, u32[]{:S(2)}, u32[]{:S(2)}) collective-permute-start(bf16[2,2,192,768]{3,2,1,0:T(8,128)(2,1)} %pad_maximum_fusion.10), channel_id=1, source_target_pairs={{0,8},{8,0},{1,9},{9,1},{2,10},{10,2},{3,11},{11,3},{4,12},{12,4},... | collective-permute-start | bytes 3538952 | tf_op jit(solution)/shard_map/ppermute | solution.py:1186
  164.0 33.2 %collective-permute-start.17 = (bf16[2,2,192,768]{3,2,1,0:T(8,128)(2,1)}, bf16[2,2,192,768]{3,2,1,0:T(8,128)(2,1)}, u32[]{:S(2)}, u32[]{:S(2)}) collective-permute-start(bf16[2,2,192,768]{3,2,1,0:T(8,128)(2,1)} %collective-permute-done.16), channel_id=1, source_target_pairs={{0,4},{4,0},{1,5},{5,1},{2,6},{6,2},{3,7},{7,3},{8,12},{12,8},{9,1... | collective-permute-start | bytes 3538952 | tf_op jit(solution)/shard_map/ppermute | solution.py:1186
  177.4 16.0 %all-to-all-start.4 = ((bf16[16,72,128]{2,1,0:T(8,128)(2,1)}), bf16[16,72,128]{2,1,0:T(8,128)(2,1)S(1)}, u32[]{:S(2)}, u32[]{:S(2)}) async-start(bf16[16,72,128]{2,1,0:T(8,128)(2,1)} %get-tuple-element.133), calls=%async_computation.4 | async-start | bytes 589824 | tf_op jit(solution)/shard_map/all_to_all | solution.py:932
  201.9 16.1 %collective-permute-start.19 = (bf16[2,2,2,192,768]{4,3,2,1,0:T(8,128)(2,1)}, bf16[2,2,2,192,768]{4,3,2,1,0:T(8,128)(2,1)}, u32[]{:S(2)}, u32[]{:S(2)}) collective-permute-start(bf16[2,2,2,192,768]{4,3,2,1,0:T(8,128)(2,1)} %maximum_select_fusion), channel_id=1, source_target_pairs={{0,1},{1,0},{2,3},{3,2},{4,5},{5,4},{6,7},{7,6},{8,9},{9,8},{10,11... | collective-permute-start | bytes 7077896 | tf_op jit(solution)/shard_map/ppermute | solution.py:1186
  202.0 59.1 %collective-permute-start.20 = (bf16[2,2,2,192,768]{4,3,2,1,0:T(8,128)(2,1)}, bf16[2,2,2,192,768]{4,3,2,1,0:T(8,128)(2,1)}, u32[]{:S(2)}, u32[]{:S(2)}) collective-permute-start(bf16[2,2,2,192,768]{4,3,2,1,0:T(8,128)(2,1)} %narrow.3), channel_id=1, source_target_pairs={{0,1},{1,0},{2,3},{3,2},{4,5},{5,4},{6,7},{7,6},{8,9},{9,8},{10,11... | collective-permute-start | bytes 7077896 | tf_op jit(solution)/shard_map/ppermute | solution.py:1186
  205.8 52.0 %collective-permute-start.21 = (bf16[2,2,2,192,768]{4,3,2,0,1:T(8,128)(2,1)}, bf16[2,2,2,192,768]{4,3,2,0,1:T(8,128)(2,1)}, u32[]{:S(2)}, u32[]{:S(2)}) collective-permute-start(bf16[2,2,2,192,768]{4,3,2,0,1:T(8,128)(2,1)} %pad_maximum_fusion.4), channel_id=1, source_target_pairs={{0,1},{1,0},{2,3},{3,2},{4,5},{5,4},{6,7},{7,6},{8,9},{9,8},{10,11... | collective-permute-start | bytes 7077896 | tf_op jit(solution)/shard_map/ppermute | solution.py:1186
  241.5 19.5 %all-to-all-start.7 = ((bf16[16,72,128]{2,1,0:T(8,128)(2,1)}), bf16[16,72,128]{2,1,0:T(8,128)(2,1)}, u32[]{:S(2)}, u32[]{:S(2)}) async-start(bf16[16,72,128]{2,1,0:T(8,128)(2,1)} %get-tuple-element.142), calls=%async_computation.7 | async-start | bytes 589824 | tf_op jit(solution)/shard_map/all_to_all | solution.py:932
  466.1 19.8 %collective-permute-start.22 = (bf16[1536,768]{1,0:T(8,128)(2,1)}, bf16[1536,768]{1,0:T(8,128)(2,1)}, u32[]{:S(2)}, u32[]{:S(2)}) collective-permute-start(bf16[1536,768]{1,0:T(8,128)(2,1)} %convolution_convert_fusion.9), channel_id=1, source_target_pairs={{0,1},{1,0},{2,3},{3,2},{4,5},{5,4},{6,7},{7,6},{8,9},{9,8},{10,11... | collective-permute-start | bytes 7077896 | tf_op jit(solution)/shard_map/ppermute | solution.py:1186
  469.1 20.1 %collective-permute-start.23 = (bf16[1536,768]{1,0:T(8,128)(2,1)}, bf16[1536,768]{1,0:T(8,128)(2,1)}, u32[]{:S(2)}, u32[]{:S(2)}) collective-permute-start(bf16[1536,768]{1,0:T(8,128)(2,1)} %convolution_convert_fusion.8), channel_id=1, source_target_pairs={{0,1},{1,0},{2,3},{3,2},{4,5},{5,4},{6,7},{7,6},{8,9},{9,8},{10,11... | collective-permute-start | bytes 7077896 | tf_op jit(solution)/shard_map/ppermute | solution.py:1186
  469.6 25.3 %all-to-all-start.16 = ((bf16[16,72,128]{2,1,0:T(8,128)(2,1)}), bf16[16,72,128]{2,1,0:T(8,128)(2,1)S(1)}, u32[]{:S(2)}, u32[]{:S(2)}) async-start(bf16[16,72,128]{2,1,0:T(8,128)(2,1)} %get-tuple-element.185), calls=%async_computation.16 | async-start | bytes 589824 | tf_op jit(solution)/shard_map/all_to_all | solution.py:932
  557.8 265.6 %all-gather.2.cloned.1.call-start = ((), (), s32[]{:S(2)}) async-start(), calls=%async_computation.21 | async-start | bytes 5308416 | tf_op jit(solution)/shard_map/all_gather | solution.py:1561
  581.5 45.3 %collective-permute-start.29 = (bf16[2,2,2,2,212,8,128]{6,5,4,3,2,1,0:T(8,128)(2,1)}, bf16[2,2,2,2,212,8,128]{6,5,4,3,2,1,0:T(8,128)(2,1)}, u32[]{:S(2)}, u32[]{:S(2)}) collective-permute-start(bf16[2,2,2,2,212,8,128]{6,5,4,3,2,1,0:T(8,128)(2,1)} %get-tuple-element.238), channel_id=1, source_target_pairs={{0,1},{1,0},{2,3},{3,2},{4,5},{5,4},{6,7},{7,6},{8,9},{9,8},{10,11... | collective-permute-start | bytes 20840456 | tf_op jit(solution)/shard_map/ppermute | solution.py:1186
  583.1 43.2 %collective-permute-start.28 = (bf16[2,1,2,2,128,768]{5,4,3,2,1,0:T(8,128)(2,1)}, bf16[2,1,2,2,128,768]{5,4,3,2,1,0:T(8,128)(2,1)S(1)}, u32[]{:S(2)}, u32[]{:S(2)}) collective-permute-start(bf16[2,1,2,2,128,768]{5,4,3,2,1,0:T(8,128)(2,1)} %fusion.10), channel_id=1, source_target_pairs={{0,8},{8,0},{1,9},{9,1},{2,10},{10,2},{3,11},{11,3},{4,12},{12,4},... | collective-permute-start | bytes 4718600 | tf_op jit(solution)/shard_map/ppermute | solution.py:1186
  585.0 36.8 %collective-permute-start.27 = (bf16[2,2,1,2,128,768]{5,4,3,2,1,0:T(8,128)(2,1)}, bf16[2,2,1,2,128,768]{5,4,3,2,1,0:T(8,128)(2,1)}, u32[]{:S(2)}, u32[]{:S(2)}) collective-permute-start(bf16[2,2,1,2,128,768]{5,4,3,2,1,0:T(8,128)(2,1)} %pad_maximum_fusion.7), channel_id=1, source_target_pairs={{0,2},{2,0},{1,3},{3,1},{4,6},{6,4},{5,7},{7,5},{8,10},{10,8},{9,1... | collective-permute-start | bytes 4718600 | tf_op jit(solution)/shard_map/ppermute | solution.py:1186
  587.6 36.6 %collective-permute-start.26 = (bf16[2,2,2,1,128,768]{5,4,3,2,1,0:T(8,128)(2,1)}, bf16[2,2,2,1,128,768]{5,4,3,2,1,0:T(8,128)(2,1)}, u32[]{:S(2)}, u32[]{:S(2)}) collective-permute-start(bf16[2,2,2,1,128,768]{5,4,3,2,1,0:T(8,128)(2,1)} %pad_maximum_fusion.8), channel_id=1, source_target_pairs={{0,4},{4,0},{1,5},{5,1},{2,6},{6,2},{3,7},{7,3},{8,12},{12,8},{9,1... | collective-permute-start | bytes 4718600 | tf_op jit(solution)/shard_map/ppermute | solution.py:1186
  626.9 20.5 %collective-permute-start.30 = (bf16[2,2,1,1,128,768]{5,4,3,2,1,0:T(8,128)(2,1)S(1)}, bf16[2,2,1,1,128,768]{5,4,3,2,1,0:T(8,128)(2,1)S(1)}, u32[]{:S(2)}, u32[]{:S(2)}) collective-permute-start(bf16[2,2,1,1,128,768]{5,4,3,2,1,0:T(8,128)(2,1)S(1)} %slice.550), channel_id=1, source_target_pairs={{0,2},{2,0},{1,3},{3,1},{4,6},{6,4},{5,7},{7,5},{8,10},{10,8},{9,1... | collective-permute-start | bytes 2359304 | tf_op jit(solution)/shard_map/ppermute | solution.py:1186
  628.3 20.9 %collective-permute-start.32 = (bf16[2,1,1,2,128,768]{5,4,3,2,1,0:T(8,128)(2,1)S(1)}, bf16[2,1,1,2,128,768]{5,4,3,2,1,0:T(8,128)(2,1)S(1)}, u32[]{:S(2)}, u32[]{:S(2)}) collective-permute-start(bf16[2,1,1,2,128,768]{5,4,3,2,1,0:T(8,128)(2,1)S(1)} %constant_dynamic-slice_fusion.1), channel_id=1, source_target_pairs={{0,8},{8,0},{1,9},{9,1},{2,10},{10,2},{3,11},{11,3},{4,12},{12,4},... | collective-permute-start | bytes 2359304 | tf_op jit(solution)/shard_map/ppermute | solution.py:1186
  632.3 38.0 %collective-permute-start.40 = (bf16[2,2,2,1,70,8,128]{6,5,4,3,2,1,0:T(8,128)(2,1)S(1)}, bf16[2,2,2,1,70,8,128]{6,5,4,3,2,1,0:T(8,128)(2,1)S(1)}, u32[]{:S(2)}, u32[]{:S(2)}) collective-permute-start(bf16[2,2,2,1,70,8,128]{6,5,4,3,2,1,0:T(8,128)(2,1)S(1)} %add_convert_fusion.12), channel_id=1, source_target_pairs={{0,2},{2,0},{1,3},{3,1},{4,6},{6,4},{5,7},{7,5},{8,10},{10,8},{9,1... | collective-permute-start | bytes 3440648 | tf_op jit(solution)/shard_map/ppermute | solution.py:1186
  633.9 20.5 %collective-permute-start.34 = (bf16[2,1,2,1,128,768]{5,4,3,2,1,0:T(8,128)(2,1)S(1)}, bf16[2,1,2,1,128,768]{5,4,3,2,1,0:T(8,128)(2,1)S(1)}, u32[]{:S(2)}, u32[]{:S(2)}) collective-permute-start(bf16[2,1,2,1,128,768]{5,4,3,2,1,0:T(8,128)(2,1)S(1)} %slice.554), channel_id=1, source_target_pairs={{0,4},{4,0},{1,5},{5,1},{2,6},{6,2},{3,7},{7,3},{8,12},{12,8},{9,1... | collective-permute-start | bytes 2359304 | tf_op jit(solution)/shard_map/ppermute | solution.py:1186
  636.1 43.6 %collective-permute-start.37 = (bf16[2,2,1,2,72,8,128]{6,5,4,3,2,1,0:T(8,128)(2,1)S(1)}, bf16[2,2,1,2,72,8,128]{6,5,4,3,2,1,0:T(8,128)(2,1)S(1)}, u32[]{:S(2)}, u32[]{:S(2)}) collective-permute-start(bf16[2,2,1,2,72,8,128]{6,5,4,3,2,1,0:T(8,128)(2,1)S(1)} %add_convert_fusion.8), channel_id=1, source_target_pairs={{0,4},{4,0},{1,5},{5,1},{2,6},{6,2},{3,7},{7,3},{8,12},{12,8},{9,1... | collective-permute-start | bytes 3538952 | tf_op jit(solution)/shard_map/ppermute | solution.py:1186
  647.4 28.2 %collective-permute-start.43 = (bf16[2,1,2,2,70,8,128]{6,5,4,3,2,1,0:T(8,128)(2,1)S(1)}, bf16[2,1,2,2,70,8,128]{6,5,4,3,2,1,0:T(8,128)(2,1)S(1)}, u32[]{:S(2)}, u32[]{:S(2)}) collective-permute-start(bf16[2,1,2,2,70,8,128]{6,5,4,3,2,1,0:T(8,128)(2,1)S(1)} %add_convert_fusion.10), channel_id=1, source_target_pairs={{0,8},{8,0},{1,9},{9,1},{2,10},{10,2},{3,11},{11,3},{4,12},{12,4},... | collective-permute-start | bytes 3440648 | tf_op jit(solution)/shard_map/ppermute | solution.py:1186
  649.2 39.8 %collective-permute-start.31 = (bf16[2,1,1,1,128,768]{5,4,3,2,1,0:T(8,128)(2,1)S(1)}, bf16[2,1,1,1,128,768]{5,4,3,2,1,0:T(8,128)(2,1)S(1)}, u32[]{:S(2)}, u32[]{:S(2)}) collective-permute-start(bf16[2,1,1,1,128,768]{5,4,3,2,1,0:T(8,128)(2,1)S(1)} %constant_dynamic-slice_fusion.2), channel_id=1, source_target_pairs={{0,8},{8,0},{1,9},{9,1},{2,10},{10,2},{3,11},{11,3},{4,12},{12,4},... | collective-permute-start | bytes 1179656 | tf_op jit(solution)/shard_map/ppermute | solution.py:1186
  654.5 33.7 %collective-permute-start.33 = (bf16[2,1,1,1,128,768]{5,4,3,2,1,0:T(8,128)(2,1)S(1)}, bf16[2,1,1,1,128,768]{5,4,3,2,1,0:T(8,128)(2,1)S(1)}, u32[]{:S(2)}, u32[]{:S(2)}) collective-permute-start(bf16[2,1,1,1,128,768]{5,4,3,2,1,0:T(8,128)(2,1)S(1)} %slice.638), channel_id=1, source_target_pairs={{0,4},{4,0},{1,5},{5,1},{2,6},{6,2},{3,7},{7,3},{8,12},{12,8},{9,1... | collective-permute-start | bytes 1179656 | tf_op jit(solution)/shard_map/ppermute | solution.py:1186
  670.4 18.5 %collective-permute-start.35 = (bf16[2,1,1,1,128,768]{5,4,3,2,1,0:T(8,128)(2,1)S(1)}, bf16[2,1,1,1,128,768]{5,4,3,2,1,0:T(8,128)(2,1)S(1)}, u32[]{:S(2)}, u32[]{:S(2)}) collective-permute-start(bf16[2,1,1,1,128,768]{5,4,3,2,1,0:T(8,128)(2,1)S(1)} %slice.640), channel_id=1, source_target_pairs={{0,2},{2,0},{1,3},{3,1},{4,6},{6,4},{5,7},{7,5},{8,10},{10,8},{9,1... | collective-permute-start | bytes 1179656 | tf_op jit(solution)/shard_map/ppermute | solution.py:1186
  675.6 23.2 %collective-permute-start.41 = (bf16[2,1,2,1,70,8,128]{6,5,4,3,2,1,0:T(8,128)(2,1)S(1)}, bf16[2,1,2,1,70,8,128]{6,5,4,3,2,1,0:T(8,128)(2,1)S(1)}, u32[]{:S(2)}, u32[]{:S(2)}) collective-permute-start(bf16[2,1,2,1,70,8,128]{6,5,4,3,2,1,0:T(8,128)(2,1)S(1)} %slice.648), channel_id=1, source_target_pairs={{0,8},{8,0},{1,9},{9,1},{2,10},{10,2},{3,11},{11,3},{4,12},{12,4},... | collective-permute-start | bytes 1720328 | tf_op jit(solution)/shard_map/ppermute | solution.py:1186
  679.7 21.3 %collective-permute-start.44 = (bf16[2,1,1,2,70,8,128]{6,5,4,3,2,1,0:T(8,128)(2,1)S(1)}, bf16[2,1,1,2,70,8,128]{6,5,4,3,2,1,0:T(8,128)(2,1)S(1)}, u32[]{:S(2)}, u32[]{:S(2)}) collective-permute-start(bf16[2,1,1,2,70,8,128]{6,5,4,3,2,1,0:T(8,128)(2,1)S(1)} %slice.652), channel_id=1, source_target_pairs={{0,4},{4,0},{1,5},{5,1},{2,6},{6,2},{3,7},{7,3},{8,12},{12,8},{9,1... | collective-permute-start | bytes 1720328 | tf_op jit(solution)/shard_map/ppermute | solution.py:1186
  689.2 23.6 %collective-permute-start.36 = (bf16[384,768]{1,0:T(8,128)(2,1)S(1)}, bf16[384,768]{1,0:T(8,128)(2,1)S(1)}, u32[]{:S(2)}, u32[]{:S(2)}) collective-permute-start(bf16[384,768]{1,0:T(8,128)(2,1)S(1)} %select_bitcast_fusion), channel_id=1, source_target_pairs={{0,16},{16,0},{1,17},{17,1},{2,18},{18,2},{3,19},{19,3},{4,20},{20... | collective-permute-start | bytes 1769480 | tf_op jit(solution)/shard_map/ppermute | solution.py:1186
  717.2 19.4 %collective-permute-start.46 = (bf16[212,8,128]{2,1,0:T(8,128)(2,1)}, bf16[212,8,128]{2,1,0:T(8,128)(2,1)}, u32[]{:S(2)}, u32[]{:S(2)}) collective-permute-start(bf16[212,8,128]{2,1,0:T(8,128)(2,1)} %slice_bitcast_fusion.1), channel_id=1, source_target_pairs={{0,16},{16,0},{1,17},{17,1},{2,18},{18,2},{3,19},{19,3},{4,20},{20... | collective-permute-start | bytes 1302536 | tf_op jit(solution)/shard_map/ppermute | solution.py:1186
  742.2 23.0 %all-to-all-start.20 = ((f32[32,1,128]{2,1,0:T(1,128)}), f32[32,1,128]{2,1,0:T(1,128)S(1)}, u32[]{:S(2)}, u32[]{:S(2)}) async-start(f32[32,1,128]{2,1,0:T(1,128)} %broadcast_in_dim.104), calls=%async_computation.20 | async-start | bytes 32768 | tf_op jit(solution)/shard_map/all_to_all | solution.py:938
  775.7 16.0 %collective-permute-start.48 = (bf16[192,768]{1,0:T(8,128)(2,1)S(1)}, bf16[192,768]{1,0:T(8,128)(2,1)S(1)}, u32[]{:S(2)}, u32[]{:S(2)}) collective-permute-start(bf16[192,768]{1,0:T(8,128)(2,1)S(1)} %get-tuple-element.290), channel_id=1, source_target_pairs={{0,4},{4,0},{1,5},{5,1},{2,6},{6,2},{3,7},{7,3},{8,12},{12,8},{9,1... | collective-permute-start | bytes 884744 | tf_op jit(solution)/shard_map/ppermute | solution.py:1186
  823.4 16.0 %collective-permute-start.53 = (bf16[392,768]{1,0:T(8,128)(2,1)}, bf16[392,768]{1,0:T(8,128)(2,1)S(1)}, u32[]{:S(2)}, u32[]{:S(2)}) collective-permute-start(bf16[392,768]{1,0:T(8,128)(2,1)} %pad_maximum_fusion.18), channel_id=1, source_target_pairs={{0,8},{8,16},{16,24},{1,9},{9,17},{17,25},{2,10},{10,18},{18,26},{... | collective-permute-start | bytes 1806344 | tf_op jit(solution)/shard_map/ppermute | solution.py:1252
  831.0 17.2 %collective-permute-start.56 = (bf16[392,768]{1,0:T(8,128)(2,1)S(1)}, bf16[392,768]{1,0:T(8,128)(2,1)S(1)}, u32[]{:S(2)}, u32[]{:S(2)}) collective-permute-start(bf16[392,768]{1,0:T(8,128)(2,1)S(1)} %copy-done.69), channel_id=1, source_target_pairs={{8,0},{16,8},{24,16},{9,1},{17,9},{25,17},{10,2},{18,10},{26,18},{... | collective-permute-start | bytes 1806344 | tf_op jit(solution)/shard_map/ppermute | solution.py:1256
  848.2 16.4 %collective-permute-start.57 = (bf16[392,768]{1,0:T(8,128)(2,1)S(1)}, bf16[392,768]{1,0:T(8,128)(2,1)S(1)}, u32[]{:S(2)}, u32[]{:S(2)}) collective-permute-start(bf16[392,768]{1,0:T(8,128)(2,1)S(1)} %collective-permute-done.56), channel_id=1, source_target_pairs={{8,0},{16,8},{9,1},{17,9},{10,2},{18,10},{11,3},{19,11},{12,4},{20... | collective-permute-start | bytes 1806344 | tf_op jit(solution)/shard_map/ppermute | solution.py:1256
  849.5 16.4 %collective-permute-start.55 = (bf16[392,768]{1,0:T(8,128)(2,1)S(1)}, bf16[392,768]{1,0:T(8,128)(2,1)S(1)}, u32[]{:S(2)}, u32[]{:S(2)}) collective-permute-start(bf16[392,768]{1,0:T(8,128)(2,1)S(1)} %collective-permute-done.54), channel_id=1, source_target_pairs={{16,24},{17,25},{18,26},{19,27},{20,28},{21,29},{22,30},{23,31}} | collective-permute-start | bytes 1806344 | tf_op jit(solution)/shard_map/ppermute | solution.py:1252
  864.6 18.6 %collective-permute-start.58 = (bf16[392,768]{1,0:T(8,128)(2,1)S(1)}, bf16[392,768]{1,0:T(8,128)(2,1)S(1)}, u32[]{:S(2)}, u32[]{:S(2)}) collective-permute-start(bf16[392,768]{1,0:T(8,128)(2,1)S(1)} %collective-permute-done.57), channel_id=1, source_target_pairs={{8,0},{9,1},{10,2},{11,3},{12,4},{13,5},{14,6},{15,7}} | collective-permute-start | bytes 1806344 | tf_op jit(solution)/shard_map/ppermute | solution.py:1256
  (186 other events, 2505.9 us)
Sparse Core Ops, SparseCore 0:
  714.0 95.8 all-gather.1
